TPU v7x, 32 devices: a whole 2x2x4 slice. The times are simulated.
32 devices in a mesh: row: 4 (over z), col: 8 (over y, x, core).
Axes of the slice: x: 2, y: 2, z: 4, core: 2. Of those that a mesh axis runs over, the one named last changes fastest.
Arguments:
- slip_load: bfloat16 [4, 8, 1024, 128], P('row', 'col'), may hold values from -6 to 6
- flexibility: bfloat16 [4, 8, 1024, 1024], P('row', 'col'), as said below
- schur: bfloat16 [4, 8, 1024, 1024], P('row', 'col'), as said below
- corner_coupling: float32 [4, 8, 12, 1024], P('row', 'col'), may hold values from -0.1875 to 0.1875
- coarse_inverse: float32 [384, 384], P('row', 'col'), as said below
- bounds_table: float32 [16], replicated, may hold values from 0.3 to 3
- bound_index: int32 [4, 8, 1024], P('row', 'col'), may hold values from 0 to 15
- face_rows: int32 [4, 8, 4], P('row', 'col'), may hold values from 0 to 256, as said below
Outputs:
- multipliers: bfloat16 [4, 8, 1024, 128], P('row', 'col')
Inputs may be any that keep to these rules, and one draw needn't show every extreme that they name: `face_rows`: face counts agree between the two subdomains of a shared face, are 0 on faces at the edge of the grid, and some face has exactly 256 live slots. `coarse_inverse`: symmetric. `flexibility`: symmetric and positive definite. `schur`: symmetric and positive definite.
All inputs are finite; a program needn't handle non-finite values.
Results may differ from a plain program's by a relative error of at most 0.0038.
Values sent between devices are 32-bit elements; how exact they have to be, the bound alone decides.
No kernel may reach another device: no remote copies, remote signals or barrier semaphores. Data moves between devices by JAX's collectives and lax.ppermute only.
A program may use at most 64 MiB of HBM per device.

v0:
```python
import jax
import jax.numpy as jnp
from jax import lax
from jax.sharding import PartitionSpec as P

ITERS = 2


def passed_along(x, axis, by):
    count = lax.axis_size(axis)
    pairs = [(i, i + by) for i in range(count) if 0 <= i + by < count]
    return lax.ppermute(x, axis, pairs)


def broadcast(block, axis, holder):
    block = jnp.where(lax.axis_index(axis) == holder, block, jnp.zeros_like(block))
    return lax.psum(block, axis)


def local(
    slip_load,
    flexibility,
    schur,
    corner_coupling,
    coarse_inverse,
    bounds_table,
    bound_index,
    face_rows,
):
    loads = slip_load[0, 0].astype(jnp.float32)
    flex_block = flexibility[0, 0]
    schur_block = schur[0, 0]
    coupling = corner_coupling[0, 0]
    row_count = flex_block.shape[0]
    face_size = row_count // 4
    corners = coupling.shape[0]
    row_devices = lax.axis_size("row")
    row_index = lax.axis_index("row")
    col_index = lax.axis_index("col")
    levels = jnp.arange(bounds_table.shape[0], dtype=jnp.int32)
    onehot = (bound_index[0, 0][:, None] == levels[None, :]).astype(jnp.float32)
    bound = jnp.sum(onehot * bounds_table[None, :], axis=1)[:, None]
    slots = jnp.arange(face_size, dtype=jnp.int32)
    live = (slots[None, :] < face_rows[0, 0][:, None]).astype(jnp.float32).reshape(row_count, 1)
    lam = jnp.clip(loads, -bound, bound)
    for iteration in range(ITERS):
        displacement = jnp.dot(
            flex_block, lam.astype(jnp.bfloat16), preferred_element_type=jnp.float32
        )
        nb_west = passed_along(displacement[face_size : 2 * face_size], "col", 1)
        nb_east = passed_along(displacement[0:face_size], "col", -1)
        nb_lower = passed_along(displacement[3 * face_size :], "row", 1)
        nb_upper = passed_along(displacement[2 * face_size : 3 * face_size], "row", -1)
        paired = jnp.concatenate([nb_west, nb_east, nb_lower, nb_upper], axis=0)
        jump = live * (displacement - paired - loads)
        corner_force = jnp.dot(coupling, jump, precision=lax.Precision.HIGHEST)
        gathered = lax.all_gather(corner_force, "row", axis=0, tiled=True)
        partial_value = jnp.dot(coarse_inverse, gathered, precision=lax.Precision.HIGHEST)
        total = lax.psum(partial_value, "col")
        picked = broadcast(total, "row", col_index // 2)
        offset = col_index % 2 * (corners * row_devices) + row_index * corners
        coarse = lax.dynamic_slice_in_dim(picked, offset, corners, 0)
        correction = lax.dot_general(
            coupling, coarse, (((0,), (0,)), ((), ())), precision=lax.Precision.HIGHEST
        )
        projected = jump - correction
        projected_b = projected.astype(jnp.bfloat16)
        search = jnp.dot(schur_block, projected_b, preferred_element_type=jnp.float32)
        gain_local = jnp.sum(projected_b.astype(jnp.float32) * search, axis=0)
        search_b = search.astype(jnp.bfloat16)
        gain = lax.psum(gain_local, ("row", "col"))
        curved = jnp.dot(flex_block, search_b, preferred_element_type=jnp.float32)
        curvature = lax.psum(jnp.sum(search_b.astype(jnp.float32) * curved, axis=0), ("row", "col"))
        lam = jnp.clip(lam - (gain / curvature)[None, :] * search, -bound, bound)
    return lam.astype(jnp.bfloat16)[None, None]


def solution(mesh):
    return jax.shard_map(
        local,
        mesh=mesh,
        in_specs=(
            P("row", "col", None, None),
            P("row", "col", None, None),
            P("row", "col", None, None),
            P("row", "col", None, None),
            P("row", "col"),
            P(),
            P("row", "col", None),
            P("row", "col", None),
        ),
        out_specs=P("row", "col", None, None),
        check_vma=False,
    )
```

profile of v0, /device:TPU:0, one launch (start us, length us, event | category | flops | bytes accessed | tf_op | source)
XLA Modules:
  0.0 234.9 jit_solution(16768184671712670383)
XLA Ops:
  2.1 2.4 %fusion.14 = f32[1024,128]{0,1:T(8,128)S(1)} fusion(bf16[1,1,1024,1024]{3,2,1,0:T(8,128)(2,1)} %param.9, bf16[1,1,1024,128]{2,3,1,0:T(8,128)(2,1)S(1)} %copy.15, f32[1024]{0:T(1024)S(1)} %neg.10, f32[1024]{0:T(1024)S(1)} %select_reduce_fusion), kind=kOutput, calls=%fused_computation.16 | convolution fusion | flops 269221888 | bytes 2891776 | tf_op jit(solution)/shard_map/dot_general | solution.py:47
  5.3 2.4 %collective-permute-start = (f32[256,128]{0,1:T(8,128)}, f32[256,128]{0,1:T(8,128)S(1)}, u32[]{:S(2)}, u32[]{:S(2)}) collective-permute-start(f32[256,128]{0,1:T(8,128)} %get-tuple-element.13), channel_id=1, source_target_pairs={{0,1},{1,2},{2,3},{3,4},{4,5},{5,6},{6,7},{8,9},{9,10},{10,11},{11... | collective-permute-start | bytes 393224 | tf_op jit(solution)/shard_map/ppermute | solution.py:12
  7.7 1.3 collective-permute-start.3
  9.0 4.9 %collective-permute-start.2 = (f32[256,128]{0,1:T(8,128)}, f32[256,128]{0,1:T(8,128)S(1)}, u32[]{:S(2)}, u32[]{:S(2)}) collective-permute-start(f32[256,128]{0,1:T(8,128)} %get-tuple-element.15), channel_id=1, source_target_pairs={{0,8},{8,16},{16,24},{1,9},{9,17},{17,25},{2,10},{10,18},{18,26},{... | collective-permute-start | bytes 393224 | tf_op jit(solution)/shard_map/ppermute | solution.py:12
  13.9 1.3 collective-permute-start.1
  15.4 1.8 collective-permute-done.2
  17.2 1.3 collective-permute-done.1
  18.5 1.5 convolution_bitcast_fusion.5
  19.9 13.8 %all-gather = f32[4,12,128]{2,1,0:T(8,128)S(1)} all-gather(f32[1,12,128]{2,1,0:T(8,128)S(1)} %convolution_bitcast_fusion.5), channel_id=1, replica_groups=mesh['row'=4,'col'=8] {'row'}, dimensions={0}, use_global_device_ids=true | all-gather | bytes 30720 | tf_op jit(solution)/shard_map/all_gather | solution.py:57
  34.0 23.9 %psum.56 = f32[96,128]{1,0:T(8,128)S(1)} all-reduce(f32[96,128]{1,0:T(8,128)S(1)} %convolution_bitcast_fusion.3), channel_id=1, replica_groups=mesh['row'=4,'col'=8] {'col'}, use_global_device_ids=true, to_apply=%region_1.2 | all-reduce | flops 12288 | bytes 98304 | tf_op jit(solution)/shard_map/psum | solution.py:59
  57.9 18.3 %psum.57 = f32[96,128]{1,0:T(8,128)S(1)} all-reduce(f32[96,128]{1,0:T(8,128)S(1)} %broadcast_select_fusion.1), channel_id=1, replica_groups=mesh['row'=4,'col'=8] {'row'}, use_global_device_ids=true, to_apply=%region_2.3 | all-reduce | flops 12288 | bytes 98304 | tf_op jit(solution)/shard_map/psum | solution.py:17
  76.2 1.7 fusion.39
  79.8 37.5 %all-reduce.1 = (f32[128]{0:T(128)S(1)}, f32[128]{0:T(128)S(1)}) all-reduce(f32[128]{0:T(128)S(1)} %get-tuple-element.17, f32[128]{0:T(128)S(1)} %fusion.40), channel_id=1, replica_groups=mesh['row'=4,'col'=8] {'row','col'}, use_global_device_ids=true, to_apply=%region_4.5 | all-reduce | flops 256 | bytes 2048 | tf_op jit(solution)/shard_map/psum | solution.py:71
  117.3 2.4 %fusion.20 = f32[1024,128]{0,1:T(8,128)S(1)} fusion(bf16[1,1,1024,1024]{3,2,1,0:T(8,128)(2,1)} %param.9, bf16[1,1,1024,128]{2,3,1,0:T(8,128)(2,1)S(1)} %copy.15, f32[1024,128]{0,1:T(8,128)S(1)} %get-tuple-element.18, f32[128]{0:T(128)S(1)} %div.18, f32[1024]{0:T(1024)S(1)} %neg.10, f32[1024]{0:T(1024)S(1)} %select_reduce_fusion), kind=kOutput, calls=%fused_computation.18 | convolution fusion | flops 269484032 | bytes 3416576 | tf_op jit(solution)/shard_map/dot_general | solution.py:47
  119.8 1.3 collective-permute-start.4
  121.1 1.3 collective-permute-start.7
  122.4 4.7 %collective-permute-start.6 = (f32[256,128]{0,1:T(8,128)S(1)}, f32[256,128]{0,1:T(8,128)S(1)}, u32[]{:S(2)}, u32[]{:S(2)}) collective-permute-start(f32[256,128]{0,1:T(8,128)S(1)} %get-tuple-element.11), channel_id=1, source_target_pairs={{0,8},{8,16},{16,24},{1,9},{9,17},{17,25},{2,10},{10,18},{18,26},{... | collective-permute-start | bytes 393224 | tf_op jit(solution)/shard_map/ppermute | solution.py:12
  129.7 3.0 %collective-permute-done.5 = f32[256,128]{0,1:T(8,128)S(1)} collective-permute-done((f32[256,128]{0,1:T(8,128)S(1)}, f32[256,128]{0,1:T(8,128)S(1)}, u32[]{:S(2)}, u32[]{:S(2)}) %collective-permute-start.5) | collective-permute-done | bytes 131104 | tf_op jit(solution)/shard_map/ppermute | solution.py:12
  133.3 13.1 %all-gather.1 = f32[4,12,128]{2,1,0:T(8,128)S(1)} all-gather(f32[1,12,128]{2,1,0:T(8,128)S(1)} %convolution_bitcast_fusion.4), channel_id=1, replica_groups=mesh['row'=4,'col'=8] {'row'}, dimensions={0}, use_global_device_ids=true | all-gather | bytes 30720 | tf_op jit(solution)/shard_map/all_gather | solution.py:57
  148.1 24.8 %psum.60 = f32[96,128]{1,0:T(8,128)S(1)} all-reduce(f32[96,128]{1,0:T(8,128)S(1)} %convolution_bitcast_fusion.2), channel_id=1, replica_groups=mesh['row'=4,'col'=8] {'col'}, use_global_device_ids=true, to_apply=%region_7.8 | all-reduce | flops 12288 | bytes 98304 | tf_op jit(solution)/shard_map/psum | solution.py:59
  172.9 17.8 %psum.61 = f32[96,128]{1,0:T(8,128)S(1)} all-reduce(f32[96,128]{1,0:T(8,128)S(1)} %broadcast_select_fusion), channel_id=1, replica_groups=mesh['row'=4,'col'=8] {'row'}, use_global_device_ids=true, to_apply=%region_8.9 | all-reduce | flops 12288 | bytes 98304 | tf_op jit(solution)/shard_map/psum | solution.py:17
  190.7 1.9 fusion.38
  194.5 37.6 %all-reduce = (f32[128]{0:T(128)S(1)}, f32[128]{0:T(128)S(1)}) all-reduce(f32[128]{0:T(128)S(1)} %get-tuple-element.19, f32[128]{0:T(128)S(1)} %fusion.43), channel_id=1, replica_groups=mesh['row'=4,'col'=8] {'row','col'}, use_global_device_ids=true, to_apply=%region_10.11 | all-reduce | flops 256 | bytes 2048 | tf_op jit(solution)/shard_map/psum | solution.py:71
  233.1 1.8 copy.16
  (61 shorter events, 12.6 us)
Async XLA Ops:
  0.0 77.9 %copy-start = (bf16[1,1,1024,1024]{3,2,1,0:T(8,128)(2,1)S(1)}, bf16[1,1,1024,1024]{3,2,1,0:T(8,128)(2,1)}, u32[]{:S(2)}) copy-start(bf16[1,1,1024,1024]{3,2,1,0:T(8,128)(2,1)} %param.10) | copy-start | bytes 6291460
  0.9 116.4 %copy-start.8 = (f32[1024]{0:T(1024)}, f32[1024]{0:T(1024)S(1)}, u32[]{:S(2)}) copy-start(f32[1024]{0:T(1024)S(1)} %select_reduce_fusion) | copy-start | bytes 12292
  1.0 116.4 %copy-start.11 = (f32[1024]{0:T(1024)}, f32[1024]{0:T(1024)S(1)}, u32[]{:S(2)}) copy-start(f32[1024]{0:T(1024)S(1)} %neg.10) | copy-start | bytes 12292
  2.1 13.2 %copy-start.16 = (s32[1,1,4]{2,1,0:T(1,128)S(1)}, s32[1,1,4]{2,1,0:T(1,128)}, u32[]{:S(2)}) copy-start(s32[1,1,4]{2,1,0:T(1,128)} %param.15) | copy-start | bytes 52
  2.1 16.4 %copy-start.3 = (f32[1,1,12,1024]{3,1,2,0:T(1,128)S(1)}, f32[1,1,12,1024]{3,1,2,0:T(1,128)}, u32[]{:S(2)}) copy-start(f32[1,1,12,1024]{3,1,2,0:T(1,128)} %param.11) | copy-start | bytes 147460
  2.1 31.6 %copy-start.10 = (f32[96,48]{0,1:T(8,128)S(1)}, f32[96,48]{0,1:T(8,128)}, u32[]{:S(2)}) copy-start(f32[96,48]{0,1:T(8,128)} %param.12) | copy-start | bytes 55300
  5.3 10.1 %collective-permute-start = (f32[256,128]{0,1:T(8,128)}, f32[256,128]{0,1:T(8,128)S(1)}, u32[]{:S(2)}, u32[]{:S(2)}) collective-permute-start(f32[256,128]{0,1:T(8,128)} %get-tuple-element.13), channel_id=1, source_target_pairs={{0,1},{1,2},{2,3},{3,4},{4,5},{5,6},{6,7},{8,9},{9,10},{10,11},{11... | collective-permute-start | bytes 393224 | tf_op jit(solution)/shard_map/ppermute | solution.py:12
  7.7 7.7 %collective-permute-start.3 = (f32[256,128]{0,1:T(8,128)}, f32[256,128]{0,1:T(8,128)S(1)}, u32[]{:S(2)}, u32[]{:S(2)}) collective-permute-start(f32[256,128]{0,1:T(8,128)} %get-tuple-element.14), channel_id=1, source_target_pairs={{8,0},{16,8},{24,16},{9,1},{17,9},{25,17},{10,2},{18,10},{26,18},{... | collective-permute-start | bytes 393224 | tf_op jit(solution)/shard_map/ppermute | solution.py:12
  9.0 8.2 %collective-permute-start.2 = (f32[256,128]{0,1:T(8,128)}, f32[256,128]{0,1:T(8,128)S(1)}, u32[]{:S(2)}, u32[]{:S(2)}) collective-permute-start(f32[256,128]{0,1:T(8,128)} %get-tuple-element.15), channel_id=1, source_target_pairs={{0,8},{8,16},{16,24},{1,9},{9,17},{17,25},{2,10},{10,18},{18,26},{... | collective-permute-start | bytes 393224 | tf_op jit(solution)/shard_map/ppermute | solution.py:12
  13.9 4.5 %collective-permute-start.1 = (f32[256,128]{0,1:T(8,128)S(1)}, f32[256,128]{0,1:T(8,128)}, u32[]{:S(2)}, u32[]{:S(2)}) collective-permute-start(f32[256,128]{0,1:T(8,128)S(1)} %get-tuple-element.16), channel_id=1, source_target_pairs={{1,0},{2,1},{3,2},{4,3},{5,4},{6,5},{7,6},{9,8},{10,9},{11,10},{12... | collective-permute-start | bytes 393224 | tf_op jit(solution)/shard_map/ppermute | solution.py:12
  15.4 117.3 %copy-start.13 = (f32[1,2,4,128]{3,1,2,0:T(2,128)}, f32[1,2,4,128]{3,1,2,0:T(2,128)S(1)}, u32[]{:S(2)}) copy-start(f32[1,2,4,128]{3,1,2,0:T(2,128)S(1)} %copy.18) | copy-start | bytes 12292
  76.2 2.6 %copy-start.1 = (bf16[1,1,1024,1024]{3,2,1,0:T(8,128)(2,1)S(1)}, bf16[1,1,1024,1024]{3,2,1,0:T(8,128)(2,1)}, u32[]{:S(2)}) copy-start(bf16[1,1,1024,1024]{3,2,1,0:T(8,128)(2,1)} %param.9) | copy-start | bytes 6291460
  117.3 2.5 %copy-start.14 = (f32[128]{0:T(128)}, f32[128]{0:T(128)S(1)}, u32[]{:S(2)}) copy-start(f32[128]{0:T(128)S(1)} %div.18) | copy-start | bytes 1540
  119.8 8.7 %collective-permute-start.4 = (f32[256,128]{0,1:T(8,128)S(1)}, f32[256,128]{0,1:T(8,128)S(1)}, u32[]{:S(2)}, u32[]{:S(2)}) collective-permute-start(f32[256,128]{0,1:T(8,128)S(1)} %get-tuple-element.9), channel_id=1, source_target_pairs={{0,1},{1,2},{2,3},{3,4},{4,5},{5,6},{6,7},{8,9},{9,10},{10,11},{11... | collective-permute-start | bytes 393224 | tf_op jit(solution)/shard_map/ppermute | solution.py:12
  121.1 7.4 %collective-permute-start.7 = (f32[256,128]{0,1:T(8,128)S(1)}, f32[256,128]{0,1:T(8,128)S(1)}, u32[]{:S(2)}, u32[]{:S(2)}) collective-permute-start(f32[256,128]{0,1:T(8,128)S(1)} %get-tuple-element.10), channel_id=1, source_target_pairs={{8,0},{16,8},{24,16},{9,1},{17,9},{25,17},{10,2},{18,10},{26,18},{... | collective-permute-start | bytes 393224 | tf_op jit(solution)/shard_map/ppermute | solution.py:12
  122.4 7.2 %collective-permute-start.6 = (f32[256,128]{0,1:T(8,128)S(1)}, f32[256,128]{0,1:T(8,128)S(1)}, u32[]{:S(2)}, u32[]{:S(2)}) collective-permute-start(f32[256,128]{0,1:T(8,128)S(1)} %get-tuple-element.11), channel_id=1, source_target_pairs={{0,8},{8,16},{16,24},{1,9},{9,17},{17,25},{2,10},{10,18},{18,26},{... | collective-permute-start | bytes 393224 | tf_op jit(solution)/shard_map/ppermute | solution.py:12
  127.2 5.5 %collective-permute-start.5 = (f32[256,128]{0,1:T(8,128)S(1)}, f32[256,128]{0,1:T(8,128)S(1)}, u32[]{:S(2)}, u32[]{:S(2)}) collective-permute-start(f32[256,128]{0,1:T(8,128)S(1)} %get-tuple-element.12), channel_id=1, source_target_pairs={{1,0},{2,1},{3,2},{4,3},{5,4},{6,5},{7,6},{9,8},{10,9},{11,10},{12... | collective-permute-start | bytes 393224 | tf_op jit(solution)/shard_map/ppermute | solution.py:12
  128.5 4.2 %copy-start.4 = (f32[256,128]{0,1:T(8,128)}, f32[256,128]{0,1:T(8,128)S(1)}, u32[]{:S(2)}) copy-start(f32[256,128]{0,1:T(8,128)S(1)} %collective-permute-done.4) | copy-start | bytes 393220
  128.5 4.7 %copy-start.5 = (f32[256,128]{0,1:T(8,128)}, f32[256,128]{0,1:T(8,128)S(1)}, u32[]{:S(2)}) copy-start(f32[256,128]{0,1:T(8,128)S(1)} %collective-permute-done.7) | copy-start | bytes 393220
  129.7 3.6 %copy-start.6 = (f32[256,128]{0,1:T(8,128)}, f32[256,128]{0,1:T(8,128)S(1)}, u32[]{:S(2)}) copy-start(f32[256,128]{0,1:T(8,128)S(1)} %collective-permute-done.6) | copy-start | bytes 393220
  190.7 2.9 %copy-start.2 = (bf16[1,1,1024,1024]{3,2,1,0:T(8,128)(2,1)S(1)}, bf16[1,1,1024,1024]{3,2,1,0:T(8,128)(2,1)}, u32[]{:S(2)}) copy-start(bf16[1,1,1024,1024]{3,2,1,0:T(8,128)(2,1)} %param.9) | copy-start | bytes 6291460
  192.6 39.5 %copy-start.9 = (f32[1024]{0:T(1024)S(1)}, f32[1024]{0:T(1024)}, u32[]{:S(2)}) copy-start(f32[1024]{0:T(1024)} %copy-done.8) | copy-start | bytes 12292
  192.7 39.5 %copy-start.12 = (f32[1024]{0:T(1024)S(1)}, f32[1024]{0:T(1024)}, u32[]{:S(2)}) copy-start(f32[1024]{0:T(1024)} %copy-done.11) | copy-start | bytes 12292
  192.7 39.5 %copy-start.15 = (f32[128]{0:T(128)S(1)}, f32[128]{0:T(128)}, u32[]{:S(2)}) copy-start(f32[128]{0:T(128)} %copy-done.14) | copy-start | bytes 1540
  (1 other events, 0.7 us)
where the time goes:
time: 236 us; the launch traced here: 235 us
  blocking collectives  187 us (79%)
  starting transfers between devices  18.5 us (8%)
  matrix products  15.4 us (7%)
  waiting for transfers between devices  7.22 us (3%)
  local copies, waits for them, and re-layouts  4.43 us (2%)
    psum x2, blocking collectives, local(): gain = lax.psum(gain_local, ('row', 'col'))  75.1 us
    psum x2, blocking collectives, local(): total = lax.psum(partial_value, 'col')  48.7 us
    psum x2, blocking collectives, broadcast(): return lax.psum(block, axis)  36.1 us
    all_gather x2, blocking collectives, local(): gathered = lax.all_gather(corner_force, 'row', axis=0, tiled=True)  26.9 us
    ppermute x8, starting transfers between devices, passed_along(): return lax.ppermute(x, axis, pairs)  18.5 us
    ppermute x8, waiting for transfers between devices, passed_along(): return lax.ppermute(x, axis, pairs)  7.22 us
    dot_general x2, matrix products, local(): jnp.dot(flex_block, lam.astype(jnp.bfloat16), preferred_element_type=jnp....  4.86 us
  transfers between devices with their start and end apart: 8, of which 4 were waited for; matrix products, arithmetic and copies ran while one was open for 0% of the time, Pallas kernels for 0%

commit v1 on v0

v1 whole, which is shorter than its diff:
```python
import jax
import jax.numpy as jnp
from jax import lax
from jax.sharding import PartitionSpec as P

ITERS = 2
ALL = ("row", "col")
HIGH = lax.Precision.HIGHEST


def passed_round(x, axis, by):
    count = lax.axis_size(axis)
    return lax.ppermute(x, axis, [(i, (i + by) % count) for i in range(count)])


def shared(x):
    count = lax.axis_size(ALL)
    copies = jnp.broadcast_to(x[None], (count, *x.shape))
    return lax.all_to_all(copies, ALL, 0, 0, tiled=True)


def local(
    slip_load,
    flexibility,
    schur,
    corner_coupling,
    coarse_inverse,
    bounds_table,
    bound_index,
    face_rows,
):
    loads = slip_load[0, 0].astype(jnp.float32)
    flex_block = flexibility[0, 0]
    schur_block = schur[0, 0]
    coupling = corner_coupling[0, 0]
    row_count = flex_block.shape[0]
    face_size = row_count // 4
    corners = coupling.shape[0]
    rows, cols = lax.axis_size("row"), lax.axis_size("col")
    padded = -(-corners // 8) * 8
    levels = jnp.arange(bounds_table.shape[0], dtype=jnp.int32)
    onehot = (bound_index[0, 0][:, None] == levels[None, :]).astype(jnp.float32)
    bound = jnp.sum(onehot * bounds_table[None, :], axis=1)[:, None]
    slots = jnp.arange(face_size, dtype=jnp.int32)
    live = (slots[None, :] < face_rows[0, 0][:, None]).astype(jnp.float32).reshape(row_count, 1)

    mine = lax.all_to_all(coarse_inverse.T, "row", 0, 1, tiled=True)
    mine = mine.reshape(corners, cols, rows, corners).transpose(0, 2, 1, 3)
    mine = jnp.pad(mine, ((0, 0), (0, 0), (0, 0), (0, padded - corners)))
    mine = mine.reshape(corners, rows * cols * padded)

    lam = jnp.clip(loads, -bound, bound)
    for iteration in range(ITERS):
        displacement = jnp.dot(
            flex_block, lam.astype(jnp.bfloat16), preferred_element_type=jnp.float32
        )
        faces = displacement.reshape(4, face_size, -1)
        nb_lower = passed_round(faces[3], "row", 1)
        nb_upper = passed_round(faces[2], "row", -1)
        nb_west = passed_round(faces[1], "col", 1)
        nb_east = passed_round(faces[0], "col", -1)
        paired = jnp.concatenate([nb_west, nb_east, nb_lower, nb_upper], axis=0)
        jump = live * (displacement - paired - loads)
        corner_force = jnp.dot(coupling, jump, precision=HIGH)
        forces = shared(jnp.pad(corner_force, ((0, padded - corners), (0, 0))))
        coarse = jnp.dot(mine, forces.reshape(-1, forces.shape[-1]), precision=HIGH)
        correction = lax.dot_general(
            coupling, coarse, (((0,), (0,)), ((), ())), precision=HIGH
        )
        projected = jump - correction
        projected_b = projected.astype(jnp.bfloat16)
        search = jnp.dot(schur_block, projected_b, preferred_element_type=jnp.float32)
        gain = jnp.sum(projected_b.astype(jnp.float32) * search, axis=0)
        search_b = search.astype(jnp.bfloat16)
        curved = jnp.dot(flex_block, search_b, preferred_element_type=jnp.float32)
        curvature = jnp.sum(search_b.astype(jnp.float32) * curved, axis=0)
        sums = jnp.sum(shared(jnp.stack([gain, curvature])), axis=0)
        lam = jnp.clip(lam - (sums[0] / sums[1])[None, :] * search, -bound, bound)
    return lam.astype(jnp.bfloat16)[None, None]


def solution(mesh):
    return jax.shard_map(
        local,
        mesh=mesh,
        in_specs=(
            P("row", "col", None, None),
            P("row", "col", None, None),
            P("row", "col", None, None),
            P("row", "col", None, None),
            P("row", "col"),
            P(),
            P("row", "col", None),
            P("row", "col", None),
        ),
        out_specs=P("row", "col", None, None),
        check_vma=False,
    )
```

time: 236 us -> 93.9 us (0.40)
  blocking collectives: 187 us -> 32 us
  waiting for transfers between devices: 7.22 us -> 19.1 us
  matrix products: 15.4 us -> 12.6 us
  local copies, waits for them, and re-layouts: 4.43 us -> 7.11 us
    psum x6 -> x0, blocking collectives: 160 us -> none  [the longest x2 75.1 us: local(): gain = lax.psum(gain_local, ('row', 'col'))]
    all_to_all x0 -> x3, blocking collectives: none -> 32 us  [shared(): return lax.all_to_all(copies, ALL, 0, 0, tiled=True)]
    all_gather x2 -> x0, blocking collectives: 26.9 us -> none  [local(): gathered = lax.all_gather(corner_force, 'row', axis=0, tiled=True)]
    all_to_all x0 -> x2, starting transfers between devices: none -> 9.74 us  [the longest x1 6.35 us: local(): mine = lax.all_to_all(coarse_inverse.T, 'row', 0, 1, tiled=True)]
    all_to_all x0 -> x2, waiting for transfers between devices: none -> 8.86 us  [the longest x1 8.85 us: shared(): return lax.all_to_all(copies, ALL, 0, 0, tiled=True)]
    ppermute x8, starting transfers between devices: 18.5 us -> 10.4 us  [passed_round(): return lax.ppermute(x, axis, [(i, (i + by) % count) for i in range(count)])]
    ppermute x8, waiting for transfers between devices: 7.22 us -> 10.3 us  [passed_round(): return lax.ppermute(x, axis, [(i, (i + by) % count) for i in range(count)])]
    dot_general x6, matrix products: 6.9 us -> 4.08 us  [the longest x2 2.48 us: local(): lax.dot_general(coupling, coarse, (((0,), (0,)), ((), ())), precision=HIGH)]
  transfers between devices with their start and end apart: 8 -> 10, of which waited for: 4 -> 6; matrix products, arithmetic and copies ran while one was open for 0% -> 7% of each run, Pallas kernels for 0% -> 0%
where the time goes in v1:
time: 93.9 us; the launch traced here: 93.3 us
  blocking collectives  32 us (34%)
  starting transfers between devices  20.1 us (21%)
  waiting for transfers between devices  19.1 us (20%)
  matrix products  12.6 us (13%)
  local copies, waits for them, and re-layouts  7.11 us (8%)
  other arithmetic  1.98 us (2%)
    all_to_all x3, blocking collectives, shared(): return lax.all_to_all(copies, ALL, 0, 0, tiled=True)  32 us
    ppermute x8, starting transfers between devices, passed_round(): return lax.ppermute(x, axis, [(i, (i + by) % count) for i in range(count)])  10.4 us
    ppermute x8, waiting for transfers between devices, passed_round(): return lax.ppermute(x, axis, [(i, (i + by) % count) for i in range(count)])  10.3 us
    all_to_all x1, waiting for transfers between devices, shared(): return lax.all_to_all(copies, ALL, 0, 0, tiled=True)  8.85 us
    all_to_all x1, starting transfers between devices, local(): mine = lax.all_to_all(coarse_inverse.T, 'row', 0, 1, tiled=True)  6.35 us
    dot_general x2, matrix products, local(): jnp.dot(flex_block, lam.astype(jnp.bfloat16), preferred_element_type=jnp....  4.86 us
    all_to_all x1, starting transfers between devices, shared(): return lax.all_to_all(copies, ALL, 0, 0, tiled=True)  3.39 us
    dot_general x2, matrix products, local(): lax.dot_general(coupling, coarse, (((0,), (0,)), ((), ())), precision=HIGH)  2.48 us
  transfers between devices with their start and end apart: 10, of which 6 were waited for; matrix products, arithmetic and copies ran while one was open for 7% of the time, Pallas kernels for 0%

profile of v1, /device:TPU:0, one launch (start us, length us, event | category | flops | bytes accessed | tf_op | source)
XLA Modules:
  0.0 93.3 jit_solution(16045332967238421108)
XLA Ops:
  0.0 1.5 %all_to_all.24 = f32[4,12,96]{2,1,0:T(8,128)} reshape(f32[48,96]{1,0:T(8,128)} %bitcast.155) | data formatting | bytes 36864 | tf_op jit(solution)/shard_map/all_to_all | solution.py:47
  1.5 6.3 %all-to-all-start = ((f32[4,12,96]{2,1,0:T(8,128)}), f32[4,12,96]{2,1,0:T(8,128)S(1)}, u32[]{:S(2)}, u32[]{:S(2)}) async-start(f32[4,12,96]{2,1,0:T(8,128)} %all_to_all.24), calls=%async_computation | async-start | bytes 65536 | tf_op jit(solution)/shard_map/all_to_all | solution.py:47
  8.7 1.1 %copy.19 = bf16[1,1,1024,128]{2,3,1,0:T(8,128)(2,1)S(1)} copy(bf16[1,1,1024,128]{3,2,1,0:T(8,128)(2,1)} %param.8) | data formatting | bytes 524288 | tf_op args[0]
  9.8 2.4 %fusion.14 = f32[1024,128]{0,1:T(8,128)S(1)} fusion(bf16[1,1,1024,1024]{3,2,1,0:T(8,128)(2,1)} %param.9, bf16[1,1,1024,128]{2,3,1,0:T(8,128)(2,1)S(1)} %copy.19, f32[1024]{0:T(1024)S(1)} %neg.10, f32[1024]{0:T(1024)S(1)} %select_reduce_fusion), kind=kOutput, calls=%fused_computation.16 | convolution fusion | flops 269221888 | bytes 2891776 | tf_op jit(solution)/shard_map/dot_general | solution.py:54
  12.4 3.9 %collective-permute-start.3 = (f32[256,128]{0,1:T(8,128)S(1)}, f32[256,128]{0,1:T(8,128)S(1)}, u32[]{:S(2)}, u32[]{:S(2)}) collective-permute-start(f32[256,128]{0,1:T(8,128)S(1)} %get-tuple-element.10), channel_id=1, source_target_pairs={{0,24},{8,0},{16,8},{24,16},{1,25},{9,1},{17,9},{25,17},{2,26},{10... | collective-permute-start | bytes 393224 | tf_op jit(solution)/shard_map/ppermute | solution.py:13
  16.2 2.3 %collective-permute-start.1 = (f32[256,128]{0,1:T(8,128)S(1)}, f32[256,128]{0,1:T(8,128)S(1)}, u32[]{:S(2)}, u32[]{:S(2)}) collective-permute-start(f32[256,128]{0,1:T(8,128)S(1)} %get-tuple-element.12), channel_id=1, source_target_pairs={{0,7},{1,0},{2,1},{3,2},{4,3},{5,4},{6,5},{7,6},{8,15},{9,8},{10,9... | collective-permute-start | bytes 393224 | tf_op jit(solution)/shard_map/ppermute | solution.py:13
  18.6 1.0 %collective-permute-done.3 = f32[256,128]{0,1:T(8,128)S(1)} collective-permute-done((f32[256,128]{0,1:T(8,128)S(1)}, f32[256,128]{0,1:T(8,128)S(1)}, u32[]{:S(2)}, u32[]{:S(2)}) %collective-permute-start.3) | collective-permute-done | bytes 131104 | tf_op jit(solution)/shard_map/ppermute | solution.py:13
  19.6 4.5 %collective-permute-done.2 = f32[256,128]{0,1:T(8,128)S(1)} collective-permute-done((f32[256,128]{0,1:T(8,128)S(1)}, f32[256,128]{0,1:T(8,128)S(1)}, u32[]{:S(2)}, u32[]{:S(2)}) %collective-permute-start.2) | collective-permute-done | bytes 131104 | tf_op jit(solution)/shard_map/ppermute | solution.py:13
  25.5 3.4 %all-to-all-start.1 = ((f32[32,16,128]{2,1,0:T(8,128)}), f32[32,16,128]{2,1,0:T(8,128)S(1)}, u32[]{:S(2)}, u32[]{:S(2)}) async-start(f32[32,16,128]{2,1,0:T(8,128)} %broadcast_in_dim.10), calls=%async_computation.1 | async-start | bytes 524288 | tf_op jit(solution)/shard_map/all_to_all | solution.py:19
  30.7 8.9 %all-to-all-done.1 = f32[32,16,128]{2,1,0:T(8,128)S(1)} async-done(((f32[32,16,128]{2,1,0:T(8,128)}), f32[32,16,128]{2,1,0:T(8,128)S(1)}, u32[]{:S(2)}, u32[]{:S(2)}) %all-to-all-start.1) | async-done | bytes 262176 | tf_op jit(solution)/shard_map/all_to_all | solution.py:19
  39.8 1.8 %fusion.39 = bf16[1024,128]{0,1:T(8,128)(2,1)S(1)} fusion(f32[12,128]{1,0:T(8,128)S(1)} %fusion.80, f32[1,1,12,1024]{3,1,2,0:T(1,128)S(1)} %copy-done.3, bf16[1,1,1024,128]{2,3,1,0:T(8,128)(2,1)S(1)} %copy.19, f32[1024,128]{0,1:T(8,128)S(1)} %fusion.14, f32[256,128]{0,1:T(8,128)} %copy-done.4, f32[256,128]{0,1:T(8,128)} %copy-done.5, ...), kind=kOutput, calls=%fused_computation.25 | convolution fusion | flops 20054016 | bytes 1632256 | tf_op jit(solution)/shard_map/dot_general | solution.py:67
  42.5 0.9 fusion.40
  43.5 9.5 %all_to_all.36 = f32[32,2,128]{2,1,0:T(2,128)S(1)} all-to-all(f32[32,2,128]{2,1,0:T(2,128)S(1)} %broadcast_in_dim.11), channel_id=1, replica_groups=mesh['row'=4,'col'=8] {'row','col'}, dimensions={0} | all-to-all | bytes 65536 | tf_op jit(solution)/shard_map/all_to_all | solution.py:19
  53.0 2.4 %fusion.20 = f32[1024,128]{0,1:T(8,128)S(1)} fusion(bf16[1,1,1024,1024]{3,2,1,0:T(8,128)(2,1)} %param.9, bf16[1,1,1024,128]{2,3,1,0:T(8,128)(2,1)S(1)} %copy.19, f32[1024,128]{0,1:T(8,128)S(1)} %get-tuple-element.14, f32[128]{0:T(128)S(1)} %fusion.74, f32[1024]{0:T(1024)S(1)} %copy-done.10, f32[1024]{0:T(1024)S(1)} %copy-done.8), kind=kOutput, calls=%fused_computation.18 | convolution fusion | flops 269484032 | bytes 3416576 | tf_op jit(solution)/shard_map/dot_general | solution.py:54
  56.2 1.5 %collective-permute-start.6 = (f32[256,128]{0,1:T(8,128)S(1)}, f32[256,128]{0,1:T(8,128)S(1)}, u32[]{:S(2)}, u32[]{:S(2)}) collective-permute-start(f32[256,128]{0,1:T(8,128)S(1)} %get-tuple-element.7), channel_id=1, source_target_pairs={{0,8},{8,16},{16,24},{24,0},{1,9},{9,17},{17,25},{25,1},{2,10},{10... | collective-permute-start | bytes 393224 | tf_op jit(solution)/shard_map/ppermute | solution.py:13
  57.7 2.0 %collective-permute-start.5 = (f32[256,128]{0,1:T(8,128)S(1)}, f32[256,128]{0,1:T(8,128)S(1)}, u32[]{:S(2)}, u32[]{:S(2)}) collective-permute-start(f32[256,128]{0,1:T(8,128)S(1)} %get-tuple-element.8), channel_id=1, source_target_pairs={{0,7},{1,0},{2,1},{3,2},{4,3},{5,4},{6,5},{7,6},{8,15},{9,8},{10,9... | collective-permute-start | bytes 393224 | tf_op jit(solution)/shard_map/ppermute | solution.py:13
  59.7 1.2 %collective-permute-done.4 = f32[256,128]{0,1:T(8,128)S(1)} collective-permute-done((f32[256,128]{0,1:T(8,128)S(1)}, f32[256,128]{0,1:T(8,128)S(1)}, u32[]{:S(2)}, u32[]{:S(2)}) %collective-permute-start.4) | collective-permute-done | bytes 131104 | tf_op jit(solution)/shard_map/ppermute | solution.py:13
  60.9 1.1 %collective-permute-done.7 = f32[256,128]{0,1:T(8,128)S(1)} collective-permute-done((f32[256,128]{0,1:T(8,128)S(1)}, f32[256,128]{0,1:T(8,128)S(1)}, u32[]{:S(2)}, u32[]{:S(2)}) %collective-permute-start.7) | collective-permute-done | bytes 131104 | tf_op jit(solution)/shard_map/ppermute | solution.py:13
  61.9 2.5 %collective-permute-done.6 = f32[256,128]{0,1:T(8,128)S(1)} collective-permute-done((f32[256,128]{0,1:T(8,128)S(1)}, f32[256,128]{0,1:T(8,128)S(1)}, u32[]{:S(2)}, u32[]{:S(2)}) %collective-permute-start.6) | collective-permute-done | bytes 131104 | tf_op jit(solution)/shard_map/ppermute | solution.py:13
  65.1 13.1 %all_to_all.37 = f32[32,16,128]{2,1,0:T(8,128)S(1)} all-to-all(f32[32,16,128]{2,1,0:T(8,128)S(1)} %broadcast_in_dim.12), channel_id=1, replica_groups=mesh['row'=4,'col'=8] {'row','col'}, dimensions={0} | all-to-all | bytes 524288 | tf_op jit(solution)/shard_map/all_to_all | solution.py:19
  80.0 0.9 fusion.43
  81.0 9.5 %all_to_all.38 = f32[32,2,128]{2,1,0:T(2,128)S(1)} all-to-all(f32[32,2,128]{2,1,0:T(2,128)S(1)} %broadcast_in_dim.13), channel_id=1, replica_groups=mesh['row'=4,'col'=8] {'row','col'}, dimensions={0} | all-to-all | bytes 65536 | tf_op jit(solution)/shard_map/all_to_all | solution.py:19
  90.5 1.0 %fusion.57 = bf16[1,1,1024,128]{2,3,1,0:T(8,128)(2,1)} fusion(f32[1024,128]{0,1:T(8,128)S(1)} %get-tuple-element.16, f32[128]{0:T(128)S(1)} %fusion.75, f32[1024]{0:T(1024)S(1)} %copy-done.10, f32[1024]{0:T(1024)S(1)} %copy-done.8, f32[1024,128]{0,1:T(8,128)S(1)} %get-tuple-element.14, f32[128]{0:T(128)S(1)} %fusion.74, bf16[1,1,1024,128]{2,3,1,0:T(8,128)(2,1)S(1)} %copy.19), kind=kLoop, calls=%fused_computation.48 | loop fusion | flops 1572864 | bytes 1582080 | tf_op jit(solution)/shard_map/broadcast_in_dim | solution.py:79
  91.5 1.8 %copy.24 = bf16[1,1,1024,128]{3,2,1,0:T(8,128)(2,1)} copy(bf16[1,1,1024,128]{2,3,1,0:T(8,128)(2,1)} %fusion.57) | data formatting | bytes 524288 | tf_op jit(solution)/shard_map/broadcast_in_dim | solution.py:79
  (66 shorter events, 8.6 us)
Async XLA Ops:
  0.0 41.6 %copy-start = (bf16[1,1,1024,1024]{3,2,1,0:T(8,128)(2,1)S(1)}, bf16[1,1,1024,1024]{3,2,1,0:T(8,128)(2,1)}, u32[]{:S(2)}) copy-start(bf16[1,1,1024,1024]{3,2,1,0:T(8,128)(2,1)} %param.10) | copy-start | bytes 6291460
  1.5 23.3 %all-to-all-start = ((f32[4,12,96]{2,1,0:T(8,128)}), f32[4,12,96]{2,1,0:T(8,128)S(1)}, u32[]{:S(2)}, u32[]{:S(2)}) async-start(f32[4,12,96]{2,1,0:T(8,128)} %all_to_all.24), calls=%async_computation | async-start | bytes 65536 | tf_op jit(solution)/shard_map/all_to_all | solution.py:47
  8.6 3.6 %copy-start.7 = (f32[1024]{0:T(1024)}, f32[1024]{0:T(1024)S(1)}, u32[]{:S(2)}) copy-start(f32[1024]{0:T(1024)S(1)} %select_reduce_fusion) | copy-start | bytes 12292
  8.7 3.6 %copy-start.9 = (f32[1024]{0:T(1024)}, f32[1024]{0:T(1024)S(1)}, u32[]{:S(2)}) copy-start(f32[1024]{0:T(1024)S(1)} %neg.10) | copy-start | bytes 12292
  9.8 8.8 %copy-start.13 = (s32[1,1,4]{2,1,0:T(1,128)S(1)}, s32[1,1,4]{2,1,0:T(1,128)}, u32[]{:S(2)}) copy-start(s32[1,1,4]{2,1,0:T(1,128)} %param.15) | copy-start | bytes 52
  9.8 14.4 %copy-start.3 = (f32[1,1,12,1024]{3,1,2,0:T(1,128)S(1)}, f32[1,1,12,1024]{3,1,2,0:T(1,128)}, u32[]{:S(2)}) copy-start(f32[1,1,12,1024]{3,1,2,0:T(1,128)} %param.11) | copy-start | bytes 147460
  12.3 6.3 %collective-permute-start = (f32[256,128]{0,1:T(8,128)S(1)}, f32[256,128]{0,1:T(8,128)S(1)}, u32[]{:S(2)}, u32[]{:S(2)}) collective-permute-start(f32[256,128]{0,1:T(8,128)S(1)} %get-tuple-element.9), channel_id=1, source_target_pairs={{0,1},{1,2},{2,3},{3,4},{4,5},{5,6},{6,7},{7,0},{8,9},{9,10},{10,1... | collective-permute-start | bytes 393224 | tf_op jit(solution)/shard_map/ppermute | solution.py:13
  12.4 7.2 %collective-permute-start.3 = (f32[256,128]{0,1:T(8,128)S(1)}, f32[256,128]{0,1:T(8,128)S(1)}, u32[]{:S(2)}, u32[]{:S(2)}) collective-permute-start(f32[256,128]{0,1:T(8,128)S(1)} %get-tuple-element.10), channel_id=1, source_target_pairs={{0,24},{8,0},{16,8},{24,16},{1,25},{9,1},{17,9},{25,17},{2,26},{10... | collective-permute-start | bytes 393224 | tf_op jit(solution)/shard_map/ppermute | solution.py:13
  16.2 7.9 %collective-permute-start.2 = (f32[256,128]{0,1:T(8,128)S(1)}, f32[256,128]{0,1:T(8,128)S(1)}, u32[]{:S(2)}, u32[]{:S(2)}) collective-permute-start(f32[256,128]{0,1:T(8,128)S(1)} %get-tuple-element.11), channel_id=1, source_target_pairs={{0,8},{8,16},{16,24},{24,0},{1,9},{9,17},{17,25},{25,1},{2,10},{10... | collective-permute-start | bytes 393224 | tf_op jit(solution)/shard_map/ppermute | solution.py:13
  16.2 7.9 %collective-permute-start.1 = (f32[256,128]{0,1:T(8,128)S(1)}, f32[256,128]{0,1:T(8,128)S(1)}, u32[]{:S(2)}, u32[]{:S(2)}) collective-permute-start(f32[256,128]{0,1:T(8,128)S(1)} %get-tuple-element.12), channel_id=1, source_target_pairs={{0,7},{1,0},{2,1},{3,2},{4,3},{5,4},{6,5},{7,6},{8,15},{9,8},{10,9... | collective-permute-start | bytes 393224 | tf_op jit(solution)/shard_map/ppermute | solution.py:13
  18.6 6.1 %copy-start.11 = (f32[1,2,4,128]{3,1,2,0:T(2,128)}, f32[1,2,4,128]{3,1,2,0:T(2,128)S(1)}, u32[]{:S(2)}) copy-start(f32[1,2,4,128]{3,1,2,0:T(2,128)S(1)} %copy.33) | copy-start | bytes 12292
  19.6 4.5 %copy-start.4 = (f32[256,128]{0,1:T(8,128)}, f32[256,128]{0,1:T(8,128)S(1)}, u32[]{:S(2)}) copy-start(f32[256,128]{0,1:T(8,128)S(1)} %collective-permute-done.3) | copy-start | bytes 393220
  24.1 0.7 copy-start.5
  24.1 0.7 copy-start.6
  25.5 14.0 %all-to-all-start.1 = ((f32[32,16,128]{2,1,0:T(8,128)}), f32[32,16,128]{2,1,0:T(8,128)S(1)}, u32[]{:S(2)}, u32[]{:S(2)}) async-start(f32[32,16,128]{2,1,0:T(8,128)} %broadcast_in_dim.10), calls=%async_computation.1 | async-start | bytes 524288 | tf_op jit(solution)/shard_map/all_to_all | solution.py:19
  39.8 2.8 %copy-start.1 = (bf16[1,1,1024,1024]{3,2,1,0:T(8,128)(2,1)S(1)}, bf16[1,1,1024,1024]{3,2,1,0:T(8,128)(2,1)}, u32[]{:S(2)}) copy-start(bf16[1,1,1024,1024]{3,2,1,0:T(8,128)(2,1)} %param.9) | copy-start | bytes 6291460
  42.5 10.5 %copy-start.8 = (f32[1024]{0:T(1024)S(1)}, f32[1024]{0:T(1024)}, u32[]{:S(2)}) copy-start(f32[1024]{0:T(1024)} %copy-done.7) | copy-start | bytes 12292
  42.5 10.5 %copy-start.10 = (f32[1024]{0:T(1024)S(1)}, f32[1024]{0:T(1024)}, u32[]{:S(2)}) copy-start(f32[1024]{0:T(1024)} %copy-done.9) | copy-start | bytes 12292
  53.0 11.4 %copy-start.12 = (f32[1,2,4,128]{3,1,2,0:T(2,128)S(1)}, f32[1,2,4,128]{3,1,2,0:T(2,128)}, u32[]{:S(2)}) copy-start(f32[1,2,4,128]{3,1,2,0:T(2,128)} %copy-done.11) | copy-start | bytes 12292
  55.5 5.3 %collective-permute-start.4 = (f32[256,128]{0,1:T(8,128)S(1)}, f32[256,128]{0,1:T(8,128)S(1)}, u32[]{:S(2)}, u32[]{:S(2)}) collective-permute-start(f32[256,128]{0,1:T(8,128)S(1)} %get-tuple-element.5), channel_id=1, source_target_pairs={{0,1},{1,2},{2,3},{3,4},{4,5},{5,6},{6,7},{7,0},{8,9},{9,10},{10,1... | collective-permute-start | bytes 393224 | tf_op jit(solution)/shard_map/ppermute | solution.py:13
  55.7 6.3 %collective-permute-start.7 = (f32[256,128]{0,1:T(8,128)S(1)}, f32[256,128]{0,1:T(8,128)S(1)}, u32[]{:S(2)}, u32[]{:S(2)}) collective-permute-start(f32[256,128]{0,1:T(8,128)S(1)} %get-tuple-element.6), channel_id=1, source_target_pairs={{0,24},{8,0},{16,8},{24,16},{1,25},{9,1},{17,9},{25,17},{2,26},{10... | collective-permute-start | bytes 393224 | tf_op jit(solution)/shard_map/ppermute | solution.py:13
  56.2 8.2 %collective-permute-start.6 = (f32[256,128]{0,1:T(8,128)S(1)}, f32[256,128]{0,1:T(8,128)S(1)}, u32[]{:S(2)}, u32[]{:S(2)}) collective-permute-start(f32[256,128]{0,1:T(8,128)S(1)} %get-tuple-element.7), channel_id=1, source_target_pairs={{0,8},{8,16},{16,24},{24,0},{1,9},{9,17},{17,25},{25,1},{2,10},{10... | collective-permute-start | bytes 393224 | tf_op jit(solution)/shard_map/ppermute | solution.py:13
  57.7 6.7 %collective-permute-start.5 = (f32[256,128]{0,1:T(8,128)S(1)}, f32[256,128]{0,1:T(8,128)S(1)}, u32[]{:S(2)}, u32[]{:S(2)}) collective-permute-start(f32[256,128]{0,1:T(8,128)S(1)} %get-tuple-element.8), channel_id=1, source_target_pairs={{0,7},{1,0},{2,1},{3,2},{4,3},{5,4},{6,5},{7,6},{8,15},{9,8},{10,9... | collective-permute-start | bytes 393224 | tf_op jit(solution)/shard_map/ppermute | solution.py:13
  78.4 1.6 %copy-start.2 = (bf16[1,1,1024,1024]{3,2,1,0:T(8,128)(2,1)S(1)}, bf16[1,1,1024,1024]{3,2,1,0:T(8,128)(2,1)}, u32[]{:S(2)}) copy-start(bf16[1,1,1024,1024]{3,2,1,0:T(8,128)(2,1)} %param.9) | copy-start | bytes 6291460

commit v2 on v1

v2 whole, which is shorter than its diff:
```python
import functools

import jax
import jax.numpy as jnp
from jax import lax
from jax.experimental import pallas as pl
from jax.experimental.pallas import tpu as pltpu
from jax.sharding import PartitionSpec as P


ITERS = 2
ALL = ("row", "col")
F32 = jnp.float32
BF16 = jnp.bfloat16
VMEM = pl.BlockSpec(memory_space=pltpu.VMEM)
HBM = pl.BlockSpec(memory_space=pltpu.HBM)


def kernel_call(body, specs, outs, flops, scratch=()):
    return pl.pallas_call(
        body,
        in_specs=specs,
        out_specs=[VMEM] * len(outs),
        out_shape=[jax.ShapeDtypeStruct(shape, dtype) for shape, dtype in outs],
        compiler_params=pltpu.CompilerParams(vmem_limit_bytes=16 << 20),
        cost_estimate=pl.CostEstimate(flops=flops, bytes_accessed=4 << 20, transcendentals=0),
        scratch_shapes=scratch,
    )


def passed_round(x, axis, by):
    count = lax.axis_size(axis)
    return lax.ppermute(x, axis, [(i, (i + by) % count) for i in range(count)])


def from_sides(west, east, lower, upper):
    return [
        passed_round(east, "col", 1),
        passed_round(west, "col", -1),
        passed_round(upper, "row", 1),
        passed_round(lower, "row", -1),
    ]


def in_hbm(x):
    return pltpu.with_memory_space_constraint(x, pltpu.HBM)


def halves(x):
    high = x.astype(BF16)
    return high, (x - high.astype(F32)).astype(BF16)


def fine_dot(a, b):
    a_high, a_low = halves(a)
    b_high, b_low = halves(b)
    both = jnp.concatenate([a_high, a_low], axis=0)
    out = jnp.dot(both, b_high, preferred_element_type=F32)
    rows = a.shape[0]
    return out[:rows] + out[rows:] + jnp.dot(a_high, b_low, preferred_element_type=F32)


def put_faces(flex_ref, lam, face_refs):
    displacement = jnp.dot(flex_ref[...], lam.astype(BF16), preferred_element_type=F32)
    size = face_refs[0].shape[0]
    for f, ref in enumerate(face_refs):
        ref[...] = displacement[f * size : (f + 1) * size]


def begin(levels, table_hbm, index_hbm, live_hbm, loads_hbm, block_hbm, coupling_hbm, *refs):
    flex_hbm, bound_ref, limit_ref, weights_ref, flex_ref = refs[:5]
    face_refs, own_refs = refs[5:9], refs[9:-7]
    table_ref, index_ref, live_ref, loads_ref, block_ref, coupling_ref, sems = refs[-7:]
    size = face_refs[0].shape[0]
    pairs = [
        (table_hbm, table_ref),
        (index_hbm, index_ref),
        (loads_hbm, loads_ref),
        (live_hbm, live_ref),
        (block_hbm, block_ref),
        (coupling_hbm, coupling_ref),
    ]
    slabs = [pl.ds(f * size, size) for f in range(4)]
    pairs += [(flex_hbm.at[slab], flex_ref.at[slab]) for slab in slabs]
    copies = [
        pltpu.make_async_copy(source, target, sems.at[i])
        for i, (source, target) in enumerate(pairs)
    ]
    for copy in copies:
        copy.start()
    for copy in copies[:3]:
        copy.wait()
    index = index_ref[...]
    row = jnp.zeros(index.shape, F32)
    for level in range(levels):
        row = jnp.where(index == level, table_ref[level], row)
    bound = jnp.transpose(jnp.broadcast_to(row, (loads_ref.shape[1], row.shape[1])))
    bound_ref[...] = bound
    lam = jnp.clip(loads_ref[...].astype(F32), -bound, bound).astype(BF16)
    for copy in copies[3:6]:
        copy.wait()
    for f in range(4):
        limit_ref[f : f + 1, :] = jnp.full((1, limit_ref.shape[1]), live_ref[0, f], jnp.int32)
    own(block_ref, *own_refs)
    corners, _, length = coupling_ref.shape
    padded = weights_ref.shape[0] // 3
    coupling = coupling_ref[...].reshape(corners, length)
    if padded > corners:
        rest = jnp.zeros((padded - corners, length), F32)
        coupling = jnp.concatenate([coupling, rest], axis=0)
    high, low = halves(coupling)
    weights_ref[...] = jnp.concatenate([high, low, high], axis=0)
    for f, ref in enumerate(face_refs):
        copies[6 + f].wait()
        ref[...] = jnp.dot(flex_ref[slabs[f], :], lam, preferred_element_type=F32)


def stepped(sums_ref, lam, search_ref, bound):
    sums = jnp.sum(sums_ref[...], axis=0)
    return jnp.clip(lam - (sums[0:1] / sums[1:2]) * search_ref[...], -bound, bound)


def again(sums_ref, loads_ref, search_ref, bound_ref, flex_ref, lam_ref, *face_refs):
    bound = bound_ref[...]
    lam = jnp.clip(loads_ref[...].astype(F32), -bound, bound)
    lam = stepped(sums_ref, lam, search_ref, bound)
    lam_ref[...] = lam
    put_faces(flex_ref, lam, face_refs)


def end(sums_ref, lam_ref, search_ref, bound_ref, out_ref):
    out_ref[...] = stepped(sums_ref, lam_ref[...], search_ref, bound_ref[...]).astype(BF16)


def own(block_ref, *own_refs):
    rows = len(own_refs)
    corners = block_ref.shape[0] // rows
    parts = [block_ref[r * corners : (r + 1) * corners, :] for r in range(rows)]
    for k, ref in enumerate(own_refs):
        up = lax.rem(lax.axis_index("row") + k, rows)
        chosen = parts[0]
        for r in range(1, rows):
            chosen = jnp.where(up == r, parts[r], chosen)
        ref[...] = jnp.zeros(ref.shape, F32)
        ref[0:corners, 0 : chosen.shape[1]] = chosen


def jumps(limit_ref, loads_ref, weights_ref, *refs):
    faces, paired, (jump_ref, force_ref) = refs[:4], refs[4:8], refs[8:]
    size = faces[0].shape[0]
    slot = lax.broadcasted_iota(jnp.int32, faces[0].shape, 0)
    parts = []
    for f in range(4):
        at = slice(f * size, (f + 1) * size)
        part = faces[f][...] - paired[f][...] - loads_ref[at].astype(F32)
        parts.append(jnp.where(slot < limit_ref[f : f + 1, :], part, 0.0))
    jump = jnp.concatenate(parts, axis=0)
    jump_ref[...] = jump
    _, groups, group, width = force_ref.shape
    padded = weights_ref.shape[0] // 3
    high, low = halves(jump)
    force = jnp.dot(weights_ref[0 : 2 * padded, :], high, preferred_element_type=F32)
    force = force[:padded] + force[padded:]
    force += jnp.dot(weights_ref[0:padded, :], low, preferred_element_type=F32)
    force = force[: groups * group].reshape(1, groups, group, width)
    force_ref[...] = jnp.broadcast_to(force, force_ref.shape)


def directions(
    blocks, forces_ref, weights_ref, jump_ref, schur_ref, flex_ref, *refs
):
    mine_refs, (search_ref, sums_ref, ordered_ref) = refs[:blocks], refs[blocks:]
    count, groups, group, width = forces_ref.shape
    rows = blocks
    padded, lanes = mine_refs[0].shape
    corners = groups * group
    span = count * corners // blocks
    cols = count // rows
    if lanes > span:
        for b in range(blocks):
            ordered_ref[b, span:, :] = jnp.zeros((lanes - span, width), F32)
    for r in range(rows):
        for c in range(cols):
            start = (c * rows + r) * corners
            for g in range(groups):
                at = start % span + g * group
                ordered_ref[start // span, at : at + group, :] = forces_ref[r * cols + c, g]
    coarse = jnp.zeros((padded, width), F32)
    for k, mine_ref in enumerate(mine_refs):
        coarse += fine_dot(mine_ref[...], ordered_ref[lax.rem(lax.axis_index("row") + rows - k, rows)])
    high, low = halves(coarse)
    correction = lax.dot_general(
        weights_ref[...],
        jnp.concatenate([high, high, low], axis=0),
        (((0,), (0,)), ((), ())),
        preferred_element_type=F32,
    )
    projected = (jump_ref[...] - correction).astype(BF16)
    search = jnp.dot(schur_ref[...], projected, preferred_element_type=F32)
    search_ref[...] = search
    gain = jnp.sum(projected.astype(F32) * search, axis=0, keepdims=True)
    search = search.astype(BF16)
    curved = jnp.dot(flex_ref[...], search, preferred_element_type=F32)
    curvature = jnp.sum(search.astype(F32) * curved, axis=0, keepdims=True)
    sums = jnp.concatenate([gain, curvature], axis=0)
    sums_ref[...] = jnp.broadcast_to(sums[None], sums_ref.shape)


def local(
    slip_load,
    flexibility,
    schur,
    corner_coupling,
    coarse_inverse,
    bounds_table,
    bound_index,
    face_rows,
):
    loads = slip_load[0, 0]
    flex = flexibility[0, 0]
    shell = schur[0, 0]
    coupling = corner_coupling[0, 0][:, None, :]
    row_count, width = loads.shape
    face = ((row_count // 4, width), F32)
    whole = ((row_count, width), F32)
    rows, cols = lax.axis_size("row"), lax.axis_size("col")
    count = rows * cols
    corners = coupling.shape[0]
    group = 4 if corners % 4 == 0 else 1
    shared = ((count, corners // group, group, width), F32)
    padded = -(-corners // 8) * 8
    lanes = -(-coarse_inverse.shape[0] // 128) * 128
    work = 2 * row_count * row_count * width

    def exchanged(blocks):
        return lax.all_to_all(blocks, ALL, 0, 0, tiled=True)

    inputs = (bounds_table, bound_index[0], face_rows[0], loads, coarse_inverse.T, coupling, flex)
    outs = kernel_call(
        functools.partial(begin, bounds_table.shape[0]),
        [HBM] * 7,
        [
            whole,
            ((8, width), jnp.int32),
            ((3 * padded, row_count), BF16),
            (flex.shape, BF16),
        ]
        + [face] * 4
        + [((padded, lanes), F32)] * rows,
        work,
        [
            pltpu.SMEM(bounds_table.shape, F32),
            pltpu.VMEM((1, row_count), jnp.int32),
            pltpu.SMEM((1, 4), jnp.int32),
            pltpu.VMEM(loads.shape, BF16),
            pltpu.VMEM(coarse_inverse.T.shape, F32),
            pltpu.VMEM(coupling.shape, F32),
            pltpu.SemaphoreType.DMA((10,)),
        ],
    )(*(in_hbm(x) for x in inputs))
    bound, limit, weights, flex = outs[:4]
    faces, mine = outs[4:8], outs[8:]
    for iteration in range(ITERS):
        paired = from_sides(*faces)
        if iteration == 0:
            mine = [mine[0]] + [
                passed_round(block, "row", k) for k, block in enumerate(mine[1:], 1)
            ]
            paired[0], *mine = lax.optimization_barrier((paired[0], *mine))
        jump, forces = kernel_call(
            jumps, [VMEM] * 11, [whole, shared], work // 8
        )(limit, loads, weights, *faces, *paired)
        forces = exchanged(forces)
        search, sums = kernel_call(
            functools.partial(directions, rows),
            [VMEM] * (5 + rows),
            [whole, ((count, 2, width), F32)],
            2 * work,
            [pltpu.VMEM((rows, lanes, width), F32)],
        )(forces, weights, jump, shell, flex, *mine)
        sums = exchanged(sums)
        if iteration < ITERS - 1:
            lam, *faces = kernel_call(
                again, [VMEM] * 5, [whole] + [face] * 4, work
            )(sums, loads, search, bound, flex)
        else:
            (out,) = kernel_call(
                end, [VMEM] * 4, [((row_count, width), BF16)], work // 64
            )(sums, lam, search, bound)
    return out[None, None]


def solution(mesh):
    return jax.shard_map(
        local,
        mesh=mesh,
        in_specs=(
            P("row", "col", None, None),
            P("row", "col", None, None),
            P("row", "col", None, None),
            P("row", "col", None, None),
            P("row", "col"),
            P(),
            P("row", "col", None),
            P("row", "col", None),
        ),
        out_specs=P("row", "col", None, None),
        check_vma=False,
    )
```

time: 93.9 us -> 86.7 us (0.923)
  matrix products: 12.6 us -> 0 us
  blocking collectives: 32 us -> 43.7 us
  Pallas kernels: 0 us -> 10.1 us
  starting transfers between devices: 20.1 us -> 11.3 us
  local copies, waits for them, and re-layouts: 7.11 us -> 0.01 us
  waiting for transfers between devices: 19.1 us -> 21.3 us
  other arithmetic: 1.98 us -> 0 us
    dot_general x12 -> x0, matrix products: 12.6 us -> none  [the longest x2 4.86 us: local(): jnp.dot(flex_block, lam.astype(jnp.bfloat16), preferred_element_type=jnp....]
    all_to_all x3 -> x4, blocking collectives: 32 us -> 43.7 us  [exchanged(): return lax.all_to_all(blocks, ALL, 0, 0, tiled=True)]
    ppermute x8 -> x11, waiting for transfers between devices: 10.3 us -> 21.3 us  [passed_round(): return lax.ppermute(x, axis, [(i, (i + by) % count) for i in range(count)])]
    pallas_call x0 -> x7, Pallas kernels: none -> 10.1 us  [the longest x2 5.18 us: local(): kernel_call(functools.partial(directions, rows), [VMEM] * (5 + rows), [wh...]
    all_to_all x2 -> x0, starting transfers between devices: 9.74 us -> none  [the longest x1 6.35 us: local(): mine = lax.all_to_all(coarse_inverse.T, 'row', 0, 1, tiled=True)]
    all_to_all x2 -> x0, waiting for transfers between devices: 8.86 us -> none  [the longest x1 8.85 us: shared(): return lax.all_to_all(copies, ALL, 0, 0, tiled=True)]
    broadcast_in_dim x5 -> x0, local copies, waits for them, and re-layouts: 2.55 us -> none  [the longest x1 1.79 us: local(): return lam.astype(jnp.bfloat16)[None, None]]
    all_to_all x2 -> x0, local copies, waits for them, and re-layouts: 2.12 us -> none  [local(): mine = lax.all_to_all(coarse_inverse.T, 'row', 0, 1, tiled=True)]
  transfers between devices with their start and end apart: 10 -> 11, of which waited for: 6 -> 7; matrix products, arithmetic and copies ran while one was open for 7% -> 0% of each run, Pallas kernels for 0% -> 0%
where the time goes in v2:
time: 86.7 us; the launch traced here: 86.5 us
  blocking collectives  43.7 us (50%)
  waiting for transfers between devices  21.3 us (25%)
  starting transfers between devices  11.3 us (13%)
  Pallas kernels  10.1 us (12%)
    all_to_all x4, blocking collectives, exchanged(): return lax.all_to_all(blocks, ALL, 0, 0, tiled=True)  43.7 us
    ppermute x11, waiting for transfers between devices, passed_round(): return lax.ppermute(x, axis, [(i, (i + by) % count) for i in range(count)])  21.3 us
    ppermute x11, starting transfers between devices, passed_round(): return lax.ppermute(x, axis, [(i, (i + by) % count) for i in range(count)])  11.3 us
    pallas_call x2, Pallas kernels, local(): kernel_call(functools.partial(directions, rows), [VMEM] * (5 + rows), [wh...  5.18 us
    pallas_call x1, Pallas kernels, local(): kernel_call(functools.partial(begin, bounds_table.shape[0]), [HBM] * 7, [...  2.61 us
  transfers between devices with their start and end apart: 11, of which 7 were waited for; matrix products, arithmetic and copies ran while one was open for 0% of the time, Pallas kernels for 0%

profile of v2, /device:TPU:0, one launch (start us, length us, event | category | flops | bytes accessed | tf_op | source)
XLA Modules:
  0.0 86.5 jit_solution(6549513174949051018)
XLA Ops:
  0.0 2.6 %shard_map.82 = (f32[1024,128]{1,0:T(8,128)S(1)}, s32[8,128]{1,0:T(8,128)S(1)}, bf16[48,1024]{1,0:T(8,128)(2,1)S(1)}, bf16[1024,1024]{1,0:T(8,128)(2,1)S(1)}, f3...) custom-call(f32[16]{0:T(128)} %table_hbm.1, ...), custom_call_target="tpu_custom_call" | custom-call | flops 268435456 | bytes 4194304 | tf_op jit(solution)/shard_map/pallas_call | solution.py:239
  2.6 0.5 collective-permute-start
  3.2 2.9 %collective-permute-start.4 = (f32[256,128]{1,0:T(8,128)S(1)}, f32[256,128]{1,0:T(8,128)S(1)}, u32[]{:S(2)}, u32[]{:S(2)}) collective-permute-start(f32[256,128]{1,0:T(8,128)S(1)} %get-tuple-element.37.refs_0_), channel_id=1, source_target_pairs={{0,7},{1,0},{2,1},{3,2},{4,3},{5,4},{6,5},{7,6},{8,15},{9,8},{10,9... | collective-permute-start | bytes 393224 | tf_op jit(solution)/shard_map/ppermute | solution.py:33
  6.1 4.3 %collective-permute-start.6 = (f32[256,128]{1,0:T(8,128)S(1)}, f32[256,128]{1,0:T(8,128)S(1)}, u32[]{:S(2)}, u32[]{:S(2)}) collective-permute-start(f32[256,128]{1,0:T(8,128)S(1)} %get-tuple-element.39.refs_2_), channel_id=1, source_target_pairs={{0,24},{8,0},{16,8},{24,16},{1,25},{9,1},{17,9},{25,17},{2,26},{10... | collective-permute-start | bytes 393224 | tf_op jit(solution)/shard_map/ppermute | solution.py:33
  10.4 6.8 %collective-permute-done.1.refs_1_ = f32[16,128]{1,0:T(8,128)S(1)} collective-permute-done((f32[16,128]{1,0:T(8,128)S(1)}, f32[16,128]{1,0:T(8,128)S(1)}, u32[]{:S(2)}, u32[]{:S(2)}) %collective-permute-start.1) | collective-permute-done | bytes 8224 | tf_op jit(solution)/shard_map/ppermute | solution.py:33
  17.3 4.6 %collective-permute-done.2.refs_2_ = f32[16,128]{1,0:T(8,128)S(1)} collective-permute-done((f32[16,128]{1,0:T(8,128)S(1)}, f32[16,128]{1,0:T(8,128)S(1)}, u32[]{:S(2)}, u32[]{:S(2)}) %collective-permute-start.2) | collective-permute-done | bytes 8224 | tf_op jit(solution)/shard_map/ppermute | solution.py:33
  21.8 0.9 %collective-permute-start.3 = (f32[16,128]{1,0:T(8,128)S(1)}, f32[16,128]{1,0:T(8,128)S(1)}, u32[]{:S(2)}, u32[]{:S(2)}) collective-permute-start(f32[16,128]{1,0:T(8,128)S(1)} %get-tuple-element.44), channel_id=1, source_target_pairs={{0,24},{8,0},{16,8},{24,16},{1,25},{9,1},{17,9},{25,17},{2,26},{10... | collective-permute-start | bytes 24584 | tf_op jit(solution)/shard_map/ppermute | solution.py:33
  22.7 2.8 %collective-permute-done.3.refs_3_ = f32[16,128]{1,0:T(8,128)S(1)} collective-permute-done((f32[16,128]{1,0:T(8,128)S(1)}, f32[16,128]{1,0:T(8,128)S(1)}, u32[]{:S(2)}, u32[]{:S(2)}) %collective-permute-start.3) | collective-permute-done | bytes 8224 | tf_op jit(solution)/shard_map/ppermute | solution.py:33
  25.5 0.3 shard_map.83
  25.8 12.8 %all_to_all.20.forces_ref = f32[32,3,4,128]{3,2,1,0:T(4,128)S(1)} all-to-all(f32[32,3,4,128]{3,2,1,0:T(4,128)S(1)} %get-tuple-element.46), channel_id=1, replica_groups=mesh['row'=4,'col'=8] {'row','col'}, dimensions={0} | all-to-all | bytes 393216 | tf_op jit(solution)/shard_map/all_to_all | solution.py:236
  38.6 2.6 %shard_map.84 = (f32[1024,128]{1,0:T(8,128)S(1)}, f32[32,2,128]{2,1,0:T(2,128)S(1)}) custom-call(f32[32,3,4,128]{3,2,1,0:T(4,128)S(1)} %all_to_all.20.forces_ref, bf16[48,1024]{1,0:T(8,128)(2,1)S(1)} %get-tuple-element.36.weights_ref, f32[1024,128]{1,0:T(8,128)S(1)} %get-tuple-element.47.jump_ref, bf16[1024,1024]{1,0:T(8,128)(2,1)S(1)} %bitcast.8, ...), custom_call_target="tpu_custom_call" | custom-call | flops 536870912 | bytes 4194304 | tf_op jit(solution)/shard_map/pallas_call | solution.py:274
  41.2 9.7 %all_to_all.21.sums_ref = f32[32,2,128]{2,1,0:T(2,128)S(1)} all-to-all(f32[32,2,128]{2,1,0:T(2,128)S(1)} %get-tuple-element.53), channel_id=1, replica_groups=mesh['row'=4,'col'=8] {'row','col'}, dimensions={0} | all-to-all | bytes 65536 | tf_op jit(solution)/shard_map/all_to_all | solution.py:236
  50.9 0.8 shard_map.85
  51.7 0.3 collective-permute-start.8
  52.2 0.6 collective-permute-start.10
  52.8 1.4 %collective-permute-start.9 = (f32[256,128]{1,0:T(8,128)S(1)}, f32[256,128]{1,0:T(8,128)S(1)}, u32[]{:S(2)}, u32[]{:S(2)}) collective-permute-start(f32[256,128]{1,0:T(8,128)S(1)} %get-tuple-element.59.refs_3_), channel_id=1, source_target_pairs={{0,8},{8,16},{16,24},{24,0},{1,9},{9,17},{17,25},{25,1},{2,10},{10... | collective-permute-start | bytes 393224 | tf_op jit(solution)/shard_map/ppermute | solution.py:33
  54.3 0.8 collective-permute-done.8.refs_5_
  55.0 2.8 %collective-permute-done.7.refs_4_ = f32[256,128]{1,0:T(8,128)S(1)} collective-permute-done((f32[256,128]{1,0:T(8,128)S(1)}, f32[256,128]{1,0:T(8,128)S(1)}, u32[]{:S(2)}, u32[]{:S(2)}) %collective-permute-start.7) | collective-permute-done | bytes 131104 | tf_op jit(solution)/shard_map/ppermute | solution.py:33
  57.8 0.4 collective-permute-done.10.refs_7_
  58.2 3.2 %collective-permute-done.9.refs_6_ = f32[256,128]{1,0:T(8,128)S(1)} collective-permute-done((f32[256,128]{1,0:T(8,128)S(1)}, f32[256,128]{1,0:T(8,128)S(1)}, u32[]{:S(2)}, u32[]{:S(2)}) %collective-permute-start.9) | collective-permute-done | bytes 131104 | tf_op jit(solution)/shard_map/ppermute | solution.py:33
  61.8 11.6 %all_to_all.22.forces_ref = f32[32,3,4,128]{3,2,1,0:T(4,128)S(1)} all-to-all(f32[32,3,4,128]{3,2,1,0:T(4,128)S(1)} %get-tuple-element.60), channel_id=1, replica_groups=mesh['row'=4,'col'=8] {'row','col'}, dimensions={0} | all-to-all | bytes 393216 | tf_op jit(solution)/shard_map/all_to_all | solution.py:236
  73.4 2.6 %shard_map.87 = (f32[1024,128]{1,0:T(8,128)S(1)}, f32[32,2,128]{2,1,0:T(2,128)S(1)}) custom-call(f32[32,3,4,128]{3,2,1,0:T(4,128)S(1)} %all_to_all.22.forces_ref, bf16[48,1024]{1,0:T(8,128)(2,1)S(1)} %get-tuple-element.36.weights_ref, f32[1024,128]{1,0:T(8,128)S(1)} %get-tuple-element.61.jump_ref, bf16[1024,1024]{1,0:T(8,128)(2,1)S(1)} %bitcast.9, ...), custom_call_target="tpu_custom_call" | custom-call | flops 536870912 | bytes 4194304 | tf_op jit(solution)/shard_map/pallas_call | solution.py:274
  76.0 9.7 %all_to_all.23.sums_ref = f32[32,2,128]{2,1,0:T(2,128)S(1)} all-to-all(f32[32,2,128]{2,1,0:T(2,128)S(1)} %get-tuple-element.62), channel_id=1, replica_groups=mesh['row'=4,'col'=8] {'row','col'}, dimensions={0} | all-to-all | bytes 65536 | tf_op jit(solution)/shard_map/all_to_all | solution.py:236
  85.6 0.8 shard_map.88
  (13 shorter events, 0.6 us)
Async XLA Ops:
  0.0 25.5 %copy-start.1 = (bf16[1,1,1024,128]{3,2,1,0:T(8,128)(2,1)S(1)}, bf16[1,1,1024,128]{3,2,1,0:T(8,128)(2,1)}, u32[]{:S(2)}) copy-start(bf16[1,1,1024,128]{3,2,1,0:T(8,128)(2,1)} %param.8) | copy-start | bytes 786436
  0.0 38.6 %copy-start = (bf16[1,1,1024,1024]{3,2,1,0:T(8,128)(2,1)S(1)}, bf16[1,1,1024,1024]{3,2,1,0:T(8,128)(2,1)}, u32[]{:S(2)}) copy-start(bf16[1,1,1024,1024]{3,2,1,0:T(8,128)(2,1)} %param.10) | copy-start | bytes 6291460
  2.6 22.9 %collective-permute-start = (f32[256,128]{1,0:T(8,128)S(1)}, f32[256,128]{1,0:T(8,128)S(1)}, u32[]{:S(2)}, u32[]{:S(2)}) collective-permute-start(f32[256,128]{1,0:T(8,128)S(1)} %get-tuple-element.38.refs_1_), channel_id=1, source_target_pairs={{0,1},{1,2},{2,3},{3,4},{4,5},{5,6},{6,7},{7,0},{8,9},{9,10},{10,1... | collective-permute-start | bytes 393224 | tf_op jit(solution)/shard_map/ppermute | solution.py:33
  3.2 22.3 %collective-permute-start.4 = (f32[256,128]{1,0:T(8,128)S(1)}, f32[256,128]{1,0:T(8,128)S(1)}, u32[]{:S(2)}, u32[]{:S(2)}) collective-permute-start(f32[256,128]{1,0:T(8,128)S(1)} %get-tuple-element.37.refs_0_), channel_id=1, source_target_pairs={{0,7},{1,0},{2,1},{3,2},{4,3},{5,4},{6,5},{7,6},{8,15},{9,8},{10,9... | collective-permute-start | bytes 393224 | tf_op jit(solution)/shard_map/ppermute | solution.py:33
  6.1 19.4 %collective-permute-start.6 = (f32[256,128]{1,0:T(8,128)S(1)}, f32[256,128]{1,0:T(8,128)S(1)}, u32[]{:S(2)}, u32[]{:S(2)}) collective-permute-start(f32[256,128]{1,0:T(8,128)S(1)} %get-tuple-element.39.refs_2_), channel_id=1, source_target_pairs={{0,24},{8,0},{16,8},{24,16},{1,25},{9,1},{17,9},{25,17},{2,26},{10... | collective-permute-start | bytes 393224 | tf_op jit(solution)/shard_map/ppermute | solution.py:33
  10.4 15.1 %collective-permute-start.5 = (f32[256,128]{1,0:T(8,128)S(1)}, f32[256,128]{1,0:T(8,128)S(1)}, u32[]{:S(2)}, u32[]{:S(2)}) collective-permute-start(f32[256,128]{1,0:T(8,128)S(1)} %get-tuple-element.40.refs_3_), channel_id=1, source_target_pairs={{0,8},{8,16},{16,24},{24,0},{1,9},{9,17},{17,25},{25,1},{2,10},{10... | collective-permute-start | bytes 393224 | tf_op jit(solution)/shard_map/ppermute | solution.py:33
  10.4 6.9 %collective-permute-start.1 = (f32[16,128]{1,0:T(8,128)S(1)}, f32[16,128]{1,0:T(8,128)S(1)}, u32[]{:S(2)}, u32[]{:S(2)}) collective-permute-start(f32[16,128]{1,0:T(8,128)S(1)} %get-tuple-element.42), channel_id=1, source_target_pairs={{0,8},{8,16},{16,24},{24,0},{1,9},{9,17},{17,25},{25,1},{2,10},{10... | collective-permute-start | bytes 24584 | tf_op jit(solution)/shard_map/ppermute | solution.py:33
  17.3 4.6 %collective-permute-start.2 = (f32[16,128]{1,0:T(8,128)S(1)}, f32[16,128]{1,0:T(8,128)S(1)}, u32[]{:S(2)}, u32[]{:S(2)}) collective-permute-start(f32[16,128]{1,0:T(8,128)S(1)} %get-tuple-element.43), channel_id=1, source_target_pairs={{0,16},{8,24},{16,0},{24,8},{1,17},{9,25},{17,1},{25,9},{2,18},{10... | collective-permute-start | bytes 24584 | tf_op jit(solution)/shard_map/ppermute | solution.py:33
  21.8 3.7 %collective-permute-start.3 = (f32[16,128]{1,0:T(8,128)S(1)}, f32[16,128]{1,0:T(8,128)S(1)}, u32[]{:S(2)}, u32[]{:S(2)}) collective-permute-start(f32[16,128]{1,0:T(8,128)S(1)} %get-tuple-element.44), channel_id=1, source_target_pairs={{0,24},{8,0},{16,8},{24,16},{1,25},{9,1},{17,9},{25,17},{2,26},{10... | collective-permute-start | bytes 24584 | tf_op jit(solution)/shard_map/ppermute | solution.py:33
  51.7 3.3 %collective-permute-start.8 = (f32[256,128]{1,0:T(8,128)S(1)}, f32[256,128]{1,0:T(8,128)S(1)}, u32[]{:S(2)}, u32[]{:S(2)}) collective-permute-start(f32[256,128]{1,0:T(8,128)S(1)} %get-tuple-element.56.refs_0_), channel_id=1, source_target_pairs={{0,7},{1,0},{2,1},{3,2},{4,3},{5,4},{6,5},{7,6},{8,15},{9,8},{10,9... | collective-permute-start | bytes 393224 | tf_op jit(solution)/shard_map/ppermute | solution.py:33
  52.0 5.8 %collective-permute-start.7 = (f32[256,128]{1,0:T(8,128)S(1)}, f32[256,128]{1,0:T(8,128)S(1)}, u32[]{:S(2)}, u32[]{:S(2)}) collective-permute-start(f32[256,128]{1,0:T(8,128)S(1)} %get-tuple-element.57.refs_1_), channel_id=1, source_target_pairs={{0,1},{1,2},{2,3},{3,4},{4,5},{5,6},{6,7},{7,0},{8,9},{9,10},{10,1... | collective-permute-start | bytes 393224 | tf_op jit(solution)/shard_map/ppermute | solution.py:33
  52.2 6.0 %collective-permute-start.10 = (f32[256,128]{1,0:T(8,128)S(1)}, f32[256,128]{1,0:T(8,128)S(1)}, u32[]{:S(2)}, u32[]{:S(2)}) collective-permute-start(f32[256,128]{1,0:T(8,128)S(1)} %get-tuple-element.58.refs_2_), channel_id=1, source_target_pairs={{0,24},{8,0},{16,8},{24,16},{1,25},{9,1},{17,9},{25,17},{2,26},{10... | collective-permute-start | bytes 393224 | tf_op jit(solution)/shard_map/ppermute | solution.py:33
  52.8 8.6 %collective-permute-start.9 = (f32[256,128]{1,0:T(8,128)S(1)}, f32[256,128]{1,0:T(8,128)S(1)}, u32[]{:S(2)}, u32[]{:S(2)}) collective-permute-start(f32[256,128]{1,0:T(8,128)S(1)} %get-tuple-element.59.refs_3_), channel_id=1, source_target_pairs={{0,8},{8,16},{16,24},{24,0},{1,9},{9,17},{17,25},{25,1},{2,10},{10... | collective-permute-start | bytes 393224 | tf_op jit(solution)/shard_map/ppermute | solution.py:33

commit v3 on v2

v3 whole, which is shorter than its diff:
```python
import functools

import jax
import jax.numpy as jnp
from jax import lax
from jax.experimental import pallas as pl
from jax.experimental.pallas import tpu as pltpu
from jax.sharding import PartitionSpec as P


ITERS = 2
ALL = ("row", "col")
F32 = jnp.float32
BF16 = jnp.bfloat16
VMEM = pl.BlockSpec(memory_space=pltpu.VMEM)
HBM = pl.BlockSpec(memory_space=pltpu.HBM)


def kernel_call(body, specs, outs, flops, scratch=()):
    return pl.pallas_call(
        body,
        in_specs=specs,
        out_specs=[VMEM] * len(outs),
        out_shape=[jax.ShapeDtypeStruct(shape, dtype) for shape, dtype in outs],
        compiler_params=pltpu.CompilerParams(vmem_limit_bytes=16 << 20),
        cost_estimate=pl.CostEstimate(flops=flops, bytes_accessed=4 << 20, transcendentals=0),
        scratch_shapes=scratch,
    )


def partner(position, count, k):
    return position ^ k if count & (count - 1) == 0 else (position + k) % count


def passed(x, axis, targets):
    return lax.ppermute(x, axis, list(enumerate(targets)))


def swapped(x, axis, first, ends):
    count = lax.axis_size(axis)
    targets = list(range(count))
    for i in range(first, count - 1, 2):
        targets[i], targets[i + 1] = i + 1, i
    if ends and first == 1 and count % 2 == 0:
        targets[0], targets[-1] = count - 1, 0
    return passed(x, axis, targets)


def across(faces):
    return [
        swapped(faces[0], "row", 0, False),
        swapped(faces[1], "row", 1, False),
        swapped(faces[2], "col", 1, True),
        swapped(faces[3], "col", 0, True),
    ]


def face_order():
    row, col = lax.rem(lax.axis_index("row"), 2), lax.rem(lax.axis_index("col"), 2)
    return [3 - row, 2 + row, col, 1 - col]


def in_hbm(x):
    return pltpu.with_memory_space_constraint(x, pltpu.HBM)


def halves(x):
    high = x.astype(BF16)
    return high, (x - high.astype(F32)).astype(BF16)


def two_part_dot(parts_ref, high, low):
    rows = parts_ref.shape[0] // 2
    out = jnp.dot(parts_ref[...], high, preferred_element_type=F32)
    return out[:rows] + out[rows:] + jnp.dot(parts_ref[0:rows, :], low, preferred_element_type=F32)


def slab(face, size):
    return pl.ds(pl.multiple_of(face * size, size), size)


def put_faces(flex_ref, lam, face_refs):
    size = face_refs[0].shape[0]
    for face, ref in zip(face_order(), face_refs):
        ref[...] = jnp.dot(flex_ref[slab(face, size), :], lam, preferred_element_type=F32)


def begin(levels, table_hbm, index_hbm, live_hbm, loads_hbm, coupling_hbm, flex_hbm, *refs):
    bound_ref, limit_ref, weights_ref, flex_ref = refs[:4]
    face_refs = refs[4:8]
    table_ref, index_ref, live_ref, loads_ref, coupling_ref, sems = refs[8:]
    size = face_refs[0].shape[0]
    pairs = [
        (table_hbm, table_ref),
        (index_hbm, index_ref),
        (loads_hbm, loads_ref),
        (live_hbm, live_ref),
        (coupling_hbm, coupling_ref),
    ]
    slabs = [pl.ds(f * size, size) for f in (2, 3, 0, 1)]
    pairs += [(flex_hbm.at[part], flex_ref.at[part]) for part in slabs]
    copies = [
        pltpu.make_async_copy(source, target, sems.at[i])
        for i, (source, target) in enumerate(pairs)
    ]
    for copy in copies:
        copy.start()
    for copy in copies[:3]:
        copy.wait()
    index = index_ref[...]
    row = jnp.zeros(index.shape, F32)
    for level in range(levels):
        row = jnp.where(index == level, table_ref[level], row)
    bound = jnp.transpose(jnp.broadcast_to(row, (loads_ref.shape[1], row.shape[1])))
    bound_ref[...] = bound
    lam = jnp.clip(loads_ref[...].astype(F32), -bound, bound).astype(BF16)
    for copy in copies[3:5]:
        copy.wait()
    for k, face in enumerate(face_order()):
        limit_ref[k : k + 1, :] = jnp.full((1, limit_ref.shape[1]), live_ref[0, face], jnp.int32)
    corners, _, length = coupling_ref.shape
    padded = weights_ref.shape[0] // 3
    coupling = coupling_ref[...].reshape(corners, length)
    if padded > corners:
        rest = jnp.zeros((padded - corners, length), F32)
        coupling = jnp.concatenate([coupling, rest], axis=0)
    high, low = halves(coupling)
    weights_ref[...] = jnp.concatenate([high, low, high], axis=0)
    for half in (slice(0, 2), slice(2, 4)):
        for copy in copies[5:][half]:
            copy.wait()
        for face, ref in list(zip(face_order(), face_refs))[half]:
            ref[...] = jnp.dot(flex_ref[slab(face, size), :], lam, preferred_element_type=F32)


def stepped(sums_ref, lam, search_ref, bound):
    sums = jnp.sum(sums_ref[...], axis=0)
    return jnp.clip(lam - (sums[0:1] / sums[1:2]) * search_ref[...], -bound, bound)


def again(sums_ref, loads_ref, search_ref, bound_ref, flex_ref, lam_ref, *face_refs):
    bound = bound_ref[...]
    lam = jnp.clip(loads_ref[...].astype(F32), -bound, bound)
    lam = stepped(sums_ref, lam, search_ref, bound)
    lam_ref[...] = lam
    put_faces(flex_ref, lam.astype(BF16), face_refs)


def end(sums_ref, lam_ref, search_ref, bound_ref, out_ref):
    out_ref[...] = stepped(sums_ref, lam_ref[...], search_ref, bound_ref[...]).astype(BF16)


def own_rows(block_refs, mine_ref):
    rows = len(block_refs)
    corners = block_refs[0].shape[0] // rows
    padded, lanes = mine_ref.shape[0] // 2, mine_ref.shape[1] // rows
    here = lax.axis_index("row")
    mine_ref[...] = jnp.zeros(mine_ref.shape, BF16)
    for k, ref in enumerate(block_refs):
        chosen = ref[0:corners, :]
        for r in range(1, rows):
            chosen = jnp.where(here == r, ref[r * corners : (r + 1) * corners, :], chosen)
        at = slice(k * lanes, k * lanes + chosen.shape[1])
        high, low = halves(chosen)
        mine_ref[0:corners, at] = high
        mine_ref[padded : padded + corners, at] = low


def jumps(blocks, limit_ref, loads_ref, weights_ref, *refs):
    faces, paired, block_refs = refs[:4], refs[4:8], refs[8 : 8 + blocks]
    jump_ref, force_ref, *mine_refs = refs[8 + blocks :]
    if blocks:
        own_rows(block_refs, *mine_refs)
    size = faces[0].shape[0]
    slot = lax.broadcasted_iota(jnp.int32, faces[0].shape, 0)
    for k, face in enumerate(face_order()):
        at = slab(face, size)
        part = faces[k][...] - paired[k][...] - loads_ref[at, :].astype(F32)
        jump_ref[at, :] = jnp.where(slot < limit_ref[k : k + 1, :], part, 0.0)
    jump = jump_ref[...]
    _, groups, group, width = force_ref.shape
    padded = weights_ref.shape[0] // 3
    high, low = halves(jump)
    force = two_part_dot(weights_ref.at[0 : 2 * padded], high, low)
    force = force[: groups * group].reshape(1, groups, group, width)
    force_ref[...] = jnp.broadcast_to(force, force_ref.shape)


def directions(
    blocks, forces_ref, mine_ref, weights_ref, jump_ref, schur_ref, flex_ref, *refs
):
    search_ref, sums_ref, ordered_ref = refs
    count, groups, group, width = forces_ref.shape
    rows = blocks
    lanes = mine_ref.shape[1] // blocks
    corners = groups * group
    span = count * corners // blocks
    cols = count // rows
    if lanes > span:
        for b in range(blocks):
            ordered_ref[b, span:, :] = jnp.zeros((lanes - span, width), F32)
    for r in range(rows):
        for c in range(cols):
            start = (c * rows + r) * corners
            for g in range(groups):
                at = start % span + g * group
                ordered_ref[start // span, at : at + group, :] = forces_ref[r * cols + c, g]
    here = lax.axis_index("row")
    sources = [partner(here, rows, rows - k if rows & (rows - 1) else k) for k in range(rows)]
    high, low = halves(jnp.concatenate([ordered_ref[source] for source in sources], axis=0))
    coarse = two_part_dot(mine_ref, high, low)
    high, low = halves(coarse)
    correction = lax.dot_general(
        weights_ref[...],
        jnp.concatenate([high, high, low], axis=0),
        (((0,), (0,)), ((), ())),
        preferred_element_type=F32,
    )
    projected = (jump_ref[...] - correction).astype(BF16)
    search = jnp.dot(schur_ref[...], projected, preferred_element_type=F32)
    search_ref[...] = search
    gain = jnp.sum(projected.astype(F32) * search, axis=0, keepdims=True)
    search = search.astype(BF16)
    curved = jnp.dot(flex_ref[...], search, preferred_element_type=F32)
    curvature = jnp.sum(search.astype(F32) * curved, axis=0, keepdims=True)
    sums = jnp.concatenate([gain, curvature], axis=0)
    sums_ref[...] = jnp.broadcast_to(sums[None], sums_ref.shape)


def local(
    slip_load,
    flexibility,
    schur,
    corner_coupling,
    coarse_inverse,
    bounds_table,
    bound_index,
    face_rows,
):
    loads = slip_load[0, 0]
    flex = flexibility[0, 0]
    shell = schur[0, 0]
    coupling = corner_coupling[0, 0][:, None, :]
    row_count, width = loads.shape
    face = ((row_count // 4, width), F32)
    whole = ((row_count, width), F32)
    rows, cols = lax.axis_size("row"), lax.axis_size("col")
    count = rows * cols
    corners = coupling.shape[0]
    group = 4 if corners % 4 == 0 else 1
    shared = ((count, corners // group, group, width), F32)
    padded = -(-corners // 8) * 8
    lanes = -(-coarse_inverse.shape[0] // 128) * 128
    work = 2 * row_count * row_count * width

    def exchanged(blocks):
        return lax.all_to_all(blocks, ALL, 0, 0, tiled=True)

    block = coarse_inverse.T
    blocks = [block] + [
        passed(block, "row", [partner(r, rows, k) for r in range(rows)])
        for k in range(1, rows)
    ]
    inputs = (
        bounds_table,
        bound_index[0],
        face_rows[0],
        loads,
        coupling,
        flex,
    )
    outs = kernel_call(
        functools.partial(begin, bounds_table.shape[0]),
        [HBM] * 6,
        [
            whole,
            ((8, width), jnp.int32),
            ((3 * padded, row_count), BF16),
            (flex.shape, BF16),
        ]
        + [face] * 4,
        work,
        [
            pltpu.SMEM(bounds_table.shape, F32),
            pltpu.VMEM((1, row_count), jnp.int32),
            pltpu.SMEM((1, 4), jnp.int32),
            pltpu.VMEM(loads.shape, BF16),
            pltpu.VMEM(coupling.shape, F32),
            pltpu.SemaphoreType.DMA((9,)),
        ],
    )(*(in_hbm(x) for x in inputs))
    bound, limit, weights, flex = outs[:4]
    faces = outs[4:]
    for iteration in range(ITERS):
        paired = across(faces)
        if iteration == 0:
            paired[0], *blocks = lax.optimization_barrier((paired[0], *blocks))
            jump, forces, mine = kernel_call(
                functools.partial(jumps, rows),
                [VMEM] * (11 + rows),
                [whole, shared, ((2 * padded, rows * lanes), BF16)],
                work // 8,
            )(limit, loads, weights, *faces, *paired, *blocks)
        else:
            jump, forces = kernel_call(
                functools.partial(jumps, 0), [VMEM] * 11, [whole, shared], work // 8
            )(limit, loads, weights, *faces, *paired)
        forces = exchanged(forces)
        search, sums = kernel_call(
            functools.partial(directions, rows),
            [VMEM] * 6,
            [whole, ((count, 2, width), F32)],
            2 * work,
            [pltpu.VMEM((rows, lanes, width), F32)],
        )(forces, mine, weights, jump, shell, flex)
        sums = exchanged(sums)
        if iteration < ITERS - 1:
            lam, *faces = kernel_call(
                again, [VMEM] * 5, [whole] + [face] * 4, work
            )(sums, loads, search, bound, flex)
        else:
            (out,) = kernel_call(
                end, [VMEM] * 4, [((row_count, width), BF16)], work // 64
            )(sums, lam, search, bound)
    return out[None, None]


def solution(mesh):
    return jax.shard_map(
        local,
        mesh=mesh,
        in_specs=(
            P("row", "col", None, None),
            P("row", "col", None, None),
            P("row", "col", None, None),
            P("row", "col", None, None),
            P("row", "col"),
            P(),
            P("row", "col", None),
            P("row", "col", None),
        ),
        out_specs=P("row", "col", None, None),
        check_vma=False,
    )
```

time: 86.7 us -> 83.9 us (0.968)
  waiting for transfers between devices: 21.3 us -> 12.4 us
  starting transfers between devices: 11.3 us -> 15 us
  blocking collectives: 43.7 us -> 46.2 us
    ppermute x11, waiting for transfers between devices: 21.3 us -> 12.4 us  [passed(): return lax.ppermute(x, axis, list(enumerate(targets)))]
    ppermute x11, starting transfers between devices: 11.3 us -> 15 us  [passed(): return lax.ppermute(x, axis, list(enumerate(targets)))]
    all_to_all x4, blocking collectives: 43.7 us -> 46.2 us  [exchanged(): return lax.all_to_all(blocks, ALL, 0, 0, tiled=True)]
  transfers between devices with their start and end apart: 11 -> 11, of which waited for: 7 -> 5; matrix products, arithmetic and copies ran while one was open for 0% -> 0% of each run, Pallas kernels for 0% -> 0%
where the time goes in v3:
time: 83.9 us; the launch traced here: 83.6 us
  blocking collectives  46.2 us (55%)
  starting transfers between devices  15 us (18%)
  waiting for transfers between devices  12.4 us (15%)
  Pallas kernels  9.94 us (12%)
    all_to_all x4, blocking collectives, exchanged(): return lax.all_to_all(blocks, ALL, 0, 0, tiled=True)  46.2 us
    ppermute x11, starting transfers between devices, passed(): return lax.ppermute(x, axis, list(enumerate(targets)))  15 us
    ppermute x11, waiting for transfers between devices, passed(): return lax.ppermute(x, axis, list(enumerate(targets)))  12.4 us
    pallas_call x2, Pallas kernels, local(): kernel_call(functools.partial(directions, rows), [VMEM] * 6, [whole, ((co...  5.13 us
    pallas_call x1, Pallas kernels, local(): kernel_call(functools.partial(begin, bounds_table.shape[0]), [HBM] * 6, [...  2.39 us
  transfers between devices with their start and end apart: 11, of which 5 were waited for; matrix products, arithmetic and copies ran while one was open for 0% of the time, Pallas kernels for 0%

profile of v3, /device:TPU:0, one launch (start us, length us, event | category | flops | bytes accessed | tf_op | source)
XLA Modules:
  0.0 83.6 jit_solution(13004636352861084522)
XLA Ops:
  0.0 2.4 %shard_map.82 = (f32[1024,128]{1,0:T(8,128)S(1)}, s32[8,128]{1,0:T(8,128)S(1)}, bf16[48,1024]{1,0:T(8,128)(2,1)S(1)}, bf16[1024,1024]{1,0:T(8,128)(2,1)S(1)}, f3...) custom-call(f32[16]{0:T(128)} %table_hbm.1, ...), custom_call_target="tpu_custom_call" | custom-call | flops 268435456 | bytes 4194304 | tf_op jit(solution)/shard_map/pallas_call | solution.py:272
  2.4 3.1 %collective-permute-start = (f32[256,128]{1,0:T(8,128)S(1)}, f32[256,128]{1,0:T(8,128)S(1)}, u32[]{:S(2)}, u32[]{:S(2)}) collective-permute-start(f32[256,128]{1,0:T(8,128)S(1)} %get-tuple-element.34.refs_0_), channel_id=1, source_target_pairs={{0,8},{8,0},{16,24},{24,16},{1,9},{9,1},{17,25},{25,17},{2,10},{10... | collective-permute-start | bytes 393224 | tf_op jit(solution)/shard_map/ppermute | solution.py:36
  5.5 0.7 collective-permute-start.4
  6.2 1.7 %collective-permute-start.5 = (f32[256,128]{1,0:T(8,128)S(1)}, f32[256,128]{1,0:T(8,128)S(1)}, u32[]{:S(2)}, u32[]{:S(2)}) collective-permute-start(f32[256,128]{1,0:T(8,128)S(1)} %get-tuple-element.36.refs_2_), channel_id=1, source_target_pairs={{0,7},{1,2},{2,1},{3,4},{4,3},{5,6},{6,5},{7,0},{8,15},{9,10},{10,... | collective-permute-start | bytes 393224 | tf_op jit(solution)/shard_map/ppermute | solution.py:36
  7.9 2.5 %collective-permute-start.3 = (f32[48,96]{1,0:T(8,128)S(1)}, f32[48,96]{1,0:T(8,128)S(1)}, u32[]{:S(2)}, u32[]{:S(2)}) collective-permute-start(f32[48,96]{1,0:T(8,128)S(1)} %bitcast.14), channel_id=1, source_target_pairs={{0,24},{8,16},{16,8},{24,0},{1,25},{9,17},{17,9},{25,1},{2,26},{10... | collective-permute-start | bytes 55304 | tf_op jit(solution)/shard_map/ppermute | solution.py:36
  10.3 3.2 %collective-permute-done.3.refs_11_ = f32[48,96]{1,0:T(8,128)S(1)} collective-permute-done((f32[48,96]{1,0:T(8,128)S(1)}, f32[48,96]{1,0:T(8,128)S(1)}, u32[]{:S(2)}, u32[]{:S(2)}) %collective-permute-start.3) | collective-permute-done | bytes 18464 | tf_op jit(solution)/shard_map/ppermute | solution.py:36
  13.5 2.5 %collective-permute-start.2 = (f32[48,96]{1,0:T(8,128)S(1)}, f32[48,96]{1,0:T(8,128)S(1)}, u32[]{:S(2)}, u32[]{:S(2)}) collective-permute-start(f32[48,96]{1,0:T(8,128)S(1)} %bitcast.15), channel_id=1, source_target_pairs={{0,16},{8,24},{16,0},{24,8},{1,17},{9,25},{17,1},{25,9},{2,18},{10... | collective-permute-start | bytes 55304 | tf_op jit(solution)/shard_map/ppermute | solution.py:36
  16.0 2.2 %collective-permute-done.2.refs_10_ = f32[48,96]{1,0:T(8,128)S(1)} collective-permute-done((f32[48,96]{1,0:T(8,128)S(1)}, f32[48,96]{1,0:T(8,128)S(1)}, u32[]{:S(2)}, u32[]{:S(2)}) %collective-permute-start.2) | collective-permute-done | bytes 18464 | tf_op jit(solution)/shard_map/ppermute | solution.py:36
  18.2 2.6 %collective-permute-start.1 = (f32[48,96]{1,0:T(8,128)S(1)}, f32[48,96]{1,0:T(8,128)S(1)}, u32[]{:S(2)}, u32[]{:S(2)}) collective-permute-start(f32[48,96]{1,0:T(8,128)S(1)} %bitcast.16), channel_id=1, source_target_pairs={{0,8},{8,0},{16,24},{24,16},{1,9},{9,1},{17,25},{25,17},{2,10},{10... | collective-permute-start | bytes 55304 | tf_op jit(solution)/shard_map/ppermute | solution.py:36
  20.8 1.8 %collective-permute-done.1.refs_9_ = f32[48,96]{1,0:T(8,128)S(1)} collective-permute-done((f32[48,96]{1,0:T(8,128)S(1)}, f32[48,96]{1,0:T(8,128)S(1)}, u32[]{:S(2)}, u32[]{:S(2)}) %collective-permute-start.1) | collective-permute-done | bytes 18464 | tf_op jit(solution)/shard_map/ppermute | solution.py:36
  23.0 12.9 %all_to_all.20.forces_ref = f32[32,3,4,128]{3,2,1,0:T(4,128)S(1)} all-to-all(f32[32,3,4,128]{3,2,1,0:T(4,128)S(1)} %get-tuple-element.43), channel_id=1, replica_groups=mesh['row'=4,'col'=8] {'row','col'}, dimensions={0} | all-to-all | bytes 393216 | tf_op jit(solution)/shard_map/all_to_all | solution.py:257
  36.0 2.6 %shard_map.84 = (f32[1024,128]{1,0:T(8,128)S(1)}, f32[32,2,128]{2,1,0:T(2,128)S(1)}) custom-call(f32[32,3,4,128]{3,2,1,0:T(4,128)S(1)} %all_to_all.20.forces_ref, bf16[32,512]{1,0:T(8,128)(2,1)S(1)} %get-tuple-element.44.mine_ref, bf16[48,1024]{1,0:T(8,128)(2,1)S(1)} %get-tuple-element.33.weights_ref, f32[1024,128]{1,0:T(8,128)S(1)} %get-tuple-element.45.jump_ref, ...), custom_call_target="tpu_custom_call" | custom-call | flops 536870912 | bytes 4194304 | tf_op jit(solution)/shard_map/pallas_call | solution.py:309
  38.6 9.7 %all_to_all.21.sums_ref = f32[32,2,128]{2,1,0:T(2,128)S(1)} all-to-all(f32[32,2,128]{2,1,0:T(2,128)S(1)} %get-tuple-element.47), channel_id=1, replica_groups=mesh['row'=4,'col'=8] {'row','col'}, dimensions={0} | all-to-all | bytes 65536 | tf_op jit(solution)/shard_map/all_to_all | solution.py:257
  48.3 0.8 shard_map.85
  49.1 0.6 collective-permute-start.7
  49.7 0.7 collective-permute-start.8
  50.5 0.6 collective-permute-start.10
  51.1 3.6 %collective-permute-done.7.refs_4_ = f32[256,128]{1,0:T(8,128)S(1)} collective-permute-done((f32[256,128]{1,0:T(8,128)S(1)}, f32[256,128]{1,0:T(8,128)S(1)}, u32[]{:S(2)}, u32[]{:S(2)}) %collective-permute-start.7) | collective-permute-done | bytes 131104 | tf_op jit(solution)/shard_map/ppermute | solution.py:36
  54.6 1.6 %collective-permute-done.9.refs_6_ = f32[256,128]{1,0:T(8,128)S(1)} collective-permute-done((f32[256,128]{1,0:T(8,128)S(1)}, f32[256,128]{1,0:T(8,128)S(1)}, u32[]{:S(2)}, u32[]{:S(2)}) %collective-permute-start.9) | collective-permute-done | bytes 131104 | tf_op jit(solution)/shard_map/ppermute | solution.py:36
  56.2 0.4 shard_map.86
  56.6 13.9 %all_to_all.22.forces_ref = f32[32,3,4,128]{3,2,1,0:T(4,128)S(1)} all-to-all(f32[32,3,4,128]{3,2,1,0:T(4,128)S(1)} %get-tuple-element.54), channel_id=1, replica_groups=mesh['row'=4,'col'=8] {'row','col'}, dimensions={0} | all-to-all | bytes 393216 | tf_op jit(solution)/shard_map/all_to_all | solution.py:257
  70.5 2.6 %shard_map.87 = (f32[1024,128]{1,0:T(8,128)S(1)}, f32[32,2,128]{2,1,0:T(2,128)S(1)}) custom-call(f32[32,3,4,128]{3,2,1,0:T(4,128)S(1)} %all_to_all.22.forces_ref, bf16[32,512]{1,0:T(8,128)(2,1)S(1)} %get-tuple-element.44.mine_ref, bf16[48,1024]{1,0:T(8,128)(2,1)S(1)} %get-tuple-element.33.weights_ref, f32[1024,128]{1,0:T(8,128)S(1)} %get-tuple-element.55.jump_ref, ...), custom_call_target="tpu_custom_call" | custom-call | flops 536870912 | bytes 4194304 | tf_op jit(solution)/shard_map/pallas_call | solution.py:309
  73.1 9.7 %all_to_all.23.sums_ref = f32[32,2,128]{2,1,0:T(2,128)S(1)} all-to-all(f32[32,2,128]{2,1,0:T(2,128)S(1)} %get-tuple-element.56), channel_id=1, replica_groups=mesh['row'=4,'col'=8] {'row','col'}, dimensions={0} | all-to-all | bytes 65536 | tf_op jit(solution)/shard_map/all_to_all | solution.py:257
  82.8 0.8 %shard_map.88 = bf16[1024,128]{1,0:T(8,128)(2,1)} custom-call(f32[32,2,128]{2,1,0:T(2,128)S(1)} %all_to_all.23.sums_ref, f32[1024,128]{1,0:T(8,128)S(1)} %get-tuple-element.57.lam_ref, f32[1024,128]{1,0:T(8,128)S(1)} %get-tuple-element.58.search_ref, f32[1024,128]{1,0:T(8,128)S(1)} %get-tuple-element.49.bound_ref), custom_call_target="tpu_custom_call" | custom-call | flops 4194304 | bytes 4194304 | tf_op jit(solution)/shard_map/pallas_call | solution.py:322
  (15 shorter events, 0.5 us)
Async XLA Ops:
  0.0 22.6 %copy-start.1 = (bf16[1,1,1024,128]{3,2,1,0:T(8,128)(2,1)S(1)}, bf16[1,1,1024,128]{3,2,1,0:T(8,128)(2,1)}, u32[]{:S(2)}) copy-start(bf16[1,1,1024,128]{3,2,1,0:T(8,128)(2,1)} %param.8) | copy-start | bytes 786436
  0.0 7.9 %copy-start.2 = (f32[96,48]{0,1:T(8,128)S(1)}, f32[96,48]{0,1:T(8,128)}, u32[]{:S(2)}) copy-start(f32[96,48]{0,1:T(8,128)} %param.12) | copy-start | bytes 55300
  0.0 36.0 %copy-start = (bf16[1,1,1024,1024]{3,2,1,0:T(8,128)(2,1)S(1)}, bf16[1,1,1024,1024]{3,2,1,0:T(8,128)(2,1)}, u32[]{:S(2)}) copy-start(bf16[1,1,1024,1024]{3,2,1,0:T(8,128)(2,1)} %param.10) | copy-start | bytes 6291460
  2.4 20.2 %collective-permute-start = (f32[256,128]{1,0:T(8,128)S(1)}, f32[256,128]{1,0:T(8,128)S(1)}, u32[]{:S(2)}, u32[]{:S(2)}) collective-permute-start(f32[256,128]{1,0:T(8,128)S(1)} %get-tuple-element.34.refs_0_), channel_id=1, source_target_pairs={{0,8},{8,0},{16,24},{24,16},{1,9},{9,1},{17,25},{25,17},{2,10},{10... | collective-permute-start | bytes 393224 | tf_op jit(solution)/shard_map/ppermute | solution.py:36
  5.5 17.1 %collective-permute-start.4 = (f32[256,128]{1,0:T(8,128)S(1)}, f32[256,128]{1,0:T(8,128)S(1)}, u32[]{:S(2)}, u32[]{:S(2)}) collective-permute-start(f32[256,128]{1,0:T(8,128)S(1)} %get-tuple-element.35.refs_1_), channel_id=1, source_target_pairs={{0,0},{8,16},{16,8},{24,24},{1,1},{9,17},{17,9},{25,25},{2,2},{10,... | collective-permute-start | bytes 393224 | tf_op jit(solution)/shard_map/ppermute | solution.py:36
  6.2 16.4 %collective-permute-start.5 = (f32[256,128]{1,0:T(8,128)S(1)}, f32[256,128]{1,0:T(8,128)S(1)}, u32[]{:S(2)}, u32[]{:S(2)}) collective-permute-start(f32[256,128]{1,0:T(8,128)S(1)} %get-tuple-element.36.refs_2_), channel_id=1, source_target_pairs={{0,7},{1,2},{2,1},{3,4},{4,3},{5,6},{6,5},{7,0},{8,15},{9,10},{10,... | collective-permute-start | bytes 393224 | tf_op jit(solution)/shard_map/ppermute | solution.py:36
  7.9 14.8 %collective-permute-start.6 = (f32[256,128]{1,0:T(8,128)S(1)}, f32[256,128]{1,0:T(8,128)S(1)}, u32[]{:S(2)}, u32[]{:S(2)}) collective-permute-start(f32[256,128]{1,0:T(8,128)S(1)} %get-tuple-element.37.refs_3_), channel_id=1, source_target_pairs={{0,1},{1,0},{2,3},{3,2},{4,5},{5,4},{6,7},{7,6},{8,9},{9,8},{10,11... | collective-permute-start | bytes 393224 | tf_op jit(solution)/shard_map/ppermute | solution.py:36
  7.9 5.6 %collective-permute-start.3 = (f32[48,96]{1,0:T(8,128)S(1)}, f32[48,96]{1,0:T(8,128)S(1)}, u32[]{:S(2)}, u32[]{:S(2)}) collective-permute-start(f32[48,96]{1,0:T(8,128)S(1)} %bitcast.14), channel_id=1, source_target_pairs={{0,24},{8,16},{16,8},{24,0},{1,25},{9,17},{17,9},{25,1},{2,26},{10... | collective-permute-start | bytes 55304 | tf_op jit(solution)/shard_map/ppermute | solution.py:36
  13.5 4.7 %collective-permute-start.2 = (f32[48,96]{1,0:T(8,128)S(1)}, f32[48,96]{1,0:T(8,128)S(1)}, u32[]{:S(2)}, u32[]{:S(2)}) collective-permute-start(f32[48,96]{1,0:T(8,128)S(1)} %bitcast.15), channel_id=1, source_target_pairs={{0,16},{8,24},{16,0},{24,8},{1,17},{9,25},{17,1},{25,9},{2,18},{10... | collective-permute-start | bytes 55304 | tf_op jit(solution)/shard_map/ppermute | solution.py:36
  18.2 4.4 %collective-permute-start.1 = (f32[48,96]{1,0:T(8,128)S(1)}, f32[48,96]{1,0:T(8,128)S(1)}, u32[]{:S(2)}, u32[]{:S(2)}) collective-permute-start(f32[48,96]{1,0:T(8,128)S(1)} %bitcast.16), channel_id=1, source_target_pairs={{0,8},{8,0},{16,24},{24,16},{1,9},{9,1},{17,25},{25,17},{2,10},{10... | collective-permute-start | bytes 55304 | tf_op jit(solution)/shard_map/ppermute | solution.py:36
  49.1 5.6 %collective-permute-start.7 = (f32[256,128]{1,0:T(8,128)S(1)}, f32[256,128]{1,0:T(8,128)S(1)}, u32[]{:S(2)}, u32[]{:S(2)}) collective-permute-start(f32[256,128]{1,0:T(8,128)S(1)} %get-tuple-element.50.refs_0_), channel_id=1, source_target_pairs={{0,8},{8,0},{16,24},{24,16},{1,9},{9,1},{17,25},{25,17},{2,10},{10... | collective-permute-start | bytes 393224 | tf_op jit(solution)/shard_map/ppermute | solution.py:36
  49.7 4.9 %collective-permute-start.8 = (f32[256,128]{1,0:T(8,128)S(1)}, f32[256,128]{1,0:T(8,128)S(1)}, u32[]{:S(2)}, u32[]{:S(2)}) collective-permute-start(f32[256,128]{1,0:T(8,128)S(1)} %get-tuple-element.51.refs_1_), channel_id=1, source_target_pairs={{0,0},{8,16},{16,8},{24,24},{1,1},{9,17},{17,9},{25,25},{2,2},{10,... | collective-permute-start | bytes 393224 | tf_op jit(solution)/shard_map/ppermute | solution.py:36
  50.4 5.9 %collective-permute-start.9 = (f32[256,128]{1,0:T(8,128)S(1)}, f32[256,128]{1,0:T(8,128)S(1)}, u32[]{:S(2)}, u32[]{:S(2)}) collective-permute-start(f32[256,128]{1,0:T(8,128)S(1)} %get-tuple-element.52.refs_2_), channel_id=1, source_target_pairs={{0,7},{1,2},{2,1},{3,4},{4,3},{5,6},{6,5},{7,0},{8,15},{9,10},{10,... | collective-permute-start | bytes 393224 | tf_op jit(solution)/shard_map/ppermute | solution.py:36
  50.5 5.8 %collective-permute-start.10 = (f32[256,128]{1,0:T(8,128)S(1)}, f32[256,128]{1,0:T(8,128)S(1)}, u32[]{:S(2)}, u32[]{:S(2)}) collective-permute-start(f32[256,128]{1,0:T(8,128)S(1)} %get-tuple-element.53.refs_3_), channel_id=1, source_target_pairs={{0,1},{1,0},{2,3},{3,2},{4,5},{5,4},{6,7},{7,6},{8,9},{9,8},{10,11... | collective-permute-start | bytes 393224 | tf_op jit(solution)/shard_map/ppermute | solution.py:36

commit v4 on v3

--- a/solution.py
+++ b/solution.py
@@ -47,12 +47,11 @@
 
 
 def across(faces):
-    return [
-        swapped(faces[0], "row", 0, False),
-        swapped(faces[1], "row", 1, False),
-        swapped(faces[2], "col", 1, True),
-        swapped(faces[3], "col", 0, True),
-    ]
+    ways = (("row", 0, False), ("row", 1, False), ("col", 1, True), ("col", 0, True))
+    out = []
+    for k, way in enumerate(ways):
+        out.append(swapped(faces[k], *way))
+    return out
 
 
 def face_order():
@@ -189,7 +188,7 @@
 def directions(
     blocks, forces_ref, mine_ref, weights_ref, jump_ref, schur_ref, flex_ref, *refs
 ):
-    search_ref, sums_ref, ordered_ref = refs
+    search_ref, sums_ref, ordered_ref = refs[:3]
     count, groups, group, width = forces_ref.shape
     rows = blocks
     lanes = mine_ref.shape[1] // blocks
@@ -216,13 +215,21 @@
         (((0,), (0,)), ((), ())),
         preferred_element_type=F32,
     )
-    projected = (jump_ref[...] - correction).astype(BF16)
-    search = jnp.dot(schur_ref[...], projected, preferred_element_type=F32)
-    search_ref[...] = search
-    gain = jnp.sum(projected.astype(F32) * search, axis=0, keepdims=True)
-    search = search.astype(BF16)
-    curved = jnp.dot(flex_ref[...], search, preferred_element_type=F32)
-    curvature = jnp.sum(search.astype(F32) * curved, axis=0, keepdims=True)
+    projected_ref, along_ref = refs[3:]
+    projected_ref[...] = (jump_ref[...] - correction).astype(BF16)
+    size = jump_ref.shape[0] // 4
+    slabs = [slice(at, at + size) for at in range(0, jump_ref.shape[0], size)]
+    gain = curvature = jnp.zeros((1, width), F32)
+    projected = projected_ref[...]
+    for at in slabs:
+        search = jnp.dot(schur_ref[at, :], projected, preferred_element_type=F32)
+        search_ref[at, :] = search
+        along_ref[at, :] = search.astype(BF16)
+        gain += jnp.sum(projected_ref[at, :].astype(F32) * search, axis=0, keepdims=True)
+    along = along_ref[...]
+    for at in slabs:
+        curved = jnp.dot(flex_ref[at, :], along, preferred_element_type=F32)
+        curvature += jnp.sum(along_ref[at, :].astype(F32) * curved, axis=0, keepdims=True)
     sums = jnp.concatenate([gain, curvature], axis=0)
     sums_ref[...] = jnp.broadcast_to(sums[None], sums_ref.shape)
 
@@ -257,10 +264,10 @@
         return lax.all_to_all(blocks, ALL, 0, 0, tiled=True)
 
     block = coarse_inverse.T
-    blocks = [block] + [
-        passed(block, "row", [partner(r, rows, k) for r in range(rows)])
-        for k in range(1, rows)
-    ]
+    blocks = [block]
+    for k in range(1, rows):
+        to = [partner(r, rows, k) for r in range(rows)]
+        blocks.append(passed(block, "row", to))
     inputs = (
         bounds_table,
         bound_index[0],
@@ -311,7 +318,11 @@
             [VMEM] * 6,
             [whole, ((count, 2, width), F32)],
             2 * work,
-            [pltpu.VMEM((rows, lanes, width), F32)],
+            [
+                pltpu.VMEM((rows, lanes, width), F32),
+                pltpu.VMEM((row_count, width), BF16),
+                pltpu.VMEM((row_count, width), BF16),
+            ],
         )(forces, mine, weights, jump, shell, flex)
         sums = exchanged(sums)
         if iteration < ITERS - 1:

time: 83.9 us -> 82.2 us (0.980)
  Pallas kernels: 9.94 us -> 8.32 us
    pallas_call x2, Pallas kernels: 5.13 us -> 3.51 us  [local(): kernel_call(functools.partial(directions, rows), [VMEM] * 6, [whole, ((co...]
where the time goes in v4:
time: 82.2 us; the launch traced here: 82 us
  blocking collectives  46.2 us (56%)
  starting transfers between devices  15 us (18%)
  waiting for transfers between devices  12.4 us (15%)
  Pallas kernels  8.32 us (10%)
    all_to_all x4, blocking collectives, exchanged(): return lax.all_to_all(blocks, ALL, 0, 0, tiled=True)  46.2 us
    ppermute x11, starting transfers between devices, passed(): return lax.ppermute(x, axis, list(enumerate(targets)))  15 us
    ppermute x11, waiting for transfers between devices, passed(): return lax.ppermute(x, axis, list(enumerate(targets)))  12.4 us
    pallas_call x2, Pallas kernels, local(): kernel_call(functools.partial(directions, rows), [VMEM] * 6, [whole, ((co...  3.51 us
    pallas_call x1, Pallas kernels, local(): kernel_call(functools.partial(begin, bounds_table.shape[0]), [HBM] * 6, [...  2.39 us
  transfers between devices with their start and end apart: 11, of which 5 were waited for; matrix products, arithmetic and copies ran while one was open for 0% of the time, Pallas kernels for 0%

profile of v4, /device:TPU:0, one launch (start us, length us, event | category | flops | bytes accessed | tf_op | source)
XLA Modules:
  0.0 82.0 jit_solution(18058904431198278044)
XLA Ops:
  0.0 2.4 %shard_map.82 = (f32[1024,128]{1,0:T(8,128)S(1)}, s32[8,128]{1,0:T(8,128)S(1)}, bf16[48,1024]{1,0:T(8,128)(2,1)S(1)}, bf16[1024,1024]{1,0:T(8,128)(2,1)S(1)}, f3...) custom-call(f32[16]{0:T(128)} %table_hbm.1, ...), custom_call_target="tpu_custom_call" | custom-call | flops 268435456 | bytes 4194304 | tf_op jit(solution)/shard_map/pallas_call | solution.py:279
  2.4 3.1 %collective-permute-start = (f32[256,128]{1,0:T(8,128)S(1)}, f32[256,128]{1,0:T(8,128)S(1)}, u32[]{:S(2)}, u32[]{:S(2)}) collective-permute-start(f32[256,128]{1,0:T(8,128)S(1)} %get-tuple-element.34.refs_0_), channel_id=1, source_target_pairs={{0,8},{8,0},{16,24},{24,16},{1,9},{9,1},{17,25},{25,17},{2,10},{10... | collective-permute-start | bytes 393224 | tf_op jit(solution)/shard_map/ppermute | solution.py:36
  5.5 0.7 collective-permute-start.4
  6.2 1.7 %collective-permute-start.5 = (f32[256,128]{1,0:T(8,128)S(1)}, f32[256,128]{1,0:T(8,128)S(1)}, u32[]{:S(2)}, u32[]{:S(2)}) collective-permute-start(f32[256,128]{1,0:T(8,128)S(1)} %get-tuple-element.36.refs_2_), channel_id=1, source_target_pairs={{0,7},{1,2},{2,1},{3,4},{4,3},{5,6},{6,5},{7,0},{8,15},{9,10},{10,... | collective-permute-start | bytes 393224 | tf_op jit(solution)/shard_map/ppermute | solution.py:36
  7.9 2.5 %collective-permute-start.3 = (f32[48,96]{1,0:T(8,128)S(1)}, f32[48,96]{1,0:T(8,128)S(1)}, u32[]{:S(2)}, u32[]{:S(2)}) collective-permute-start(f32[48,96]{1,0:T(8,128)S(1)} %bitcast.14), channel_id=1, source_target_pairs={{0,24},{8,16},{16,8},{24,0},{1,25},{9,17},{17,9},{25,1},{2,26},{10... | collective-permute-start | bytes 55304 | tf_op jit(solution)/shard_map/ppermute | solution.py:36
  10.3 3.2 %collective-permute-done.3.refs_11_ = f32[48,96]{1,0:T(8,128)S(1)} collective-permute-done((f32[48,96]{1,0:T(8,128)S(1)}, f32[48,96]{1,0:T(8,128)S(1)}, u32[]{:S(2)}, u32[]{:S(2)}) %collective-permute-start.3) | collective-permute-done | bytes 18464 | tf_op jit(solution)/shard_map/ppermute | solution.py:36
  13.5 2.5 %collective-permute-start.2 = (f32[48,96]{1,0:T(8,128)S(1)}, f32[48,96]{1,0:T(8,128)S(1)}, u32[]{:S(2)}, u32[]{:S(2)}) collective-permute-start(f32[48,96]{1,0:T(8,128)S(1)} %bitcast.15), channel_id=1, source_target_pairs={{0,16},{8,24},{16,0},{24,8},{1,17},{9,25},{17,1},{25,9},{2,18},{10... | collective-permute-start | bytes 55304 | tf_op jit(solution)/shard_map/ppermute | solution.py:36
  16.0 2.2 %collective-permute-done.2.refs_10_ = f32[48,96]{1,0:T(8,128)S(1)} collective-permute-done((f32[48,96]{1,0:T(8,128)S(1)}, f32[48,96]{1,0:T(8,128)S(1)}, u32[]{:S(2)}, u32[]{:S(2)}) %collective-permute-start.2) | collective-permute-done | bytes 18464 | tf_op jit(solution)/shard_map/ppermute | solution.py:36
  18.2 2.6 %collective-permute-start.1 = (f32[48,96]{1,0:T(8,128)S(1)}, f32[48,96]{1,0:T(8,128)S(1)}, u32[]{:S(2)}, u32[]{:S(2)}) collective-permute-start(f32[48,96]{1,0:T(8,128)S(1)} %bitcast.16), channel_id=1, source_target_pairs={{0,8},{8,0},{16,24},{24,16},{1,9},{9,1},{17,25},{25,17},{2,10},{10... | collective-permute-start | bytes 55304 | tf_op jit(solution)/shard_map/ppermute | solution.py:36
  20.8 1.8 %collective-permute-done.1.refs_9_ = f32[48,96]{1,0:T(8,128)S(1)} collective-permute-done((f32[48,96]{1,0:T(8,128)S(1)}, f32[48,96]{1,0:T(8,128)S(1)}, u32[]{:S(2)}, u32[]{:S(2)}) %collective-permute-start.1) | collective-permute-done | bytes 18464 | tf_op jit(solution)/shard_map/ppermute | solution.py:36
  23.0 12.9 %all_to_all.20.forces_ref = f32[32,3,4,128]{3,2,1,0:T(4,128)S(1)} all-to-all(f32[32,3,4,128]{3,2,1,0:T(4,128)S(1)} %get-tuple-element.43), channel_id=1, replica_groups=mesh['row'=4,'col'=8] {'row','col'}, dimensions={0} | all-to-all | bytes 393216 | tf_op jit(solution)/shard_map/all_to_all | solution.py:264
  36.0 1.8 %shard_map.84 = (f32[1024,128]{1,0:T(8,128)S(1)}, f32[32,2,128]{2,1,0:T(2,128)S(1)}) custom-call(f32[32,3,4,128]{3,2,1,0:T(4,128)S(1)} %all_to_all.20.forces_ref, bf16[32,512]{1,0:T(8,128)(2,1)S(1)} %get-tuple-element.44.mine_ref, bf16[48,1024]{1,0:T(8,128)(2,1)S(1)} %get-tuple-element.33.weights_ref, f32[1024,128]{1,0:T(8,128)S(1)} %get-tuple-element.45.jump_ref, ...), custom_call_target="tpu_custom_call" | custom-call | flops 536870912 | bytes 4194304 | tf_op jit(solution)/shard_map/pallas_call | solution.py:316
  37.8 9.7 %all_to_all.21.sums_ref = f32[32,2,128]{2,1,0:T(2,128)S(1)} all-to-all(f32[32,2,128]{2,1,0:T(2,128)S(1)} %get-tuple-element.47), channel_id=1, replica_groups=mesh['row'=4,'col'=8] {'row','col'}, dimensions={0} | all-to-all | bytes 65536 | tf_op jit(solution)/shard_map/all_to_all | solution.py:264
  47.4 0.8 shard_map.85
  48.3 0.6 collective-permute-start.7
  48.9 0.7 collective-permute-start.8
  49.7 0.6 collective-permute-start.10
  50.2 3.6 %collective-permute-done.7.refs_4_ = f32[256,128]{1,0:T(8,128)S(1)} collective-permute-done((f32[256,128]{1,0:T(8,128)S(1)}, f32[256,128]{1,0:T(8,128)S(1)}, u32[]{:S(2)}, u32[]{:S(2)}) %collective-permute-start.7) | collective-permute-done | bytes 131104 | tf_op jit(solution)/shard_map/ppermute | solution.py:36
  53.8 1.6 %collective-permute-done.9.refs_6_ = f32[256,128]{1,0:T(8,128)S(1)} collective-permute-done((f32[256,128]{1,0:T(8,128)S(1)}, f32[256,128]{1,0:T(8,128)S(1)}, u32[]{:S(2)}, u32[]{:S(2)}) %collective-permute-start.9) | collective-permute-done | bytes 131104 | tf_op jit(solution)/shard_map/ppermute | solution.py:36
  55.4 0.4 shard_map.86
  55.8 13.9 %all_to_all.22.forces_ref = f32[32,3,4,128]{3,2,1,0:T(4,128)S(1)} all-to-all(f32[32,3,4,128]{3,2,1,0:T(4,128)S(1)} %get-tuple-element.54), channel_id=1, replica_groups=mesh['row'=4,'col'=8] {'row','col'}, dimensions={0} | all-to-all | bytes 393216 | tf_op jit(solution)/shard_map/all_to_all | solution.py:264
  69.7 1.8 %shard_map.87 = (f32[1024,128]{1,0:T(8,128)S(1)}, f32[32,2,128]{2,1,0:T(2,128)S(1)}) custom-call(f32[32,3,4,128]{3,2,1,0:T(4,128)S(1)} %all_to_all.22.forces_ref, bf16[32,512]{1,0:T(8,128)(2,1)S(1)} %get-tuple-element.44.mine_ref, bf16[48,1024]{1,0:T(8,128)(2,1)S(1)} %get-tuple-element.33.weights_ref, f32[1024,128]{1,0:T(8,128)S(1)} %get-tuple-element.55.jump_ref, ...), custom_call_target="tpu_custom_call" | custom-call | flops 536870912 | bytes 4194304 | tf_op jit(solution)/shard_map/pallas_call | solution.py:316
  71.5 9.7 %all_to_all.23.sums_ref = f32[32,2,128]{2,1,0:T(2,128)S(1)} all-to-all(f32[32,2,128]{2,1,0:T(2,128)S(1)} %get-tuple-element.56), channel_id=1, replica_groups=mesh['row'=4,'col'=8] {'row','col'}, dimensions={0} | all-to-all | bytes 65536 | tf_op jit(solution)/shard_map/all_to_all | solution.py:264
  81.2 0.8 %shard_map.88 = bf16[1024,128]{1,0:T(8,128)(2,1)} custom-call(f32[32,2,128]{2,1,0:T(2,128)S(1)} %all_to_all.23.sums_ref, f32[1024,128]{1,0:T(8,128)S(1)} %get-tuple-element.57.lam_ref, f32[1024,128]{1,0:T(8,128)S(1)} %get-tuple-element.58.search_ref, f32[1024,128]{1,0:T(8,128)S(1)} %get-tuple-element.49.bound_ref), custom_call_target="tpu_custom_call" | custom-call | flops 4194304 | bytes 4194304 | tf_op jit(solution)/shard_map/pallas_call | solution.py:333
  (15 shorter events, 0.5 us)
Async XLA Ops:
  0.0 22.6 %copy-start.1 = (bf16[1,1,1024,128]{3,2,1,0:T(8,128)(2,1)S(1)}, bf16[1,1,1024,128]{3,2,1,0:T(8,128)(2,1)}, u32[]{:S(2)}) copy-start(bf16[1,1,1024,128]{3,2,1,0:T(8,128)(2,1)} %param.8) | copy-start | bytes 786436
  0.0 7.9 %copy-start.2 = (f32[96,48]{0,1:T(8,128)S(1)}, f32[96,48]{0,1:T(8,128)}, u32[]{:S(2)}) copy-start(f32[96,48]{0,1:T(8,128)} %param.12) | copy-start | bytes 55300
  0.0 36.0 %copy-start = (bf16[1,1,1024,1024]{3,2,1,0:T(8,128)(2,1)S(1)}, bf16[1,1,1024,1024]{3,2,1,0:T(8,128)(2,1)}, u32[]{:S(2)}) copy-start(bf16[1,1,1024,1024]{3,2,1,0:T(8,128)(2,1)} %param.10) | copy-start | bytes 6291460
  2.4 20.2 %collective-permute-start = (f32[256,128]{1,0:T(8,128)S(1)}, f32[256,128]{1,0:T(8,128)S(1)}, u32[]{:S(2)}, u32[]{:S(2)}) collective-permute-start(f32[256,128]{1,0:T(8,128)S(1)} %get-tuple-element.34.refs_0_), channel_id=1, source_target_pairs={{0,8},{8,0},{16,24},{24,16},{1,9},{9,1},{17,25},{25,17},{2,10},{10... | collective-permute-start | bytes 393224 | tf_op jit(solution)/shard_map/ppermute | solution.py:36
  5.5 17.1 %collective-permute-start.4 = (f32[256,128]{1,0:T(8,128)S(1)}, f32[256,128]{1,0:T(8,128)S(1)}, u32[]{:S(2)}, u32[]{:S(2)}) collective-permute-start(f32[256,128]{1,0:T(8,128)S(1)} %get-tuple-element.35.refs_1_), channel_id=1, source_target_pairs={{0,0},{8,16},{16,8},{24,24},{1,1},{9,17},{17,9},{25,25},{2,2},{10,... | collective-permute-start | bytes 393224 | tf_op jit(solution)/shard_map/ppermute | solution.py:36
  6.2 16.4 %collective-permute-start.5 = (f32[256,128]{1,0:T(8,128)S(1)}, f32[256,128]{1,0:T(8,128)S(1)}, u32[]{:S(2)}, u32[]{:S(2)}) collective-permute-start(f32[256,128]{1,0:T(8,128)S(1)} %get-tuple-element.36.refs_2_), channel_id=1, source_target_pairs={{0,7},{1,2},{2,1},{3,4},{4,3},{5,6},{6,5},{7,0},{8,15},{9,10},{10,... | collective-permute-start | bytes 393224 | tf_op jit(solution)/shard_map/ppermute | solution.py:36
  7.9 14.8 %collective-permute-start.6 = (f32[256,128]{1,0:T(8,128)S(1)}, f32[256,128]{1,0:T(8,128)S(1)}, u32[]{:S(2)}, u32[]{:S(2)}) collective-permute-start(f32[256,128]{1,0:T(8,128)S(1)} %get-tuple-element.37.refs_3_), channel_id=1, source_target_pairs={{0,1},{1,0},{2,3},{3,2},{4,5},{5,4},{6,7},{7,6},{8,9},{9,8},{10,11... | collective-permute-start | bytes 393224 | tf_op jit(solution)/shard_map/ppermute | solution.py:36
  7.9 5.6 %collective-permute-start.3 = (f32[48,96]{1,0:T(8,128)S(1)}, f32[48,96]{1,0:T(8,128)S(1)}, u32[]{:S(2)}, u32[]{:S(2)}) collective-permute-start(f32[48,96]{1,0:T(8,128)S(1)} %bitcast.14), channel_id=1, source_target_pairs={{0,24},{8,16},{16,8},{24,0},{1,25},{9,17},{17,9},{25,1},{2,26},{10... | collective-permute-start | bytes 55304 | tf_op jit(solution)/shard_map/ppermute | solution.py:36
  13.5 4.7 %collective-permute-start.2 = (f32[48,96]{1,0:T(8,128)S(1)}, f32[48,96]{1,0:T(8,128)S(1)}, u32[]{:S(2)}, u32[]{:S(2)}) collective-permute-start(f32[48,96]{1,0:T(8,128)S(1)} %bitcast.15), channel_id=1, source_target_pairs={{0,16},{8,24},{16,0},{24,8},{1,17},{9,25},{17,1},{25,9},{2,18},{10... | collective-permute-start | bytes 55304 | tf_op jit(solution)/shard_map/ppermute | solution.py:36
  18.2 4.4 %collective-permute-start.1 = (f32[48,96]{1,0:T(8,128)S(1)}, f32[48,96]{1,0:T(8,128)S(1)}, u32[]{:S(2)}, u32[]{:S(2)}) collective-permute-start(f32[48,96]{1,0:T(8,128)S(1)} %bitcast.16), channel_id=1, source_target_pairs={{0,8},{8,0},{16,24},{24,16},{1,9},{9,1},{17,25},{25,17},{2,10},{10... | collective-permute-start | bytes 55304 | tf_op jit(solution)/shard_map/ppermute | solution.py:36
  48.3 5.6 %collective-permute-start.7 = (f32[256,128]{1,0:T(8,128)S(1)}, f32[256,128]{1,0:T(8,128)S(1)}, u32[]{:S(2)}, u32[]{:S(2)}) collective-permute-start(f32[256,128]{1,0:T(8,128)S(1)} %get-tuple-element.50.refs_0_), channel_id=1, source_target_pairs={{0,8},{8,0},{16,24},{24,16},{1,9},{9,1},{17,25},{25,17},{2,10},{10... | collective-permute-start | bytes 393224 | tf_op jit(solution)/shard_map/ppermute | solution.py:36
  48.9 4.9 %collective-permute-start.8 = (f32[256,128]{1,0:T(8,128)S(1)}, f32[256,128]{1,0:T(8,128)S(1)}, u32[]{:S(2)}, u32[]{:S(2)}) collective-permute-start(f32[256,128]{1,0:T(8,128)S(1)} %get-tuple-element.51.refs_1_), channel_id=1, source_target_pairs={{0,0},{8,16},{16,8},{24,24},{1,1},{9,17},{17,9},{25,25},{2,2},{10,... | collective-permute-start | bytes 393224 | tf_op jit(solution)/shard_map/ppermute | solution.py:36
  49.6 5.9 %collective-permute-start.9 = (f32[256,128]{1,0:T(8,128)S(1)}, f32[256,128]{1,0:T(8,128)S(1)}, u32[]{:S(2)}, u32[]{:S(2)}) collective-permute-start(f32[256,128]{1,0:T(8,128)S(1)} %get-tuple-element.52.refs_2_), channel_id=1, source_target_pairs={{0,7},{1,2},{2,1},{3,4},{4,3},{5,6},{6,5},{7,0},{8,15},{9,10},{10,... | collective-permute-start | bytes 393224 | tf_op jit(solution)/shard_map/ppermute | solution.py:36
  49.7 5.8 %collective-permute-start.10 = (f32[256,128]{1,0:T(8,128)S(1)}, f32[256,128]{1,0:T(8,128)S(1)}, u32[]{:S(2)}, u32[]{:S(2)}) collective-permute-start(f32[256,128]{1,0:T(8,128)S(1)} %get-tuple-element.53.refs_3_), channel_id=1, source_target_pairs={{0,1},{1,0},{2,3},{3,2},{4,5},{5,4},{6,7},{7,6},{8,9},{9,8},{10,11... | collective-permute-start | bytes 393224 | tf_op jit(solution)/shard_map/ppermute | solution.py:36

commit v5 on v4

--- a/solution.py
+++ b/solution.py
@@ -36,14 +36,23 @@
     return lax.ppermute(x, axis, list(enumerate(targets)))
 
 
-def swapped(x, axis, first, ends):
-    count = lax.axis_size(axis)
-    targets = list(range(count))
-    for i in range(first, count - 1, 2):
-        targets[i], targets[i + 1] = i + 1, i
-    if ends and first == 1 and count % 2 == 0:
-        targets[0], targets[-1] = count - 1, 0
-    return passed(x, axis, targets)
+def swapped(x, axis, first, wrap):
+    rows, cols = lax.axis_size("row"), lax.axis_size("col")
+    targets = []
+    for r in range(rows):
+        for c in range(cols):
+            count, i = (rows, r) if axis == "row" else (cols, c)
+            j = i ^ 1 if first == 0 else ((i + 1) ^ 1) - 1
+            if wrap and first == 1 and count % 2 == 0:
+                j %= count
+            if 0 <= j < count:
+                to = (j, c) if axis == "row" else (r, j)
+            elif axis == "row":
+                to = (r, c ^ 1) if c ^ 1 < cols else (r, c)
+            else:
+                to = (r ^ 1, c) if r ^ 1 < rows else (r, c)
+            targets.append(to[0] * cols + to[1])
+    return passed(x, ALL, targets)
 
 
 def across(faces):
@@ -78,10 +87,19 @@
     return pl.ds(pl.multiple_of(face * size, size), size)
 
 
+def put_pair(rows, lam, flipped, refs):
+    both = jnp.dot(rows, lam, preferred_element_type=F32)
+    size = both.shape[0] // 2
+    first, second = both[:size], both[size:]
+    refs[0][...] = jnp.where(flipped, second, first)
+    refs[1][...] = jnp.where(flipped, first, second)
+
+
 def put_faces(flex_ref, lam, face_refs):
-    size = face_refs[0].shape[0]
-    for face, ref in zip(face_order(), face_refs):
-        ref[...] = jnp.dot(flex_ref[slab(face, size), :], lam, preferred_element_type=F32)
+    size = 2 * face_refs[0].shape[0]
+    order = face_order()
+    put_pair(flex_ref[size:, :], lam, order[0] == 3, face_refs[:2])
+    put_pair(flex_ref[:size, :], lam, order[2] == 1, face_refs[2:])
 
 
 def begin(levels, table_hbm, index_hbm, live_hbm, loads_hbm, coupling_hbm, flex_hbm, *refs):
@@ -217,7 +235,7 @@
     )
     projected_ref, along_ref = refs[3:]
     projected_ref[...] = (jump_ref[...] - correction).astype(BF16)
-    size = jump_ref.shape[0] // 4
+    size = jump_ref.shape[0] // 2
     slabs = [slice(at, at + size) for at in range(0, jump_ref.shape[0], size)]
     gain = curvature = jnp.zeros((1, width), F32)
     projected = projected_ref[...]

time: 82.2 us -> 78.4 us (0.954)
  starting transfers between devices: 15 us -> 9.89 us
  waiting for transfers between devices: 12.4 us -> 17.2 us
  blocking collectives: 46.2 us -> 42.8 us
    ppermute x11, starting transfers between devices: 15 us -> 9.89 us  [passed(): return lax.ppermute(x, axis, list(enumerate(targets)))]
    ppermute x11, waiting for transfers between devices: 12.4 us -> 17.2 us  [passed(): return lax.ppermute(x, axis, list(enumerate(targets)))]
    all_to_all x4, blocking collectives: 46.2 us -> 42.8 us  [exchanged(): return lax.all_to_all(blocks, ALL, 0, 0, tiled=True)]
where the time goes in v5:
time: 78.4 us; the launch traced here: 78.2 us
  blocking collectives  42.8 us (55%)
  waiting for transfers between devices  17.2 us (22%)
  starting transfers between devices  9.89 us (13%)
  Pallas kernels  8.19 us (10%)
    all_to_all x4, blocking collectives, exchanged(): return lax.all_to_all(blocks, ALL, 0, 0, tiled=True)  42.8 us
    ppermute x11, waiting for transfers between devices, passed(): return lax.ppermute(x, axis, list(enumerate(targets)))  17.2 us
    ppermute x11, starting transfers between devices, passed(): return lax.ppermute(x, axis, list(enumerate(targets)))  9.89 us
    pallas_call x2, Pallas kernels, local(): kernel_call(functools.partial(directions, rows), [VMEM] * 6, [whole, ((co...  3.43 us
    pallas_call x1, Pallas kernels, local(): kernel_call(functools.partial(begin, bounds_table.shape[0]), [HBM] * 6, [...  2.39 us
  transfers between devices with their start and end apart: 11, of which 5 were waited for; matrix products, arithmetic and copies ran while one was open for 0% of the time, Pallas kernels for 0%

profile of v5, /device:TPU:0, one launch (start us, length us, event | category | flops | bytes accessed | tf_op | source)
XLA Modules:
  0.0 78.2 jit_solution(17869115473175710170)
XLA Ops:
  0.0 2.4 %shard_map.82 = (f32[1024,128]{1,0:T(8,128)S(1)}, s32[8,128]{1,0:T(8,128)S(1)}, bf16[48,1024]{1,0:T(8,128)(2,1)S(1)}, bf16[1024,1024]{1,0:T(8,128)(2,1)S(1)}, f3...) custom-call(f32[16]{0:T(128)} %table_hbm.1, ...), custom_call_target="tpu_custom_call" | custom-call | flops 268435456 | bytes 4194304 | tf_op jit(solution)/shard_map/pallas_call | solution.py:297
  2.4 3.1 %collective-permute-start = (f32[256,128]{1,0:T(8,128)S(1)}, f32[256,128]{1,0:T(8,128)S(1)}, u32[]{:S(2)}, u32[]{:S(2)}) collective-permute-start(f32[256,128]{1,0:T(8,128)S(1)} %get-tuple-element.34.refs_0_), channel_id=1, source_target_pairs={{0,8},{1,9},{2,10},{3,11},{4,12},{5,13},{6,14},{7,15},{8,0},{9,1},... | collective-permute-start | bytes 393224 | tf_op jit(solution)/shard_map/ppermute | solution.py:36
  5.5 2.6 %collective-permute-start.5 = (f32[256,128]{1,0:T(8,128)S(1)}, f32[256,128]{1,0:T(8,128)S(1)}, u32[]{:S(2)}, u32[]{:S(2)}) collective-permute-start(f32[256,128]{1,0:T(8,128)S(1)} %get-tuple-element.36.refs_2_), channel_id=1, source_target_pairs={{0,7},{1,2},{2,1},{3,4},{4,3},{5,6},{6,5},{7,0},{8,15},{9,10},{10,... | collective-permute-start | bytes 393224 | tf_op jit(solution)/shard_map/ppermute | solution.py:36
  8.1 2.5 %collective-permute-start.3 = (f32[48,96]{1,0:T(8,128)S(1)}, f32[48,96]{1,0:T(8,128)S(1)}, u32[]{:S(2)}, u32[]{:S(2)}) collective-permute-start(f32[48,96]{1,0:T(8,128)S(1)} %bitcast.14), channel_id=1, source_target_pairs={{0,24},{8,16},{16,8},{24,0},{1,25},{9,17},{17,9},{25,1},{2,26},{10... | collective-permute-start | bytes 55304 | tf_op jit(solution)/shard_map/ppermute | solution.py:36
  10.6 3.2 %collective-permute-done.3.refs_11_ = f32[48,96]{1,0:T(8,128)S(1)} collective-permute-done((f32[48,96]{1,0:T(8,128)S(1)}, f32[48,96]{1,0:T(8,128)S(1)}, u32[]{:S(2)}, u32[]{:S(2)}) %collective-permute-start.3) | collective-permute-done | bytes 18464 | tf_op jit(solution)/shard_map/ppermute | solution.py:36
  13.8 4.7 %collective-permute-done.2.refs_10_ = f32[48,96]{1,0:T(8,128)S(1)} collective-permute-done((f32[48,96]{1,0:T(8,128)S(1)}, f32[48,96]{1,0:T(8,128)S(1)}, u32[]{:S(2)}, u32[]{:S(2)}) %collective-permute-start.2) | collective-permute-done | bytes 18464 | tf_op jit(solution)/shard_map/ppermute | solution.py:36
  18.6 0.3 collective-permute-start.1
  18.9 3.5 %collective-permute-done.1.refs_9_ = f32[48,96]{1,0:T(8,128)S(1)} collective-permute-done((f32[48,96]{1,0:T(8,128)S(1)}, f32[48,96]{1,0:T(8,128)S(1)}, u32[]{:S(2)}, u32[]{:S(2)}) %collective-permute-start.1) | collective-permute-done | bytes 18464 | tf_op jit(solution)/shard_map/ppermute | solution.py:36
  22.4 0.0 collective-permute-done.6.refs_7_
  22.4 0.4 shard_map.83
  22.8 11.5 %all_to_all.20.forces_ref = f32[32,3,4,128]{3,2,1,0:T(4,128)S(1)} all-to-all(f32[32,3,4,128]{3,2,1,0:T(4,128)S(1)} %get-tuple-element.43), channel_id=1, replica_groups=mesh['row'=4,'col'=8] {'row','col'}, dimensions={0} | all-to-all | bytes 393216 | tf_op jit(solution)/shard_map/all_to_all | solution.py:282
  34.3 1.7 %shard_map.84 = (f32[1024,128]{1,0:T(8,128)S(1)}, f32[32,2,128]{2,1,0:T(2,128)S(1)}) custom-call(f32[32,3,4,128]{3,2,1,0:T(4,128)S(1)} %all_to_all.20.forces_ref, bf16[32,512]{1,0:T(8,128)(2,1)S(1)} %get-tuple-element.44.mine_ref, bf16[48,1024]{1,0:T(8,128)(2,1)S(1)} %get-tuple-element.33.weights_ref, f32[1024,128]{1,0:T(8,128)S(1)} %get-tuple-element.45.jump_ref, ...), custom_call_target="tpu_custom_call" | custom-call | flops 536870912 | bytes 4194304 | tf_op jit(solution)/shard_map/pallas_call | solution.py:334
  36.0 9.7 %all_to_all.21.sums_ref = f32[32,2,128]{2,1,0:T(2,128)S(1)} all-to-all(f32[32,2,128]{2,1,0:T(2,128)S(1)} %get-tuple-element.47), channel_id=1, replica_groups=mesh['row'=4,'col'=8] {'row','col'}, dimensions={0} | all-to-all | bytes 65536 | tf_op jit(solution)/shard_map/all_to_all | solution.py:282
  45.7 0.8 shard_map.85
  46.5 0.7 collective-permute-start.7
  47.1 0.8 collective-permute-start.9
  47.9 4.2 %collective-permute-done.7.refs_4_ = f32[256,128]{1,0:T(8,128)S(1)} collective-permute-done((f32[256,128]{1,0:T(8,128)S(1)}, f32[256,128]{1,0:T(8,128)S(1)}, u32[]{:S(2)}, u32[]{:S(2)}) %collective-permute-start.7) | collective-permute-done | bytes 131104 | tf_op jit(solution)/shard_map/ppermute | solution.py:36
  52.0 0.0 collective-permute-done.8.refs_5_
  52.1 1.6 %collective-permute-done.9.refs_6_ = f32[256,128]{1,0:T(8,128)S(1)} collective-permute-done((f32[256,128]{1,0:T(8,128)S(1)}, f32[256,128]{1,0:T(8,128)S(1)}, u32[]{:S(2)}, u32[]{:S(2)}) %collective-permute-start.9) | collective-permute-done | bytes 131104 | tf_op jit(solution)/shard_map/ppermute | solution.py:36
  53.6 0.4 shard_map.86
  54.0 12.0 %all_to_all.22.forces_ref = f32[32,3,4,128]{3,2,1,0:T(4,128)S(1)} all-to-all(f32[32,3,4,128]{3,2,1,0:T(4,128)S(1)} %get-tuple-element.54), channel_id=1, replica_groups=mesh['row'=4,'col'=8] {'row','col'}, dimensions={0} | all-to-all | bytes 393216 | tf_op jit(solution)/shard_map/all_to_all | solution.py:282
  66.0 1.7 %shard_map.87 = (f32[1024,128]{1,0:T(8,128)S(1)}, f32[32,2,128]{2,1,0:T(2,128)S(1)}) custom-call(f32[32,3,4,128]{3,2,1,0:T(4,128)S(1)} %all_to_all.22.forces_ref, bf16[32,512]{1,0:T(8,128)(2,1)S(1)} %get-tuple-element.44.mine_ref, bf16[48,1024]{1,0:T(8,128)(2,1)S(1)} %get-tuple-element.33.weights_ref, f32[1024,128]{1,0:T(8,128)S(1)} %get-tuple-element.55.jump_ref, ...), custom_call_target="tpu_custom_call" | custom-call | flops 536870912 | bytes 4194304 | tf_op jit(solution)/shard_map/pallas_call | solution.py:334
  67.7 9.7 %all_to_all.23.sums_ref = f32[32,2,128]{2,1,0:T(2,128)S(1)} all-to-all(f32[32,2,128]{2,1,0:T(2,128)S(1)} %get-tuple-element.56), channel_id=1, replica_groups=mesh['row'=4,'col'=8] {'row','col'}, dimensions={0} | all-to-all | bytes 65536 | tf_op jit(solution)/shard_map/all_to_all | solution.py:282
  77.4 0.8 %shard_map.88 = bf16[1024,128]{1,0:T(8,128)(2,1)} custom-call(f32[32,2,128]{2,1,0:T(2,128)S(1)} %all_to_all.23.sums_ref, f32[1024,128]{1,0:T(8,128)S(1)} %get-tuple-element.57.lam_ref, f32[1024,128]{1,0:T(8,128)S(1)} %get-tuple-element.58.search_ref, f32[1024,128]{1,0:T(8,128)S(1)} %get-tuple-element.49.bound_ref), custom_call_target="tpu_custom_call" | custom-call | flops 4194304 | bytes 4194304 | tf_op jit(solution)/shard_map/pallas_call | solution.py:351
  (15 shorter events, 0.0 us)
Async XLA Ops:
  0.0 22.4 %copy-start.1 = (bf16[1,1,1024,128]{3,2,1,0:T(8,128)(2,1)S(1)}, bf16[1,1,1024,128]{3,2,1,0:T(8,128)(2,1)}, u32[]{:S(2)}) copy-start(bf16[1,1,1024,128]{3,2,1,0:T(8,128)(2,1)} %param.8) | copy-start | bytes 786436
  0.0 8.1 %copy-start.2 = (f32[96,48]{0,1:T(8,128)S(1)}, f32[96,48]{0,1:T(8,128)}, u32[]{:S(2)}) copy-start(f32[96,48]{0,1:T(8,128)} %param.12) | copy-start | bytes 55300
  0.0 34.3 %copy-start = (bf16[1,1,1024,1024]{3,2,1,0:T(8,128)(2,1)S(1)}, bf16[1,1,1024,1024]{3,2,1,0:T(8,128)(2,1)}, u32[]{:S(2)}) copy-start(bf16[1,1,1024,1024]{3,2,1,0:T(8,128)(2,1)} %param.10) | copy-start | bytes 6291460
  2.4 20.0 %collective-permute-start = (f32[256,128]{1,0:T(8,128)S(1)}, f32[256,128]{1,0:T(8,128)S(1)}, u32[]{:S(2)}, u32[]{:S(2)}) collective-permute-start(f32[256,128]{1,0:T(8,128)S(1)} %get-tuple-element.34.refs_0_), channel_id=1, source_target_pairs={{0,8},{1,9},{2,10},{3,11},{4,12},{5,13},{6,14},{7,15},{8,0},{9,1},... | collective-permute-start | bytes 393224 | tf_op jit(solution)/shard_map/ppermute | solution.py:36
  5.5 16.9 %collective-permute-start.4 = (f32[256,128]{1,0:T(8,128)S(1)}, f32[256,128]{1,0:T(8,128)S(1)}, u32[]{:S(2)}, u32[]{:S(2)}) collective-permute-start(f32[256,128]{1,0:T(8,128)S(1)} %get-tuple-element.35.refs_1_), channel_id=1, source_target_pairs={{0,1},{1,0},{2,3},{3,2},{4,5},{5,4},{6,7},{7,6},{8,16},{9,17},{10,... | collective-permute-start | bytes 393224 | tf_op jit(solution)/shard_map/ppermute | solution.py:36
  5.5 16.9 %collective-permute-start.5 = (f32[256,128]{1,0:T(8,128)S(1)}, f32[256,128]{1,0:T(8,128)S(1)}, u32[]{:S(2)}, u32[]{:S(2)}) collective-permute-start(f32[256,128]{1,0:T(8,128)S(1)} %get-tuple-element.36.refs_2_), channel_id=1, source_target_pairs={{0,7},{1,2},{2,1},{3,4},{4,3},{5,6},{6,5},{7,0},{8,15},{9,10},{10,... | collective-permute-start | bytes 393224 | tf_op jit(solution)/shard_map/ppermute | solution.py:36
  8.1 14.3 %collective-permute-start.6 = (f32[256,128]{1,0:T(8,128)S(1)}, f32[256,128]{1,0:T(8,128)S(1)}, u32[]{:S(2)}, u32[]{:S(2)}) collective-permute-start(f32[256,128]{1,0:T(8,128)S(1)} %get-tuple-element.37.refs_3_), channel_id=1, source_target_pairs={{0,1},{1,0},{2,3},{3,2},{4,5},{5,4},{6,7},{7,6},{8,9},{9,8},{10,11... | collective-permute-start | bytes 393224 | tf_op jit(solution)/shard_map/ppermute | solution.py:36
  8.1 5.7 %collective-permute-start.3 = (f32[48,96]{1,0:T(8,128)S(1)}, f32[48,96]{1,0:T(8,128)S(1)}, u32[]{:S(2)}, u32[]{:S(2)}) collective-permute-start(f32[48,96]{1,0:T(8,128)S(1)} %bitcast.14), channel_id=1, source_target_pairs={{0,24},{8,16},{16,8},{24,0},{1,25},{9,17},{17,9},{25,1},{2,26},{10... | collective-permute-start | bytes 55304 | tf_op jit(solution)/shard_map/ppermute | solution.py:36
  13.8 4.7 %collective-permute-start.2 = (f32[48,96]{1,0:T(8,128)S(1)}, f32[48,96]{1,0:T(8,128)S(1)}, u32[]{:S(2)}, u32[]{:S(2)}) collective-permute-start(f32[48,96]{1,0:T(8,128)S(1)} %bitcast.15), channel_id=1, source_target_pairs={{0,16},{8,24},{16,0},{24,8},{1,17},{9,25},{17,1},{25,9},{2,18},{10... | collective-permute-start | bytes 55304 | tf_op jit(solution)/shard_map/ppermute | solution.py:36
  18.6 3.8 %collective-permute-start.1 = (f32[48,96]{1,0:T(8,128)S(1)}, f32[48,96]{1,0:T(8,128)S(1)}, u32[]{:S(2)}, u32[]{:S(2)}) collective-permute-start(f32[48,96]{1,0:T(8,128)S(1)} %bitcast.16), channel_id=1, source_target_pairs={{0,8},{8,0},{16,24},{24,16},{1,9},{9,1},{17,25},{25,17},{2,10},{10... | collective-permute-start | bytes 55304 | tf_op jit(solution)/shard_map/ppermute | solution.py:36
  46.5 5.6 %collective-permute-start.7 = (f32[256,128]{1,0:T(8,128)S(1)}, f32[256,128]{1,0:T(8,128)S(1)}, u32[]{:S(2)}, u32[]{:S(2)}) collective-permute-start(f32[256,128]{1,0:T(8,128)S(1)} %get-tuple-element.50.refs_0_), channel_id=1, source_target_pairs={{0,8},{1,9},{2,10},{3,11},{4,12},{5,13},{6,14},{7,15},{8,0},{9,1},... | collective-permute-start | bytes 393224 | tf_op jit(solution)/shard_map/ppermute | solution.py:36
  47.1 4.9 %collective-permute-start.8 = (f32[256,128]{1,0:T(8,128)S(1)}, f32[256,128]{1,0:T(8,128)S(1)}, u32[]{:S(2)}, u32[]{:S(2)}) collective-permute-start(f32[256,128]{1,0:T(8,128)S(1)} %get-tuple-element.51.refs_1_), channel_id=1, source_target_pairs={{0,1},{1,0},{2,3},{3,2},{4,5},{5,4},{6,7},{7,6},{8,16},{9,17},{10,... | collective-permute-start | bytes 393224 | tf_op jit(solution)/shard_map/ppermute | solution.py:36
  47.1 6.5 %collective-permute-start.9 = (f32[256,128]{1,0:T(8,128)S(1)}, f32[256,128]{1,0:T(8,128)S(1)}, u32[]{:S(2)}, u32[]{:S(2)}) collective-permute-start(f32[256,128]{1,0:T(8,128)S(1)} %get-tuple-element.52.refs_2_), channel_id=1, source_target_pairs={{0,7},{1,2},{2,1},{3,4},{4,3},{5,6},{6,5},{7,0},{8,15},{9,10},{10,... | collective-permute-start | bytes 393224 | tf_op jit(solution)/shard_map/ppermute | solution.py:36
  47.9 5.7 %collective-permute-start.10 = (f32[256,128]{1,0:T(8,128)S(1)}, f32[256,128]{1,0:T(8,128)S(1)}, u32[]{:S(2)}, u32[]{:S(2)}) collective-permute-start(f32[256,128]{1,0:T(8,128)S(1)} %get-tuple-element.53.refs_3_), channel_id=1, source_target_pairs={{0,1},{1,0},{2,3},{3,2},{4,5},{5,4},{6,7},{7,6},{8,9},{9,8},{10,11... | collective-permute-start | bytes 393224 | tf_op jit(solution)/shard_map/ppermute | solution.py:36

commit v6 on v5

--- a/solution.py
+++ b/solution.py
@@ -87,19 +87,10 @@
     return pl.ds(pl.multiple_of(face * size, size), size)
 
 
-def put_pair(rows, lam, flipped, refs):
-    both = jnp.dot(rows, lam, preferred_element_type=F32)
-    size = both.shape[0] // 2
-    first, second = both[:size], both[size:]
-    refs[0][...] = jnp.where(flipped, second, first)
-    refs[1][...] = jnp.where(flipped, first, second)
-
-
 def put_faces(flex_ref, lam, face_refs):
-    size = 2 * face_refs[0].shape[0]
-    order = face_order()
-    put_pair(flex_ref[size:, :], lam, order[0] == 3, face_refs[:2])
-    put_pair(flex_ref[:size, :], lam, order[2] == 1, face_refs[2:])
+    size = face_refs[0].shape[0]
+    for face, ref in zip(face_order(), face_refs):
+        ref[...] = jnp.dot(flex_ref[slab(face, size), :], lam, preferred_element_type=F32)
 
 
 def begin(levels, table_hbm, index_hbm, live_hbm, loads_hbm, coupling_hbm, flex_hbm, *refs):
@@ -114,7 +105,7 @@
         (live_hbm, live_ref),
         (coupling_hbm, coupling_ref),
     ]
-    slabs = [pl.ds(f * size, size) for f in (2, 3, 0, 1)]
+    slabs = [pl.ds(2 * size, 2 * size), pl.ds(0, 2 * size)]
     pairs += [(flex_hbm.at[part], flex_ref.at[part]) for part in slabs]
     copies = [
         pltpu.make_async_copy(source, target, sems.at[i])
@@ -144,8 +135,7 @@
     high, low = halves(coupling)
     weights_ref[...] = jnp.concatenate([high, low, high], axis=0)
     for half in (slice(0, 2), slice(2, 4)):
-        for copy in copies[5:][half]:
-            copy.wait()
+        copies[5 + half.start // 2].wait()
         for face, ref in list(zip(face_order(), face_refs))[half]:
             ref[...] = jnp.dot(flex_ref[slab(face, size), :], lam, preferred_element_type=F32)
 
@@ -235,7 +225,7 @@
     )
     projected_ref, along_ref = refs[3:]
     projected_ref[...] = (jump_ref[...] - correction).astype(BF16)
-    size = jump_ref.shape[0] // 2
+    size = jump_ref.shape[0] // 4
     slabs = [slice(at, at + size) for at in range(0, jump_ref.shape[0], size)]
     gain = curvature = jnp.zeros((1, width), F32)
     projected = projected_ref[...]
@@ -311,7 +301,7 @@
             pltpu.SMEM((1, 4), jnp.int32),
             pltpu.VMEM(loads.shape, BF16),
             pltpu.VMEM(coupling.shape, F32),
-            pltpu.SemaphoreType.DMA((9,)),
+            pltpu.SemaphoreType.DMA((7,)),
         ],
     )(*(in_hbm(x) for x in inputs))
     bound, limit, weights, flex = outs[:4]

time: 78.4 us -> 78.5 us (level)
  no operation moved by 1% of the time
where the time goes in v6:
time: 78.5 us; the launch traced here: 78.4 us
  blocking collectives  42.8 us (55%)
  waiting for transfers between devices  17.2 us (22%)
  starting transfers between devices  9.88 us (13%)
  Pallas kernels  8.33 us (11%)
    all_to_all x4, blocking collectives, exchanged(): return lax.all_to_all(blocks, ALL, 0, 0, tiled=True)  42.8 us
    ppermute x11, waiting for transfers between devices, passed(): return lax.ppermute(x, axis, list(enumerate(targets)))  17.2 us
    ppermute x11, starting transfers between devices, passed(): return lax.ppermute(x, axis, list(enumerate(targets)))  9.88 us
    pallas_call x2, Pallas kernels, local(): kernel_call(functools.partial(directions, rows), [VMEM] * 6, [whole, ((co...  3.51 us
    pallas_call x1, Pallas kernels, local(): kernel_call(functools.partial(begin, bounds_table.shape[0]), [HBM] * 6, [...  2.4 us
  transfers between devices with their start and end apart: 11, of which 5 were waited for; matrix products, arithmetic and copies ran while one was open for 0% of the time, Pallas kernels for 0%

profile of v6, /device:TPU:0, one launch (start us, length us, event | category | flops | bytes accessed | tf_op | source)
XLA Modules:
  0.0 78.4 jit_solution(17308873887307004574)
XLA Ops:
  0.0 2.4 %shard_map.82 = (f32[1024,128]{1,0:T(8,128)S(1)}, s32[8,128]{1,0:T(8,128)S(1)}, bf16[48,1024]{1,0:T(8,128)(2,1)S(1)}, bf16[1024,1024]{1,0:T(8,128)(2,1)S(1)}, f3...) custom-call(f32[16]{0:T(128)} %table_hbm.1, ...), custom_call_target="tpu_custom_call" | custom-call | flops 268435456 | bytes 4194304 | tf_op jit(solution)/shard_map/pallas_call | solution.py:287
  2.4 3.1 %collective-permute-start = (f32[256,128]{1,0:T(8,128)S(1)}, f32[256,128]{1,0:T(8,128)S(1)}, u32[]{:S(2)}, u32[]{:S(2)}) collective-permute-start(f32[256,128]{1,0:T(8,128)S(1)} %get-tuple-element.34.refs_0_), channel_id=1, source_target_pairs={{0,8},{1,9},{2,10},{3,11},{4,12},{5,13},{6,14},{7,15},{8,0},{9,1},... | collective-permute-start | bytes 393224 | tf_op jit(solution)/shard_map/ppermute | solution.py:36
  5.5 0.0 collective-permute-start.4
  5.5 2.6 %collective-permute-start.5 = (f32[256,128]{1,0:T(8,128)S(1)}, f32[256,128]{1,0:T(8,128)S(1)}, u32[]{:S(2)}, u32[]{:S(2)}) collective-permute-start(f32[256,128]{1,0:T(8,128)S(1)} %get-tuple-element.36.refs_2_), channel_id=1, source_target_pairs={{0,7},{1,2},{2,1},{3,4},{4,3},{5,6},{6,5},{7,0},{8,15},{9,10},{10,... | collective-permute-start | bytes 393224 | tf_op jit(solution)/shard_map/ppermute | solution.py:36
  8.1 0.0 collective-permute-start.6
  8.1 2.5 %collective-permute-start.3 = (f32[48,96]{1,0:T(8,128)S(1)}, f32[48,96]{1,0:T(8,128)S(1)}, u32[]{:S(2)}, u32[]{:S(2)}) collective-permute-start(f32[48,96]{1,0:T(8,128)S(1)} %bitcast.14), channel_id=1, source_target_pairs={{0,24},{8,16},{16,8},{24,0},{1,25},{9,17},{17,9},{25,1},{2,26},{10... | collective-permute-start | bytes 55304 | tf_op jit(solution)/shard_map/ppermute | solution.py:36
  10.6 3.2 %collective-permute-done.3.refs_11_ = f32[48,96]{1,0:T(8,128)S(1)} collective-permute-done((f32[48,96]{1,0:T(8,128)S(1)}, f32[48,96]{1,0:T(8,128)S(1)}, u32[]{:S(2)}, u32[]{:S(2)}) %collective-permute-start.3) | collective-permute-done | bytes 18464 | tf_op jit(solution)/shard_map/ppermute | solution.py:36
  13.8 4.7 %collective-permute-done.2.refs_10_ = f32[48,96]{1,0:T(8,128)S(1)} collective-permute-done((f32[48,96]{1,0:T(8,128)S(1)}, f32[48,96]{1,0:T(8,128)S(1)}, u32[]{:S(2)}, u32[]{:S(2)}) %collective-permute-start.2) | collective-permute-done | bytes 18464 | tf_op jit(solution)/shard_map/ppermute | solution.py:36
  18.6 0.3 collective-permute-start.1
  18.9 3.5 %collective-permute-done.1.refs_9_ = f32[48,96]{1,0:T(8,128)S(1)} collective-permute-done((f32[48,96]{1,0:T(8,128)S(1)}, f32[48,96]{1,0:T(8,128)S(1)}, u32[]{:S(2)}, u32[]{:S(2)}) %collective-permute-start.1) | collective-permute-done | bytes 18464 | tf_op jit(solution)/shard_map/ppermute | solution.py:36
  22.4 0.4 shard_map.83
  22.8 11.5 %all_to_all.20.forces_ref = f32[32,3,4,128]{3,2,1,0:T(4,128)S(1)} all-to-all(f32[32,3,4,128]{3,2,1,0:T(4,128)S(1)} %get-tuple-element.43), channel_id=1, replica_groups=mesh['row'=4,'col'=8] {'row','col'}, dimensions={0} | all-to-all | bytes 393216 | tf_op jit(solution)/shard_map/all_to_all | solution.py:272
  34.3 1.8 %shard_map.84 = (f32[1024,128]{1,0:T(8,128)S(1)}, f32[32,2,128]{2,1,0:T(2,128)S(1)}) custom-call(f32[32,3,4,128]{3,2,1,0:T(4,128)S(1)} %all_to_all.20.forces_ref, bf16[32,512]{1,0:T(8,128)(2,1)S(1)} %get-tuple-element.44.mine_ref, bf16[48,1024]{1,0:T(8,128)(2,1)S(1)} %get-tuple-element.33.weights_ref, f32[1024,128]{1,0:T(8,128)S(1)} %get-tuple-element.45.jump_ref, ...), custom_call_target="tpu_custom_call" | custom-call | flops 536870912 | bytes 4194304 | tf_op jit(solution)/shard_map/pallas_call | solution.py:324
  36.1 9.7 %all_to_all.21.sums_ref = f32[32,2,128]{2,1,0:T(2,128)S(1)} all-to-all(f32[32,2,128]{2,1,0:T(2,128)S(1)} %get-tuple-element.47), channel_id=1, replica_groups=mesh['row'=4,'col'=8] {'row','col'}, dimensions={0} | all-to-all | bytes 65536 | tf_op jit(solution)/shard_map/all_to_all | solution.py:272
  45.8 0.8 %shard_map.85 = (f32[1024,128]{1,0:T(8,128)S(1)}, f32[256,128]{1,0:T(8,128)S(1)}, f32[256,128]{1,0:T(8,128)S(1)}, f32[256,128]{1,0:T(8,128)S(1)}, f32[256,128]{1,0:T(8,128)S(1)}) custom-call(f32[32,2,128]{2,1,0:T(2,128)S(1)} %all_to_all.21.sums_ref, bf16[1024,128]{1,0:T(8,128)(2,1)S(1)} %bitcast.12, f32[1024,128]{1,0:T(8,128)S(1)} %get-tuple-element.48.search_ref, ...), custom_call_target="tpu_custom_call" | custom-call | flops 268435456 | bytes 4194304 | tf_op jit(solution)/shard_map/pallas_call | solution.py:337
  46.6 0.6 collective-permute-start.7
  47.2 0.8 collective-permute-start.9
  48.0 4.2 %collective-permute-done.7.refs_4_ = f32[256,128]{1,0:T(8,128)S(1)} collective-permute-done((f32[256,128]{1,0:T(8,128)S(1)}, f32[256,128]{1,0:T(8,128)S(1)}, u32[]{:S(2)}, u32[]{:S(2)}) %collective-permute-start.7) | collective-permute-done | bytes 131104 | tf_op jit(solution)/shard_map/ppermute | solution.py:36
  52.1 1.6 %collective-permute-done.9.refs_6_ = f32[256,128]{1,0:T(8,128)S(1)} collective-permute-done((f32[256,128]{1,0:T(8,128)S(1)}, f32[256,128]{1,0:T(8,128)S(1)}, u32[]{:S(2)}, u32[]{:S(2)}) %collective-permute-start.9) | collective-permute-done | bytes 131104 | tf_op jit(solution)/shard_map/ppermute | solution.py:36
  53.7 0.4 shard_map.86
  54.1 12.0 %all_to_all.22.forces_ref = f32[32,3,4,128]{3,2,1,0:T(4,128)S(1)} all-to-all(f32[32,3,4,128]{3,2,1,0:T(4,128)S(1)} %get-tuple-element.54), channel_id=1, replica_groups=mesh['row'=4,'col'=8] {'row','col'}, dimensions={0} | all-to-all | bytes 393216 | tf_op jit(solution)/shard_map/all_to_all | solution.py:272
  66.1 1.8 %shard_map.87 = (f32[1024,128]{1,0:T(8,128)S(1)}, f32[32,2,128]{2,1,0:T(2,128)S(1)}) custom-call(f32[32,3,4,128]{3,2,1,0:T(4,128)S(1)} %all_to_all.22.forces_ref, bf16[32,512]{1,0:T(8,128)(2,1)S(1)} %get-tuple-element.44.mine_ref, bf16[48,1024]{1,0:T(8,128)(2,1)S(1)} %get-tuple-element.33.weights_ref, f32[1024,128]{1,0:T(8,128)S(1)} %get-tuple-element.55.jump_ref, ...), custom_call_target="tpu_custom_call" | custom-call | flops 536870912 | bytes 4194304 | tf_op jit(solution)/shard_map/pallas_call | solution.py:324
  67.8 9.7 %all_to_all.23.sums_ref = f32[32,2,128]{2,1,0:T(2,128)S(1)} all-to-all(f32[32,2,128]{2,1,0:T(2,128)S(1)} %get-tuple-element.56), channel_id=1, replica_groups=mesh['row'=4,'col'=8] {'row','col'}, dimensions={0} | all-to-all | bytes 65536 | tf_op jit(solution)/shard_map/all_to_all | solution.py:272
  77.5 0.8 %shard_map.88 = bf16[1024,128]{1,0:T(8,128)(2,1)} custom-call(f32[32,2,128]{2,1,0:T(2,128)S(1)} %all_to_all.23.sums_ref, f32[1024,128]{1,0:T(8,128)S(1)} %get-tuple-element.57.lam_ref, f32[1024,128]{1,0:T(8,128)S(1)} %get-tuple-element.58.search_ref, f32[1024,128]{1,0:T(8,128)S(1)} %get-tuple-element.49.bound_ref), custom_call_target="tpu_custom_call" | custom-call | flops 4194304 | bytes 4194304 | tf_op jit(solution)/shard_map/pallas_call | solution.py:341
  (15 shorter events, 0.0 us)
Async XLA Ops:
  0.0 22.4 %copy-start.1 = (bf16[1,1,1024,128]{3,2,1,0:T(8,128)(2,1)S(1)}, bf16[1,1,1024,128]{3,2,1,0:T(8,128)(2,1)}, u32[]{:S(2)}) copy-start(bf16[1,1,1024,128]{3,2,1,0:T(8,128)(2,1)} %param.8) | copy-start | bytes 786436
  0.0 8.1 %copy-start.2 = (f32[96,48]{0,1:T(8,128)S(1)}, f32[96,48]{0,1:T(8,128)}, u32[]{:S(2)}) copy-start(f32[96,48]{0,1:T(8,128)} %param.12) | copy-start | bytes 55300
  0.0 34.3 %copy-start = (bf16[1,1,1024,1024]{3,2,1,0:T(8,128)(2,1)S(1)}, bf16[1,1,1024,1024]{3,2,1,0:T(8,128)(2,1)}, u32[]{:S(2)}) copy-start(bf16[1,1,1024,1024]{3,2,1,0:T(8,128)(2,1)} %param.10) | copy-start | bytes 6291460
  2.4 20.0 %collective-permute-start = (f32[256,128]{1,0:T(8,128)S(1)}, f32[256,128]{1,0:T(8,128)S(1)}, u32[]{:S(2)}, u32[]{:S(2)}) collective-permute-start(f32[256,128]{1,0:T(8,128)S(1)} %get-tuple-element.34.refs_0_), channel_id=1, source_target_pairs={{0,8},{1,9},{2,10},{3,11},{4,12},{5,13},{6,14},{7,15},{8,0},{9,1},... | collective-permute-start | bytes 393224 | tf_op jit(solution)/shard_map/ppermute | solution.py:36
  5.5 16.9 %collective-permute-start.4 = (f32[256,128]{1,0:T(8,128)S(1)}, f32[256,128]{1,0:T(8,128)S(1)}, u32[]{:S(2)}, u32[]{:S(2)}) collective-permute-start(f32[256,128]{1,0:T(8,128)S(1)} %get-tuple-element.35.refs_1_), channel_id=1, source_target_pairs={{0,1},{1,0},{2,3},{3,2},{4,5},{5,4},{6,7},{7,6},{8,16},{9,17},{10,... | collective-permute-start | bytes 393224 | tf_op jit(solution)/shard_map/ppermute | solution.py:36
  5.5 16.9 %collective-permute-start.5 = (f32[256,128]{1,0:T(8,128)S(1)}, f32[256,128]{1,0:T(8,128)S(1)}, u32[]{:S(2)}, u32[]{:S(2)}) collective-permute-start(f32[256,128]{1,0:T(8,128)S(1)} %get-tuple-element.36.refs_2_), channel_id=1, source_target_pairs={{0,7},{1,2},{2,1},{3,4},{4,3},{5,6},{6,5},{7,0},{8,15},{9,10},{10,... | collective-permute-start | bytes 393224 | tf_op jit(solution)/shard_map/ppermute | solution.py:36
  8.1 14.3 %collective-permute-start.6 = (f32[256,128]{1,0:T(8,128)S(1)}, f32[256,128]{1,0:T(8,128)S(1)}, u32[]{:S(2)}, u32[]{:S(2)}) collective-permute-start(f32[256,128]{1,0:T(8,128)S(1)} %get-tuple-element.37.refs_3_), channel_id=1, source_target_pairs={{0,1},{1,0},{2,3},{3,2},{4,5},{5,4},{6,7},{7,6},{8,9},{9,8},{10,11... | collective-permute-start | bytes 393224 | tf_op jit(solution)/shard_map/ppermute | solution.py:36
  8.1 5.7 %collective-permute-start.3 = (f32[48,96]{1,0:T(8,128)S(1)}, f32[48,96]{1,0:T(8,128)S(1)}, u32[]{:S(2)}, u32[]{:S(2)}) collective-permute-start(f32[48,96]{1,0:T(8,128)S(1)} %bitcast.14), channel_id=1, source_target_pairs={{0,24},{8,16},{16,8},{24,0},{1,25},{9,17},{17,9},{25,1},{2,26},{10... | collective-permute-start | bytes 55304 | tf_op jit(solution)/shard_map/ppermute | solution.py:36
  13.8 4.7 %collective-permute-start.2 = (f32[48,96]{1,0:T(8,128)S(1)}, f32[48,96]{1,0:T(8,128)S(1)}, u32[]{:S(2)}, u32[]{:S(2)}) collective-permute-start(f32[48,96]{1,0:T(8,128)S(1)} %bitcast.15), channel_id=1, source_target_pairs={{0,16},{8,24},{16,0},{24,8},{1,17},{9,25},{17,1},{25,9},{2,18},{10... | collective-permute-start | bytes 55304 | tf_op jit(solution)/shard_map/ppermute | solution.py:36
  18.6 3.8 %collective-permute-start.1 = (f32[48,96]{1,0:T(8,128)S(1)}, f32[48,96]{1,0:T(8,128)S(1)}, u32[]{:S(2)}, u32[]{:S(2)}) collective-permute-start(f32[48,96]{1,0:T(8,128)S(1)} %bitcast.16), channel_id=1, source_target_pairs={{0,8},{8,0},{16,24},{24,16},{1,9},{9,1},{17,25},{25,17},{2,10},{10... | collective-permute-start | bytes 55304 | tf_op jit(solution)/shard_map/ppermute | solution.py:36
  46.6 5.6 %collective-permute-start.7 = (f32[256,128]{1,0:T(8,128)S(1)}, f32[256,128]{1,0:T(8,128)S(1)}, u32[]{:S(2)}, u32[]{:S(2)}) collective-permute-start(f32[256,128]{1,0:T(8,128)S(1)} %get-tuple-element.50.refs_0_), channel_id=1, source_target_pairs={{0,8},{1,9},{2,10},{3,11},{4,12},{5,13},{6,14},{7,15},{8,0},{9,1},... | collective-permute-start | bytes 393224 | tf_op jit(solution)/shard_map/ppermute | solution.py:36
  47.2 4.9 %collective-permute-start.8 = (f32[256,128]{1,0:T(8,128)S(1)}, f32[256,128]{1,0:T(8,128)S(1)}, u32[]{:S(2)}, u32[]{:S(2)}) collective-permute-start(f32[256,128]{1,0:T(8,128)S(1)} %get-tuple-element.51.refs_1_), channel_id=1, source_target_pairs={{0,1},{1,0},{2,3},{3,2},{4,5},{5,4},{6,7},{7,6},{8,16},{9,17},{10,... | collective-permute-start | bytes 393224 | tf_op jit(solution)/shard_map/ppermute | solution.py:36
  47.2 6.5 %collective-permute-start.9 = (f32[256,128]{1,0:T(8,128)S(1)}, f32[256,128]{1,0:T(8,128)S(1)}, u32[]{:S(2)}, u32[]{:S(2)}) collective-permute-start(f32[256,128]{1,0:T(8,128)S(1)} %get-tuple-element.52.refs_2_), channel_id=1, source_target_pairs={{0,7},{1,2},{2,1},{3,4},{4,3},{5,6},{6,5},{7,0},{8,15},{9,10},{10,... | collective-permute-start | bytes 393224 | tf_op jit(solution)/shard_map/ppermute | solution.py:36
  48.0 5.7 %collective-permute-start.10 = (f32[256,128]{1,0:T(8,128)S(1)}, f32[256,128]{1,0:T(8,128)S(1)}, u32[]{:S(2)}, u32[]{:S(2)}) collective-permute-start(f32[256,128]{1,0:T(8,128)S(1)} %get-tuple-element.53.refs_3_), channel_id=1, source_target_pairs={{0,1},{1,0},{2,3},{3,2},{4,5},{5,4},{6,7},{7,6},{8,9},{9,8},{10,11... | collective-permute-start | bytes 393224 | tf_op jit(solution)/shard_map/ppermute | solution.py:36

commit v7 on v6

--- a/solution.py
+++ b/solution.py
@@ -105,7 +105,7 @@
         (live_hbm, live_ref),
         (coupling_hbm, coupling_ref),
     ]
-    slabs = [pl.ds(2 * size, 2 * size), pl.ds(0, 2 * size)]
+    slabs = [pl.ds(f * size, size) for f in (2, 3, 0, 1)]
     pairs += [(flex_hbm.at[part], flex_ref.at[part]) for part in slabs]
     copies = [
         pltpu.make_async_copy(source, target, sems.at[i])
@@ -135,7 +135,8 @@
     high, low = halves(coupling)
     weights_ref[...] = jnp.concatenate([high, low, high], axis=0)
     for half in (slice(0, 2), slice(2, 4)):
-        copies[5 + half.start // 2].wait()
+        for copy in copies[5:][half]:
+            copy.wait()
         for face, ref in list(zip(face_order(), face_refs))[half]:
             ref[...] = jnp.dot(flex_ref[slab(face, size), :], lam, preferred_element_type=F32)
 
@@ -225,7 +226,7 @@
     )
     projected_ref, along_ref = refs[3:]
     projected_ref[...] = (jump_ref[...] - correction).astype(BF16)
-    size = jump_ref.shape[0] // 4
+    size = jump_ref.shape[0] // 2
     slabs = [slice(at, at + size) for at in range(0, jump_ref.shape[0], size)]
     gain = curvature = jnp.zeros((1, width), F32)
     projected = projected_ref[...]
@@ -301,7 +302,7 @@
             pltpu.SMEM((1, 4), jnp.int32),
             pltpu.VMEM(loads.shape, BF16),
             pltpu.VMEM(coupling.shape, F32),
-            pltpu.SemaphoreType.DMA((7,)),
+            pltpu.SemaphoreType.DMA((9,)),
         ],
     )(*(in_hbm(x) for x in inputs))
     bound, limit, weights, flex = outs[:4]

time: 78.5 us -> 78.5 us (level)
  no operation moved by 1% of the time
where the time goes in v7:
time: 78.5 us; the launch traced here: 78.3 us
  blocking collectives  42.8 us (55%)
  waiting for transfers between devices  17.2 us (22%)
  starting transfers between devices  9.88 us (13%)
  Pallas kernels  8.25 us (11%)
    all_to_all x4, blocking collectives, exchanged(): return lax.all_to_all(blocks, ALL, 0, 0, tiled=True)  42.8 us
    ppermute x11, waiting for transfers between devices, passed(): return lax.ppermute(x, axis, list(enumerate(targets)))  17.2 us
    ppermute x11, starting transfers between devices, passed(): return lax.ppermute(x, axis, list(enumerate(targets)))  9.88 us
    pallas_call x2, Pallas kernels, local(): kernel_call(functools.partial(directions, rows), [VMEM] * 6, [whole, ((co...  3.44 us
    pallas_call x1, Pallas kernels, local(): kernel_call(functools.partial(begin, bounds_table.shape[0]), [HBM] * 6, [...  2.39 us
  transfers between devices with their start and end apart: 11, of which 5 were waited for; matrix products, arithmetic and copies ran while one was open for 0% of the time, Pallas kernels for 0%

profile of v7, /device:TPU:0, one launch (start us, length us, event | category | flops | bytes accessed | tf_op | source)
XLA Modules:
  0.0 78.3 jit_solution(9854866262635590142)
XLA Ops:
  0.0 2.4 %shard_map.82 = (f32[1024,128]{1,0:T(8,128)S(1)}, s32[8,128]{1,0:T(8,128)S(1)}, bf16[48,1024]{1,0:T(8,128)(2,1)S(1)}, bf16[1024,1024]{1,0:T(8,128)(2,1)S(1)}, f3...) custom-call(f32[16]{0:T(128)} %table_hbm.1, ...), custom_call_target="tpu_custom_call" | custom-call | flops 268435456 | bytes 4194304 | tf_op jit(solution)/shard_map/pallas_call | solution.py:288
  2.4 3.1 %collective-permute-start = (f32[256,128]{1,0:T(8,128)S(1)}, f32[256,128]{1,0:T(8,128)S(1)}, u32[]{:S(2)}, u32[]{:S(2)}) collective-permute-start(f32[256,128]{1,0:T(8,128)S(1)} %get-tuple-element.34.refs_0_), channel_id=1, source_target_pairs={{0,8},{1,9},{2,10},{3,11},{4,12},{5,13},{6,14},{7,15},{8,0},{9,1},... | collective-permute-start | bytes 393224 | tf_op jit(solution)/shard_map/ppermute | solution.py:36
  5.5 2.6 %collective-permute-start.5 = (f32[256,128]{1,0:T(8,128)S(1)}, f32[256,128]{1,0:T(8,128)S(1)}, u32[]{:S(2)}, u32[]{:S(2)}) collective-permute-start(f32[256,128]{1,0:T(8,128)S(1)} %get-tuple-element.36.refs_2_), channel_id=1, source_target_pairs={{0,7},{1,2},{2,1},{3,4},{4,3},{5,6},{6,5},{7,0},{8,15},{9,10},{10,... | collective-permute-start | bytes 393224 | tf_op jit(solution)/shard_map/ppermute | solution.py:36
  8.1 2.5 %collective-permute-start.3 = (f32[48,96]{1,0:T(8,128)S(1)}, f32[48,96]{1,0:T(8,128)S(1)}, u32[]{:S(2)}, u32[]{:S(2)}) collective-permute-start(f32[48,96]{1,0:T(8,128)S(1)} %bitcast.14), channel_id=1, source_target_pairs={{0,24},{8,16},{16,8},{24,0},{1,25},{9,17},{17,9},{25,1},{2,26},{10... | collective-permute-start | bytes 55304 | tf_op jit(solution)/shard_map/ppermute | solution.py:36
  10.6 3.2 %collective-permute-done.3.refs_11_ = f32[48,96]{1,0:T(8,128)S(1)} collective-permute-done((f32[48,96]{1,0:T(8,128)S(1)}, f32[48,96]{1,0:T(8,128)S(1)}, u32[]{:S(2)}, u32[]{:S(2)}) %collective-permute-start.3) | collective-permute-done | bytes 18464 | tf_op jit(solution)/shard_map/ppermute | solution.py:36
  13.8 4.7 %collective-permute-done.2.refs_10_ = f32[48,96]{1,0:T(8,128)S(1)} collective-permute-done((f32[48,96]{1,0:T(8,128)S(1)}, f32[48,96]{1,0:T(8,128)S(1)}, u32[]{:S(2)}, u32[]{:S(2)}) %collective-permute-start.2) | collective-permute-done | bytes 18464 | tf_op jit(solution)/shard_map/ppermute | solution.py:36
  18.6 0.3 collective-permute-start.1
  18.9 3.5 %collective-permute-done.1.refs_9_ = f32[48,96]{1,0:T(8,128)S(1)} collective-permute-done((f32[48,96]{1,0:T(8,128)S(1)}, f32[48,96]{1,0:T(8,128)S(1)}, u32[]{:S(2)}, u32[]{:S(2)}) %collective-permute-start.1) | collective-permute-done | bytes 18464 | tf_op jit(solution)/shard_map/ppermute | solution.py:36
  22.4 0.0 collective-permute-done.6.refs_7_
  22.4 0.4 shard_map.83
  22.8 11.5 %all_to_all.20.forces_ref = f32[32,3,4,128]{3,2,1,0:T(4,128)S(1)} all-to-all(f32[32,3,4,128]{3,2,1,0:T(4,128)S(1)} %get-tuple-element.43), channel_id=1, replica_groups=mesh['row'=4,'col'=8] {'row','col'}, dimensions={0} | all-to-all | bytes 393216 | tf_op jit(solution)/shard_map/all_to_all | solution.py:273
  34.3 1.7 %shard_map.84 = (f32[1024,128]{1,0:T(8,128)S(1)}, f32[32,2,128]{2,1,0:T(2,128)S(1)}) custom-call(f32[32,3,4,128]{3,2,1,0:T(4,128)S(1)} %all_to_all.20.forces_ref, bf16[32,512]{1,0:T(8,128)(2,1)S(1)} %get-tuple-element.44.mine_ref, bf16[48,1024]{1,0:T(8,128)(2,1)S(1)} %get-tuple-element.33.weights_ref, f32[1024,128]{1,0:T(8,128)S(1)} %get-tuple-element.45.jump_ref, ...), custom_call_target="tpu_custom_call" | custom-call | flops 536870912 | bytes 4194304 | tf_op jit(solution)/shard_map/pallas_call | solution.py:325
  36.0 9.7 %all_to_all.21.sums_ref = f32[32,2,128]{2,1,0:T(2,128)S(1)} all-to-all(f32[32,2,128]{2,1,0:T(2,128)S(1)} %get-tuple-element.47), channel_id=1, replica_groups=mesh['row'=4,'col'=8] {'row','col'}, dimensions={0} | all-to-all | bytes 65536 | tf_op jit(solution)/shard_map/all_to_all | solution.py:273
  45.7 0.8 %shard_map.85 = (f32[1024,128]{1,0:T(8,128)S(1)}, f32[256,128]{1,0:T(8,128)S(1)}, f32[256,128]{1,0:T(8,128)S(1)}, f32[256,128]{1,0:T(8,128)S(1)}, f32[256,128]{1,0:T(8,128)S(1)}) custom-call(f32[32,2,128]{2,1,0:T(2,128)S(1)} %all_to_all.21.sums_ref, bf16[1024,128]{1,0:T(8,128)(2,1)S(1)} %bitcast.12, f32[1024,128]{1,0:T(8,128)S(1)} %get-tuple-element.48.search_ref, ...), custom_call_target="tpu_custom_call" | custom-call | flops 268435456 | bytes 4194304 | tf_op jit(solution)/shard_map/pallas_call | solution.py:338
  46.5 0.6 collective-permute-start.7
  47.2 0.8 collective-permute-start.9
  47.9 0.0 collective-permute-start.10
  47.9 4.2 %collective-permute-done.7.refs_4_ = f32[256,128]{1,0:T(8,128)S(1)} collective-permute-done((f32[256,128]{1,0:T(8,128)S(1)}, f32[256,128]{1,0:T(8,128)S(1)}, u32[]{:S(2)}, u32[]{:S(2)}) %collective-permute-start.7) | collective-permute-done | bytes 131104 | tf_op jit(solution)/shard_map/ppermute | solution.py:36
  52.1 1.6 %collective-permute-done.9.refs_6_ = f32[256,128]{1,0:T(8,128)S(1)} collective-permute-done((f32[256,128]{1,0:T(8,128)S(1)}, f32[256,128]{1,0:T(8,128)S(1)}, u32[]{:S(2)}, u32[]{:S(2)}) %collective-permute-start.9) | collective-permute-done | bytes 131104 | tf_op jit(solution)/shard_map/ppermute | solution.py:36
  53.7 0.4 shard_map.86
  54.0 12.0 %all_to_all.22.forces_ref = f32[32,3,4,128]{3,2,1,0:T(4,128)S(1)} all-to-all(f32[32,3,4,128]{3,2,1,0:T(4,128)S(1)} %get-tuple-element.54), channel_id=1, replica_groups=mesh['row'=4,'col'=8] {'row','col'}, dimensions={0} | all-to-all | bytes 393216 | tf_op jit(solution)/shard_map/all_to_all | solution.py:273
  66.0 1.7 %shard_map.87 = (f32[1024,128]{1,0:T(8,128)S(1)}, f32[32,2,128]{2,1,0:T(2,128)S(1)}) custom-call(f32[32,3,4,128]{3,2,1,0:T(4,128)S(1)} %all_to_all.22.forces_ref, bf16[32,512]{1,0:T(8,128)(2,1)S(1)} %get-tuple-element.44.mine_ref, bf16[48,1024]{1,0:T(8,128)(2,1)S(1)} %get-tuple-element.33.weights_ref, f32[1024,128]{1,0:T(8,128)S(1)} %get-tuple-element.55.jump_ref, ...), custom_call_target="tpu_custom_call" | custom-call | flops 536870912 | bytes 4194304 | tf_op jit(solution)/shard_map/pallas_call | solution.py:325
  67.7 9.7 %all_to_all.23.sums_ref = f32[32,2,128]{2,1,0:T(2,128)S(1)} all-to-all(f32[32,2,128]{2,1,0:T(2,128)S(1)} %get-tuple-element.56), channel_id=1, replica_groups=mesh['row'=4,'col'=8] {'row','col'}, dimensions={0} | all-to-all | bytes 65536 | tf_op jit(solution)/shard_map/all_to_all | solution.py:273
  77.4 0.8 %shard_map.88 = bf16[1024,128]{1,0:T(8,128)(2,1)} custom-call(f32[32,2,128]{2,1,0:T(2,128)S(1)} %all_to_all.23.sums_ref, f32[1024,128]{1,0:T(8,128)S(1)} %get-tuple-element.57.lam_ref, f32[1024,128]{1,0:T(8,128)S(1)} %get-tuple-element.58.search_ref, f32[1024,128]{1,0:T(8,128)S(1)} %get-tuple-element.49.bound_ref), custom_call_target="tpu_custom_call" | custom-call | flops 4194304 | bytes 4194304 | tf_op jit(solution)/shard_map/pallas_call | solution.py:342
  (15 shorter events, 0.0 us)
Async XLA Ops:
  0.0 22.4 %copy-start.1 = (bf16[1,1,1024,128]{3,2,1,0:T(8,128)(2,1)S(1)}, bf16[1,1,1024,128]{3,2,1,0:T(8,128)(2,1)}, u32[]{:S(2)}) copy-start(bf16[1,1,1024,128]{3,2,1,0:T(8,128)(2,1)} %param.8) | copy-start | bytes 786436
  0.0 8.1 %copy-start.2 = (f32[96,48]{0,1:T(8,128)S(1)}, f32[96,48]{0,1:T(8,128)}, u32[]{:S(2)}) copy-start(f32[96,48]{0,1:T(8,128)} %param.12) | copy-start | bytes 55300
  0.0 34.3 %copy-start = (bf16[1,1,1024,1024]{3,2,1,0:T(8,128)(2,1)S(1)}, bf16[1,1,1024,1024]{3,2,1,0:T(8,128)(2,1)}, u32[]{:S(2)}) copy-start(bf16[1,1,1024,1024]{3,2,1,0:T(8,128)(2,1)} %param.10) | copy-start | bytes 6291460
  2.4 20.0 %collective-permute-start = (f32[256,128]{1,0:T(8,128)S(1)}, f32[256,128]{1,0:T(8,128)S(1)}, u32[]{:S(2)}, u32[]{:S(2)}) collective-permute-start(f32[256,128]{1,0:T(8,128)S(1)} %get-tuple-element.34.refs_0_), channel_id=1, source_target_pairs={{0,8},{1,9},{2,10},{3,11},{4,12},{5,13},{6,14},{7,15},{8,0},{9,1},... | collective-permute-start | bytes 393224 | tf_op jit(solution)/shard_map/ppermute | solution.py:36
  5.5 16.9 %collective-permute-start.4 = (f32[256,128]{1,0:T(8,128)S(1)}, f32[256,128]{1,0:T(8,128)S(1)}, u32[]{:S(2)}, u32[]{:S(2)}) collective-permute-start(f32[256,128]{1,0:T(8,128)S(1)} %get-tuple-element.35.refs_1_), channel_id=1, source_target_pairs={{0,1},{1,0},{2,3},{3,2},{4,5},{5,4},{6,7},{7,6},{8,16},{9,17},{10,... | collective-permute-start | bytes 393224 | tf_op jit(solution)/shard_map/ppermute | solution.py:36
  5.5 16.9 %collective-permute-start.5 = (f32[256,128]{1,0:T(8,128)S(1)}, f32[256,128]{1,0:T(8,128)S(1)}, u32[]{:S(2)}, u32[]{:S(2)}) collective-permute-start(f32[256,128]{1,0:T(8,128)S(1)} %get-tuple-element.36.refs_2_), channel_id=1, source_target_pairs={{0,7},{1,2},{2,1},{3,4},{4,3},{5,6},{6,5},{7,0},{8,15},{9,10},{10,... | collective-permute-start | bytes 393224 | tf_op jit(solution)/shard_map/ppermute | solution.py:36
  8.1 14.3 %collective-permute-start.6 = (f32[256,128]{1,0:T(8,128)S(1)}, f32[256,128]{1,0:T(8,128)S(1)}, u32[]{:S(2)}, u32[]{:S(2)}) collective-permute-start(f32[256,128]{1,0:T(8,128)S(1)} %get-tuple-element.37.refs_3_), channel_id=1, source_target_pairs={{0,1},{1,0},{2,3},{3,2},{4,5},{5,4},{6,7},{7,6},{8,9},{9,8},{10,11... | collective-permute-start | bytes 393224 | tf_op jit(solution)/shard_map/ppermute | solution.py:36
  8.1 5.7 %collective-permute-start.3 = (f32[48,96]{1,0:T(8,128)S(1)}, f32[48,96]{1,0:T(8,128)S(1)}, u32[]{:S(2)}, u32[]{:S(2)}) collective-permute-start(f32[48,96]{1,0:T(8,128)S(1)} %bitcast.14), channel_id=1, source_target_pairs={{0,24},{8,16},{16,8},{24,0},{1,25},{9,17},{17,9},{25,1},{2,26},{10... | collective-permute-start | bytes 55304 | tf_op jit(solution)/shard_map/ppermute | solution.py:36
  13.8 4.7 %collective-permute-start.2 = (f32[48,96]{1,0:T(8,128)S(1)}, f32[48,96]{1,0:T(8,128)S(1)}, u32[]{:S(2)}, u32[]{:S(2)}) collective-permute-start(f32[48,96]{1,0:T(8,128)S(1)} %bitcast.15), channel_id=1, source_target_pairs={{0,16},{8,24},{16,0},{24,8},{1,17},{9,25},{17,1},{25,9},{2,18},{10... | collective-permute-start | bytes 55304 | tf_op jit(solution)/shard_map/ppermute | solution.py:36
  18.6 3.8 %collective-permute-start.1 = (f32[48,96]{1,0:T(8,128)S(1)}, f32[48,96]{1,0:T(8,128)S(1)}, u32[]{:S(2)}, u32[]{:S(2)}) collective-permute-start(f32[48,96]{1,0:T(8,128)S(1)} %bitcast.16), channel_id=1, source_target_pairs={{0,8},{8,0},{16,24},{24,16},{1,9},{9,1},{17,25},{25,17},{2,10},{10... | collective-permute-start | bytes 55304 | tf_op jit(solution)/shard_map/ppermute | solution.py:36
  46.5 5.6 %collective-permute-start.7 = (f32[256,128]{1,0:T(8,128)S(1)}, f32[256,128]{1,0:T(8,128)S(1)}, u32[]{:S(2)}, u32[]{:S(2)}) collective-permute-start(f32[256,128]{1,0:T(8,128)S(1)} %get-tuple-element.50.refs_0_), channel_id=1, source_target_pairs={{0,8},{1,9},{2,10},{3,11},{4,12},{5,13},{6,14},{7,15},{8,0},{9,1},... | collective-permute-start | bytes 393224 | tf_op jit(solution)/shard_map/ppermute | solution.py:36
  47.2 4.9 %collective-permute-start.8 = (f32[256,128]{1,0:T(8,128)S(1)}, f32[256,128]{1,0:T(8,128)S(1)}, u32[]{:S(2)}, u32[]{:S(2)}) collective-permute-start(f32[256,128]{1,0:T(8,128)S(1)} %get-tuple-element.51.refs_1_), channel_id=1, source_target_pairs={{0,1},{1,0},{2,3},{3,2},{4,5},{5,4},{6,7},{7,6},{8,16},{9,17},{10,... | collective-permute-start | bytes 393224 | tf_op jit(solution)/shard_map/ppermute | solution.py:36
  47.2 6.5 %collective-permute-start.9 = (f32[256,128]{1,0:T(8,128)S(1)}, f32[256,128]{1,0:T(8,128)S(1)}, u32[]{:S(2)}, u32[]{:S(2)}) collective-permute-start(f32[256,128]{1,0:T(8,128)S(1)} %get-tuple-element.52.refs_2_), channel_id=1, source_target_pairs={{0,7},{1,2},{2,1},{3,4},{4,3},{5,6},{6,5},{7,0},{8,15},{9,10},{10,... | collective-permute-start | bytes 393224 | tf_op jit(solution)/shard_map/ppermute | solution.py:36
  47.9 5.7 %collective-permute-start.10 = (f32[256,128]{1,0:T(8,128)S(1)}, f32[256,128]{1,0:T(8,128)S(1)}, u32[]{:S(2)}, u32[]{:S(2)}) collective-permute-start(f32[256,128]{1,0:T(8,128)S(1)} %get-tuple-element.53.refs_3_), channel_id=1, source_target_pairs={{0,1},{1,0},{2,3},{3,2},{4,5},{5,4},{6,7},{7,6},{8,9},{9,8},{10,11... | collective-permute-start | bytes 393224 | tf_op jit(solution)/shard_map/ppermute | solution.py:36
